TPU v7x, 32 devices: a whole 2x2x4 slice. The times are simulated.
32 devices in a mesh: dp: 8 (over y, x, core), tensor: 4 (over z).
Axes of the slice: x: 2, y: 2, z: 4, core: 2. Of those that a mesh axis runs over, the one named last changes fastest.
Arguments:
- tokens: bfloat16 [6144, 2048], P(('dp', 'tensor')), may hold values from -6 to 6
- cotangent: bfloat16 [6144, 2048], P(('dp', 'tensor')), may hold values from -6 to 6
- deal: int32 [6144], P(('dp', 'tensor')), may hold values from 0 to 6143, as said below
- segment: int32 [6144], P('dp'), may hold values from 0 to 3, as said below
- norm1_gain: float32 [2, 2048], replicated, may hold values from 0.5 to 1.5
- norm1_shift: float32 [2, 2048], replicated, may hold values from -1.25 to 1.25
- query_weight: bfloat16 [2, 2048, 2048], P(None, 'dp', 'tensor'), may hold values from -0.125 to 0.125
- query_bias: float32 [2, 2048], P(None, 'tensor'), may hold values from -3 to 3
- kv_weight: bfloat16 [2, 2048, 256], P(None, 'dp', 'tensor'), may hold values from -0.125 to 0.125
- value_bias: float32 [2, 128], replicated, may hold values from -0.3125 to 0.3125
- out_weight: bfloat16 [2, 2048, 2048], P(None, 'tensor', 'dp'), may hold values from -1.5 to 1.5
- out_bias: float32 [2, 2048], replicated, may hold values from -1.75 to 1.75
- norm2_gain: float32 [2, 2048], replicated, may hold values from 0.5 to 1.5
- norm2_shift: float32 [2, 2048], replicated, may hold values from -1.25 to 1.25
- up_weight: bfloat16 [2, 2048, 8192], P(None, 'dp', 'tensor'), may hold values from -0.125 to 0.125
- up_bias: float32 [2, 8192], P(None, 'tensor'), may hold values from -3 to 3
- down_weight: bfloat16 [2, 8192, 2048], P(None, 'tensor', 'dp'), may hold values from -0.0625 to 0.0625
- down_bias: float32 [2, 2048], replicated, may hold values from -1.75 to 1.75
Outputs:
- layer_out: bfloat16 [6144, 2048], P(('dp', 'tensor'))
- tokens_grad: bfloat16 [6144, 2048], P(('dp', 'tensor'))
- norm1_gain_grad: float32 [2, 2048], replicated
- norm1_shift_grad: float32 [2, 2048], replicated
- query_weight_grad: float32 [2, 2048, 2048], P(None, 'dp', 'tensor')
- query_bias_grad: float32 [2, 2048], P(None, 'tensor')
- kv_weight_grad: float32 [2, 2048, 256], P(None, 'dp', 'tensor')
- value_bias_grad: float32 [2, 128], replicated
- out_weight_grad: float32 [2, 2048, 2048], P(None, 'tensor', 'dp')
- out_bias_grad: float32 [2, 2048], replicated
- norm2_gain_grad: float32 [2, 2048], replicated
- norm2_shift_grad: float32 [2, 2048], replicated
- up_weight_grad: float32 [2, 2048, 8192], P(None, 'dp', 'tensor')
- up_bias_grad: float32 [2, 8192], P(None, 'tensor')
- down_weight_grad: float32 [2, 8192, 2048], P(None, 'tensor', 'dp')
- down_bias_grad: float32 [2, 2048], replicated
Inputs may be any that keep to these rules, and one draw needn't show every extreme that they name: deal is a permutation: input row i becomes working row deal[i]; rows of both orders are laid out over the devices in order, 192 a device; a row stays on a device of the same tensor index, and every device deals exactly 24 rows to each dp index. `segment`: within each group of 768 working rows the labels never fall; each run of equal labels is one sequence of 96 to 768 rows; the first group is one sequence of all its rows.
All inputs are finite; a program needn't handle non-finite values.
Results may differ from a plain program's by a relative error of at most 0.025.
Values may be sent and summed in bfloat16 or wider, within the bound.
No kernel may reach another device: no remote copies, remote signals or barrier semaphores. Data moves between devices by JAX's collectives and lax.ppermute only.
A program may use at most 256 MiB of HBM per device.

v0:
```python
import jax
import jax.numpy as jnp
from jax import lax
from jax.sharding import PartitionSpec as P

HEAD = 128


EPSILON = 1e-05


def layer_norm(values, scales, offsets):
    row_mean = jnp.mean(values, axis=-1, keepdims=True)
    centred = values - row_mean
    row_var = jnp.mean(centred * centred, axis=-1, keepdims=True)
    return centred * lax.rsqrt(row_var + EPSILON) * scales + offsets


def gelu_tanh(values):
    return jax.nn.gelu(values, approximate=True)


def matmul(left, right):
    return jnp.dot(left, right, preferred_element_type=jnp.float32)


def contract_rows(left, right):
    return lax.dot_general(
        left, right, (((0,), (0,)), ((), ())), preferred_element_type=jnp.float32
    )


def contract_cols(left, right):
    return lax.dot_general(
        left, right, (((1,), (1,)), ((), ())), preferred_element_type=jnp.float32
    )


def rows_gather(values):
    return lax.all_gather(values, "tensor", axis=0, tiled=True)


def grad_gather(values):
    return lax.all_gather(values, "tensor", axis=0, tiled=True)


def rows_scatter(left, right):
    return lax.psum_scatter(
        matmul(left, right).astype(jnp.bfloat16), "tensor", scatter_dimension=0, tiled=True
    ).astype(jnp.float32)


def grad_scatter(factor_pairs):
    running = None
    for gradient, weight in factor_pairs:
        product_piece = contract_cols(gradient, weight)
        running = product_piece if running is None else running + product_piece
    return lax.psum_scatter(
        running.astype(jnp.bfloat16), "tensor", scatter_dimension=0, tiled=True
    ).astype(jnp.float32)


def place_slice(values, full_width, tensor_rank):
    start_col = tensor_rank * values.shape[0]
    return lax.dynamic_update_slice(jnp.zeros((full_width,), jnp.float32), values, (start_col,))


def local(
    tokens,
    cotangent,
    deal,
    segment,
    norm1_gain,
    norm1_shift,
    query_weight,
    query_bias,
    kv_weight,
    value_bias,
    out_weight,
    out_bias,
    norm2_gain,
    norm2_shift,
    up_weight,
    up_bias,
    down_weight,
    down_bias,
):
    local_rows = tokens.shape[0]
    dp_count = lax.axis_size("dp")
    tensor_count = lax.axis_size("tensor")
    tensor_rank = lax.axis_index("tensor")
    slot_rows = local_rows // dp_count
    layer_total = query_weight.shape[0]
    group_rows = local_rows * tensor_count
    query_cols = query_weight.shape[2]
    pair_width = kv_weight.shape[2]
    hidden_cols = up_weight.shape[2]
    head_count = query_cols // HEAD
    score_scale = HEAD ** (-0.5)
    target_dev = deal // local_rows // tensor_count
    target_row = deal % local_rows
    dev_ids = jnp.arange(dp_count, dtype=jnp.int32)
    dev_match = (target_dev[:, None] == dev_ids[None, :]).astype(jnp.int32)
    earlier = jnp.cumsum(dev_match, axis=0) - dev_match
    slot_of = target_dev * slot_rows + jnp.sum(earlier * dev_match, axis=1)
    row_ids = jnp.arange(local_rows, dtype=jnp.int32)
    send_mask = row_ids[:, None] == slot_of[None, :]
    send_table = send_mask.astype(jnp.bfloat16)
    sent_place = jnp.sum(jnp.where(send_mask, target_row[None, :], 0), axis=1)
    arrived_place = lax.all_to_all(sent_place, "dp", split_axis=0, concat_axis=0, tiled=True)
    tokens_sent = matmul(send_table, tokens).astype(jnp.bfloat16)
    tangent_sent = matmul(send_table, cotangent).astype(jnp.bfloat16)
    tokens_come, tangent_come = (
        lax.all_to_all(tokens_sent, "dp", split_axis=0, concat_axis=0, tiled=True),
        lax.all_to_all(tangent_sent, "dp", split_axis=0, concat_axis=0, tiled=True),
    )
    place_table = (row_ids[:, None] == arrived_place[None, :]).astype(jnp.bfloat16)
    stream = matmul(place_table, tokens_come)
    tangent = matmul(place_table, tangent_come)
    places = jnp.arange(group_rows, dtype=jnp.int32)
    allowed = (places[None, :] <= places[:, None]) & (segment[:, None] == segment[None, :])
    saved = []
    kept_weights = []
    for layer_index in range(layer_total):
        w_query, w_pair, w_out, w_up, w_down = (
            lax.all_gather(query_weight[layer_index], "dp", axis=0, tiled=True),
            lax.all_gather(kv_weight[layer_index], "dp", axis=0, tiled=True),
            lax.all_gather(out_weight[layer_index], "dp", axis=1, tiled=True),
            lax.all_gather(up_weight[layer_index], "dp", axis=0, tiled=True),
            lax.all_gather(down_weight[layer_index], "dp", axis=1, tiled=True),
        )
        kept_weights.append(None)
        normed_one = layer_norm(stream, norm1_gain[layer_index], norm1_shift[layer_index]).astype(
            jnp.bfloat16
        )
        normed_all = rows_gather(normed_one)
        queries = (matmul(normed_all, w_query) + query_bias[layer_index]).astype(jnp.bfloat16)
        full_bias = jnp.concatenate([jnp.zeros((HEAD,), jnp.float32), value_bias[layer_index]])
        pair_bias = lax.dynamic_slice_in_dim(full_bias, tensor_rank * pair_width, pair_width)
        pair_local = (matmul(normed_all, w_pair) + pair_bias).astype(jnp.bfloat16)
        pair_all = lax.all_gather(pair_local, "tensor", axis=1, tiled=True)
        key_rows = pair_all[:, :HEAD]
        value_rows = pair_all[:, HEAD:]
        query_heads = jnp.transpose(queries.reshape(group_rows, head_count, HEAD), (1, 0, 2))

        def attend(query_one):
            scores = jnp.where(allowed, contract_cols(query_one, key_rows) * score_scale, -1e30)
            row_top = jnp.max(scores, axis=-1, keepdims=True)
            exp_score = jnp.exp(scores - row_top)
            row_total = jnp.sum(exp_score, axis=-1, keepdims=True)
            weights = (exp_score / row_total).astype(jnp.bfloat16)
            return (matmul(weights, value_rows), (row_top + jnp.log(row_total))[:, 0])

        head_outs, log_totals = lax.map(attend, query_heads)
        mixed = (
            jnp.transpose(head_outs, (1, 0, 2)).reshape(group_rows, query_cols).astype(jnp.bfloat16)
        )
        hidden_state = stream + rows_scatter(mixed, w_out) + out_bias[layer_index]
        normed_two = layer_norm(
            hidden_state, norm2_gain[layer_index], norm2_shift[layer_index]
        ).astype(jnp.bfloat16)
        normed_two_all = rows_gather(normed_two)
        pre_gelu = matmul(normed_two_all, w_up) + up_bias[layer_index]
        activation = gelu_tanh(pre_gelu).astype(jnp.bfloat16)
        saved.append(
            (
                stream,
                normed_all,
                queries,
                pair_all,
                log_totals,
                mixed,
                hidden_state,
                normed_two_all,
                pre_gelu,
                activation,
            )
        )
        stream = hidden_state + rows_scatter(activation, w_down) + down_bias[layer_index]
    layer_out = stream.astype(jnp.bfloat16)
    reduced_by_layer = [None] * layer_total
    small_by_layer = [None] * layer_total
    for layer_index in reversed(range(layer_total)):
        (
            stream_in,
            normed_all,
            queries,
            pair_all,
            log_totals,
            mixed,
            hidden_state,
            normed_two_all,
            pre_gelu,
            activation,
        ) = saved[layer_index]
        w_query, w_pair, w_out, w_up, w_down = (
            lax.all_gather(query_weight[layer_index], "dp", axis=0, tiled=True),
            lax.all_gather(kv_weight[layer_index], "dp", axis=0, tiled=True),
            lax.all_gather(out_weight[layer_index], "dp", axis=1, tiled=True),
            lax.all_gather(up_weight[layer_index], "dp", axis=0, tiled=True),
            lax.all_gather(down_weight[layer_index], "dp", axis=1, tiled=True),
        )
        key_rows = pair_all[:, :HEAD]
        value_rows = pair_all[:, HEAD:]
        branch_grad = tangent.astype(jnp.bfloat16)
        down_bias_part = jnp.sum(branch_grad.astype(jnp.float32), axis=0)
        branch_all = grad_gather(branch_grad)
        down_grad = contract_rows(activation, branch_all)
        act_grad = contract_cols(branch_all, w_down)
        pre_grad = jax.vjp(gelu_tanh, pre_gelu)[1](act_grad)[0].astype(jnp.bfloat16)
        up_bias_part = jnp.sum(pre_grad.astype(jnp.float32), axis=0)
        up_grad = contract_rows(normed_two_all, pre_grad)
        normed_two_grad = grad_scatter(((pre_grad, w_up),))
        norm_pull_two = jax.vjp(
            layer_norm, hidden_state, norm2_gain[layer_index], norm2_shift[layer_index]
        )[1]
        hidden_part, gain_two_part, shift_two_part = norm_pull_two(normed_two_grad)
        hidden_grad = tangent + hidden_part
        attn_grad = hidden_grad.astype(jnp.bfloat16)
        out_bias_part = jnp.sum(attn_grad.astype(jnp.float32), axis=0)
        attn_all = grad_gather(attn_grad)
        out_grad = contract_rows(mixed, attn_all)
        mixed_grad = contract_cols(attn_all, w_out).astype(jnp.bfloat16)
        query_heads = jnp.transpose(queries.reshape(group_rows, head_count, HEAD), (1, 0, 2))
        dout_heads = jnp.transpose(mixed_grad.reshape(group_rows, head_count, HEAD), (1, 0, 2))

        def attend_back(carried, inputs):
            query_one, dout_one, log_one = inputs
            scores = jnp.where(allowed, contract_cols(query_one, key_rows) * score_scale, -1e30)
            probs = jnp.exp(scores - log_one[:, None])
            prob_grad = contract_cols(dout_one, value_rows)
            inner = jnp.sum(probs * prob_grad, axis=-1, keepdims=True)
            score_grad = (probs * (prob_grad - inner) * score_scale).astype(jnp.bfloat16)
            key_acc = carried[0] + contract_rows(score_grad, query_one)
            value_acc = carried[1] + contract_rows(probs.astype(jnp.bfloat16), dout_one)
            return ((key_acc, value_acc), matmul(score_grad, key_rows))

        start_acc = (
            jnp.zeros((group_rows, HEAD), jnp.float32),
            jnp.zeros((group_rows, HEAD), jnp.float32),
        )
        (key_grad, value_grad), query_grads = lax.scan(
            attend_back, start_acc, (query_heads, dout_heads, log_totals)
        )
        query_grad = (
            jnp.transpose(query_grads, (1, 0, 2))
            .reshape(group_rows, query_cols)
            .astype(jnp.bfloat16)
        )
        query_bias_part = jnp.sum(query_grad.astype(jnp.float32), axis=0)
        pair_part = jnp.concatenate([key_grad, value_grad], axis=1)
        pair_grad = lax.psum_scatter(
            pair_part.astype(jnp.bfloat16), "tensor", scatter_dimension=1, tiled=True
        )
        pair_bias_part = jnp.sum(pair_grad.astype(jnp.float32), axis=0)
        query_w_grad = contract_rows(normed_all, query_grad)
        pair_w_grad = contract_rows(normed_all, pair_grad)
        normed_grad = grad_scatter(((query_grad, w_query), (pair_grad, w_pair)))
        norm_pull_one = jax.vjp(
            layer_norm, stream_in, norm1_gain[layer_index], norm1_shift[layer_index]
        )[1]
        stream_part, gain_one_part, shift_one_part = norm_pull_one(normed_grad)
        tangent = hidden_grad + stream_part
        small_by_layer[layer_index] = (
            gain_one_part,
            shift_one_part,
            place_slice(query_bias_part, query_cols * tensor_count, tensor_rank),
            place_slice(pair_bias_part, pair_width * tensor_count, tensor_rank),
            out_bias_part,
            gain_two_part,
            shift_two_part,
            place_slice(up_bias_part, hidden_cols * tensor_count, tensor_rank),
            down_bias_part,
        )
        reduced_by_layer[layer_index] = (
            lax.psum_scatter(
                query_w_grad.astype(jnp.bfloat16), "dp", scatter_dimension=0, tiled=True
            ).astype(jnp.float32),
            lax.psum_scatter(
                pair_w_grad.astype(jnp.bfloat16), "dp", scatter_dimension=0, tiled=True
            ).astype(jnp.float32),
            lax.psum_scatter(
                out_grad.astype(jnp.bfloat16), "dp", scatter_dimension=1, tiled=True
            ).astype(jnp.float32),
            lax.psum_scatter(
                up_grad.astype(jnp.bfloat16), "dp", scatter_dimension=0, tiled=True
            ).astype(jnp.float32),
            lax.psum_scatter(
                down_grad.astype(jnp.bfloat16), "dp", scatter_dimension=1, tiled=True
            ).astype(jnp.float32),
        )
    summed = [
        jnp.stack([reduced_by_layer[layer_index][member] for layer_index in range(layer_total)])
        for member in range(5)
    ]
    smalls = [
        jnp.stack([small_by_layer[layer_index][member] for layer_index in range(layer_total)])
        for member in range(9)
    ]
    (
        gain_one_sum,
        shift_one_sum,
        query_bias_sum,
        pair_bias_sum,
        out_bias_sum,
        gain_two_sum,
        shift_two_sum,
        up_bias_sum,
        down_bias_sum,
    ) = lax.psum(
        (
            smalls[0],
            smalls[1],
            smalls[2],
            smalls[3],
            smalls[4],
            smalls[5],
            smalls[6],
            smalls[7],
            smalls[8],
        ),
        ("dp", "tensor"),
    )
    query_bias_grad = lax.dynamic_slice_in_dim(
        query_bias_sum, tensor_rank * query_cols, query_cols, 1
    )
    up_bias_grad = lax.dynamic_slice_in_dim(up_bias_sum, tensor_rank * hidden_cols, hidden_cols, 1)
    value_bias_grad = pair_bias_sum[:, HEAD:]
    out_slots = contract_rows(place_table, layer_out).astype(jnp.bfloat16)
    grad_slots = contract_rows(place_table, tangent.astype(jnp.bfloat16)).astype(jnp.bfloat16)
    out_back, grad_back = (
        lax.all_to_all(out_slots, "dp", split_axis=0, concat_axis=0, tiled=True),
        lax.all_to_all(grad_slots, "dp", split_axis=0, concat_axis=0, tiled=True),
    )
    layer_rows = contract_rows(send_table, out_back).astype(jnp.bfloat16)
    token_rows = contract_rows(send_table, grad_back).astype(jnp.bfloat16)
    return (
        layer_rows,
        token_rows,
        gain_one_sum,
        shift_one_sum,
        summed[0],
        query_bias_grad,
        summed[1],
        value_bias_grad,
        summed[2],
        out_bias_sum,
        gain_two_sum,
        shift_two_sum,
        summed[3],
        up_bias_grad,
        summed[4],
        down_bias_sum,
    )


def solution(mesh):
    in_specs = (
        P(("dp", "tensor"), None),
        P(("dp", "tensor"), None),
        P(("dp", "tensor")),
        P("dp"),
        P(),
        P(),
        P(None, "dp", "tensor"),
        P(None, "tensor"),
        P(None, "dp", "tensor"),
        P(),
        P(None, "tensor", "dp"),
        P(),
        P(),
        P(),
        P(None, "dp", "tensor"),
        P(None, "tensor"),
        P(None, "tensor", "dp"),
        P(),
    )
    out_specs = (
        P(("dp", "tensor"), None),
        P(("dp", "tensor"), None),
        P(),
        P(),
        P(None, "dp", "tensor"),
        P(None, "tensor"),
        P(None, "dp", "tensor"),
        P(),
        P(None, "tensor", "dp"),
        P(),
        P(),
        P(),
        P(None, "dp", "tensor"),
        P(None, "tensor"),
        P(None, "tensor", "dp"),
        P(),
    )
    return jax.shard_map(local, mesh=mesh, in_specs=in_specs, out_specs=out_specs, check_vma=False)
```

profile of v0, /device:TPU:0, one launch (start us, length us, event | category | flops | bytes accessed | tf_op | source)
XLA Modules:
  0.0 2494.6 jit_solution(4482688082752972419)
XLA Ops:
  9.8 5.2 all-to-all-start
  25.6 10.0 all-to-all-done.1
  41.3 8.8 all-gather.1
  50.9 50.5 %all-gather.27.cloned.1.call-done = bf16[768,2048]{1,0:T(8,128)(2,1)} async-done(((bf16[192,2048]{1,0:T(8,128)(2,1)}), bf16[768,2048]{1,0:T(8,128)(2,1)}) %all-gather.27.cloned.1.call-update) | async-done | bytes 3145744 | tf_op jit(solution)/shard_map/all_gather | solution.py:40
  104.3 15.1 all_gather.73
  119.7 10.7 all-gather.43.cloned.1.call-done
  135.8 34.1 %while.56 = (s32[]{:T(128)}, bf16[4,768,128]{1,2,0:T(8,128)(2,1)S(1)}, f32[4,768]{1,0:T(4,128)}, bf16[4,768,128]{2,1,0:T(8,128)(2,1)S(1)}, bf16[768,128]{1,0:T(8...) while((s32[]{:T(128)}, ...), condition=%wide.region_9.10_spmd.clone, body=%wide.region_6.9_spmd.clone.sunk | while | flops 308477184 | bytes 8108645 | solution.py:154
  170.0 5.7 convolution_convert_fusion.5
  179.2 56.9 %reduce-scatter.25.cloned.1.call-done = bf16[192,2048]{1,0:T(8,128)(2,1)} async-done(((bf16[768,2048]{1,0:T(8,128)(2,1)}), bf16[192,2048]{1,0:T(8,128)(2,1)}) %reduce-scatter.25.cloned.1.call-update) | async-done | bytes 786448 | tf_op jit(solution)/shard_map/reduce_scatter | solution.py:48
  242.8 50.0 %all-gather.47.cloned.1.call-done = bf16[1,2048,2048]{2,1,0:T(8,128)(2,1)} async-done(((bf16[1,256,2048]{2,1,0:T(8,128)(2,1)}), bf16[1,2048,2048]{2,1,0:T(8,128)(2,1)}) %all-gather.47.cloned.1.call-update) | async-done | bytes 8388624 | tf_op jit(solution)/shard_map/all_gather | solution.py:129
  292.9 65.5 %all-gather.29.cloned.1.call-done = bf16[768,2048]{1,0:T(8,128)(2,1)} async-done(((bf16[192,2048]{1,0:T(8,128)(2,1)}), bf16[768,2048]{1,0:T(8,128)(2,1)}) %all-gather.29.cloned.1.call-update) | async-done | bytes 3145744 | tf_op jit(solution)/shard_map/all_gather | solution.py:40
  358.4 11.7 fusion.66
  370.1 45.4 %all-gather.49.cloned.1.call-done = bf16[1,2048,2048]{2,1,0:T(8,128)(2,1)} async-done(((bf16[1,2048,256]{2,1,0:T(8,128)(2,1)}), bf16[1,2048,2048]{2,1,0:T(8,128)(2,1)}) %all-gather.49.cloned.1.call-update) | async-done | bytes 8388624 | tf_op jit(solution)/shard_map/all_gather | solution.py:130
  415.5 13.1 fusion.85
  430.0 59.0 %reduce-scatter.27.cloned.1.call-done = bf16[192,2048]{1,0:T(8,128)(2,1)} async-done(((bf16[768,2048]{1,0:T(8,128)(2,1)}), bf16[192,2048]{1,0:T(8,128)(2,1)}) %reduce-scatter.27.cloned.1.call-update) | async-done | bytes 786448 | tf_op jit(solution)/shard_map/reduce_scatter | solution.py:48
  493.0 11.0 all-gather.6
  504.0 14.9 all-gather.51.cloned.1.call-done
  518.9 65.5 %all-gather.31.cloned.1.call-done = bf16[768,2048]{1,0:T(8,128)(2,1)} async-done(((bf16[192,2048]{1,0:T(8,128)(2,1)}), bf16[768,2048]{1,0:T(8,128)(2,1)}) %all-gather.31.cloned.1.call-update) | async-done | bytes 3145744 | tf_op jit(solution)/shard_map/all_gather | solution.py:40
  584.4 5.3 add_convert_fusion.5
  594.3 15.1 all_gather.81
  611.0 33.6 %while.57 = (s32[]{:T(128)}, bf16[4,768,128]{1,2,0:T(8,128)(2,1)S(1)}, f32[4,768]{1,0:T(4,128)}, bf16[4,768,128]{2,1,0:T(8,128)(2,1)S(1)}, bf16[768,128]{1,0:T(8...) while((s32[]{:T(128)}, ...), condition=%wide.region_19.20_spmd.clone, body=%wide.region_16.19_spmd.clone.sunk | while | flops 308477184 | bytes 8108645 | solution.py:154
  644.7 5.7 convolution_convert_fusion.4
  651.2 57.8 %reduce-scatter.29.cloned.1.call-done = bf16[192,2048]{1,0:T(8,128)(2,1)} async-done(((bf16[768,2048]{1,0:T(8,128)(2,1)}), bf16[192,2048]{1,0:T(8,128)(2,1)}) %reduce-scatter.29.cloned.1.call-update) | async-done | bytes 786448 | tf_op jit(solution)/shard_map/reduce_scatter | solution.py:48
  712.6 22.7 all_to_all.57
  738.0 32.3 %all-gather.55.cloned.1.call-done = bf16[1,2048,2048]{2,1,0:T(8,128)(2,1)} async-done(((bf16[1,256,2048]{2,1,0:T(8,128)(2,1)}), bf16[1,2048,2048]{2,1,0:T(8,128)(2,1)}) %all-gather.55.cloned.1.call-update) | async-done | bytes 8388624 | tf_op jit(solution)/shard_map/all_gather | solution.py:129
  770.2 65.5 %all-gather.33.cloned.1.call-done = bf16[768,2048]{1,0:T(8,128)(2,1)} async-done(((bf16[192,2048]{1,0:T(8,128)(2,1)}), bf16[768,2048]{1,0:T(8,128)(2,1)}) %all-gather.33.cloned.1.call-update) | async-done | bytes 3145744 | tf_op jit(solution)/shard_map/all_gather | solution.py:40
  835.7 11.8 fusion.58
  847.5 52.4 %all-gather.35.cloned.1.call-done = bf16[768,2048]{1,0:T(8,128)(2,1)} async-done(((bf16[192,2048]{1,0:T(8,128)(2,1)}), bf16[768,2048]{1,0:T(8,128)(2,1)}) %all-gather.35.cloned.1.call-update) | async-done | bytes 3145744 | tf_op jit(solution)/shard_map/all_gather | solution.py:44
  899.9 56.9 %all-gather.57.cloned.1.call-done = bf16[1,2048,2048]{2,1,0:T(8,128)(2,1)} async-done(((bf16[1,2048,256]{2,1,0:T(8,128)(2,1)}), bf16[1,2048,2048]{2,1,0:T(8,128)(2,1)}) %all-gather.57.cloned.1.call-update) | async-done | bytes 8388624 | tf_op jit(solution)/shard_map/all_gather | solution.py:130
  956.9 15.4 convert_reduce_fusion
  973.9 8.1 fusion.88
  982.1 60.4 %reduce-scatter.33.cloned.1.call-done = bf16[192,2048]{1,0:T(8,128)(2,1)} async-done(((bf16[768,2048]{1,0:T(8,128)(2,1)}), bf16[192,2048]{1,0:T(8,128)(2,1)}) %reduce-scatter.33.cloned.1.call-update) | async-done | bytes 786448 | tf_op jit(solution)/shard_map/reduce_scatter | solution.py:58
  1047.8 63.4 %all-gather.37.cloned.1.call-done = bf16[768,2048]{1,0:T(8,128)(2,1)} async-done(((bf16[192,2048]{1,0:T(8,128)(2,1)}), bf16[768,2048]{1,0:T(8,128)(2,1)}) %all-gather.37.cloned.1.call-update) | async-done | bytes 3145744 | tf_op jit(solution)/shard_map/all_gather | solution.py:44
  1116.9 44.3 %while.58 = (s32[]{:T(128)}, f32[768,128]{1,0:T(8,128)}, f32[768,128]{1,0:T(8,128)}, bf16[4,768,128]{1,2,0:T(8,128)(2,1)}, bf16[4,768,128]{2,1,0:T(8,128)(2,1)},...) while((s32[]{:T(128)}, f32[768,128]{1,0:T(8,128)}, ...), condition=%wide.region_29.30_spmd.clone, body=%wide.region_27.29_spmd.clone.sunk | while | flops 763034880 | bytes 28140772 | solution.py:242
  1164.4 5.7 fusion.101
  1170.0 13.7 reduce-scatter.61.cloned.1.call-done
  1183.7 5.5 add_convert_fusion.1
  1189.3 58.6 %reduce-scatter.35.cloned.1.call-done = bf16[192,2048]{1,0:T(8,128)(2,1)} async-done(((bf16[768,2048]{1,0:T(8,128)(2,1)}), bf16[192,2048]{1,0:T(8,128)(2,1)}) %reduce-scatter.35.cloned.1.call-update) | async-done | bytes 786448 | tf_op jit(solution)/shard_map/reduce_scatter | solution.py:58
  1256.2 63.2 %all-gather.39.cloned.1.call-done = bf16[768,2048]{1,0:T(8,128)(2,1)} async-done(((bf16[192,2048]{1,0:T(8,128)(2,1)}), bf16[768,2048]{1,0:T(8,128)(2,1)}) %all-gather.39.cloned.1.call-update) | async-done | bytes 3145744 | tf_op jit(solution)/shard_map/all_gather | solution.py:44
  1319.4 14.7 convert_reduce_fusion.1
  1335.8 10.2 fusion.82
  1346.1 59.0 %reduce-scatter.37.cloned.1.call-done = bf16[192,2048]{1,0:T(8,128)(2,1)} async-done(((bf16[768,2048]{1,0:T(8,128)(2,1)}), bf16[192,2048]{1,0:T(8,128)(2,1)}) %reduce-scatter.37.cloned.1.call-update) | async-done | bytes 786448 | tf_op jit(solution)/shard_map/reduce_scatter | solution.py:58
  1411.3 63.4 %all-gather.41.cloned.1.call-done = bf16[768,2048]{1,0:T(8,128)(2,1)} async-done(((bf16[192,2048]{1,0:T(8,128)(2,1)}), bf16[768,2048]{1,0:T(8,128)(2,1)}) %all-gather.41.cloned.1.call-update) | async-done | bytes 3145744 | tf_op jit(solution)/shard_map/all_gather | solution.py:44
  1480.6 39.8 %while.59 = (s32[]{:T(128)}, f32[768,128]{1,0:T(8,128)}, f32[768,128]{1,0:T(8,128)}, bf16[4,768,128]{1,2,0:T(8,128)(2,1)}, bf16[4,768,128]{2,1,0:T(8,128)(2,1)},...) while((s32[]{:T(128)}, f32[768,128]{1,0:T(8,128)}, ...), condition=%wide.region_39.40_spmd.clone, body=%wide.region_37.39_spmd.clone.sunk | while | flops 763034880 | bytes 28927240 | solution.py:242
  1523.5 13.1 fusion.91
  1545.4 12.6 convolution_convert_fusion
  1558.7 12.6 convolution_convert_fusion.1
  1580.6 10.9 convolution_convert_fusion.2
  1593.4 10.8 convolution_convert_fusion.3
  1610.5 5.4 convolution_convert_fusion.7
  1629.0 12.4 all-to-all-done.2
  1647.6 80.4 %all-reduce.7.cloned.1.call-done = f32[2,8192]{1,0:T(2,128)} async-done(((f32[2,8192]{1,0:T(2,128)}), f32[2,8192]{1,0:T(2,128)}) %all-reduce.7.cloned.1.call-update) | async-done | bytes 65552 | tf_op jit(solution)/shard_map/psum | solution.py:310
  1738.0 27.2 %reduce-scatter.47.cloned.1.call-done = bf16[256,64]{0,1:T(8,128)(2,1)} async-done(((bf16[2048,64]{0,1:T(8,128)(2,1)}), bf16[256,64]{0,1:T(8,128)(2,1)}) %reduce-scatter.47.cloned.1.call-update) | async-done | bytes 32784 | tf_op jit(solution)/shard_map/reduce_scatter | solution.py:279
  1765.2 36.9 %reduce-scatter.45.cloned.1.call-done = bf16[256,64]{0,1:T(8,128)(2,1)} async-done(((bf16[2048,64]{0,1:T(8,128)(2,1)}), bf16[256,64]{0,1:T(8,128)(2,1)}) %reduce-scatter.45.cloned.1.call-update) | async-done | bytes 32784 | tf_op jit(solution)/shard_map/reduce_scatter | solution.py:279
  1803.6 73.3 %reduce-scatter.59.cloned.1.call-done = bf16[2048,256]{1,0:T(8,128)(2,1)} async-done(((bf16[2048,2048]{1,0:T(8,128)(2,1)}), bf16[2048,256]{1,0:T(8,128)(2,1)}) %reduce-scatter.59.cloned.1.call-update) | async-done | bytes 1048592 | tf_op jit(solution)/shard_map/reduce_scatter | solution.py:288
  1876.9 75.0 %reduce-scatter.57.cloned.1.call-done = bf16[2048,256]{1,0:T(8,128)(2,1)} async-done(((bf16[2048,2048]{1,0:T(8,128)(2,1)}), bf16[2048,256]{1,0:T(8,128)(2,1)}) %reduce-scatter.57.cloned.1.call-update) | async-done | bytes 1048592 | tf_op jit(solution)/shard_map/reduce_scatter | solution.py:288
  1955.9 59.2 %reduce-scatter.39.cloned.1.call-done = bf16[192,2048]{1,0:T(8,128)(2,1)} async-done(((bf16[768,2048]{1,0:T(8,128)(2,1)}), bf16[192,2048]{1,0:T(8,128)(2,1)}) %reduce-scatter.39.cloned.1.call-update) | async-done | bytes 786448 | tf_op jit(solution)/shard_map/reduce_scatter | solution.py:58
  2024.5 65.4 %reduce-scatter.55.cloned.1.call-done = bf16[256,2048]{1,0:T(8,128)(2,1)} async-done(((bf16[2048,2048]{1,0:T(8,128)(2,1)}), bf16[256,2048]{1,0:T(8,128)(2,1)}) %reduce-scatter.55.cloned.1.call-update) | async-done | bytes 1048592 | tf_op jit(solution)/shard_map/reduce_scatter | solution.py:285
  2089.9 75.0 %reduce-scatter.53.cloned.1.call-done = bf16[256,2048]{1,0:T(8,128)(2,1)} async-done(((bf16[2048,2048]{1,0:T(8,128)(2,1)}), bf16[256,2048]{1,0:T(8,128)(2,1)}) %reduce-scatter.53.cloned.1.call-update) | async-done | bytes 1048592 | tf_op jit(solution)/shard_map/reduce_scatter | solution.py:285
  2168.8 40.7 %reduce-scatter.51.cloned.1.call-done = bf16[512,256]{1,0:T(8,128)(2,1)} async-done(((bf16[512,2048]{1,0:T(8,128)(2,1)}), bf16[512,256]{1,0:T(8,128)(2,1)}) %reduce-scatter.51.cloned.1.call-update) | async-done | bytes 262160 | tf_op jit(solution)/shard_map/reduce_scatter | solution.py:282
  2209.5 44.9 %reduce-scatter.49.cloned.1.call-done = bf16[512,256]{1,0:T(8,128)(2,1)} async-done(((bf16[512,2048]{1,0:T(8,128)(2,1)}), bf16[512,256]{1,0:T(8,128)(2,1)}) %reduce-scatter.49.cloned.1.call-update) | async-done | bytes 262160 | tf_op jit(solution)/shard_map/reduce_scatter | solution.py:282
  2257.2 41.6 %reduce-scatter.43.cloned.1.call-done = bf16[256,512]{1,0:T(8,128)(2,1)} async-done(((bf16[2048,512]{1,0:T(8,128)(2,1)}), bf16[256,512]{1,0:T(8,128)(2,1)}) %reduce-scatter.43.cloned.1.call-update) | async-done | bytes 262160 | tf_op jit(solution)/shard_map/reduce_scatter | solution.py:276
  2298.8 44.8 %reduce-scatter.41.cloned.1.call-done = bf16[256,512]{1,0:T(8,128)(2,1)} async-done(((bf16[2048,512]{1,0:T(8,128)(2,1)}), bf16[256,512]{1,0:T(8,128)(2,1)}) %reduce-scatter.41.cloned.1.call-update) | async-done | bytes 262160 | tf_op jit(solution)/shard_map/reduce_scatter | solution.py:276
  2345.6 130.5 %all-reduce.9.cloned.1.call-done = (f32[2,2048]{1,0:T(2,128)}, f32[2,2048]{1,0:T(2,128)}, f32[2,2048]{1,0:T(2,128)}, f32[2,256]{1,0:T(2,128)}, f32[2,2048]{1,0:T...) async-done(((f32[2,2048]{1,0:T(2,128)}, f32[2,2048]{1,0:T(2,128)}, f32[2,2048]{1,0:T(2,128)}, f32[2,256]{1,0:T(2,128)}, f32[2,2048]{1,0:T(2,128)}, ...) | async-done | bytes 116752 | tf_op jit(solution)/shard_map/psum | solution.py:310
  (616 shorter events, 339.9 us)
Async XLA Ops:
  9.0 703.2 %copy-start.63 = (s32[192]{0:T(256)}, s32[192]{0:T(256)S(1)}, u32[]{:S(2)}) copy-start(s32[192]{0:T(256)S(1)} %multiply_add_fusion.4) | copy-start | bytes 2308
  9.8 9.8 all-to-all-start
  19.5 16.1 all-to-all-start.1
  23.1 78.2 %all-gather.27.cloned.1.call-start = ((), (), s32[]{:S(2)}) async-start(), calls=%async_computation.25 | async-start | bytes 3932160 | tf_op jit(solution)/shard_map/all_gather | solution.py:40
  36.1 200.0 %copy-start.4 = (f32[192,2048]{1,0:T(8,128)}, f32[192,2048]{1,0:T(8,128)S(1)}, u32[]{:S(2)}) copy-start(f32[192,2048]{1,0:T(8,128)S(1)} %get-tuple-element.604) | copy-start | bytes 4718596
  38.3 92.1 %all-gather.43.cloned.1.call-start = ((), (), s32[]{:S(2)}) async-start(), calls=%async_computation.52 | async-start | bytes 2359296 | tf_op jit(solution)/shard_map/all_gather | solution.py:126
  39.2 130.8 %all-gather.45.cloned.1.call-start = ((), (), s32[]{:S(2)}) async-start(), calls=%async_computation.53 | async-start | bytes 2359296 | tf_op jit(solution)/shard_map/all_gather | solution.py:128
  40.1 196.0 %reduce-scatter.25.cloned.1.call-start = ((), (), s32[]{:S(2)}) async-start(), calls=%async_computation.26 | async-start | bytes 3932160 | tf_op jit(solution)/shard_map/reduce_scatter | solution.py:48
  50.2 69.2 %copy-start.40 = (bf16[1,2048,64]{1,2,0:T(8,128)(2,1)}, bf16[1,2048,64]{1,2,0:T(8,128)(2,1)S(1)}, u32[]{:S(2)}) copy-start(bf16[1,2048,64]{1,2,0:T(8,128)(2,1)S(1)} %all-gather.1) | copy-start | bytes 786436
  175.8 117.1 %all-gather.47.cloned.1.call-start = ((), (), s32[]{:S(2)}) async-start(), calls=%async_computation.54 | async-start | bytes 9437184 | tf_op jit(solution)/shard_map/all_gather | solution.py:129
  179.0 179.4 %all-gather.29.cloned.1.call-start = ((), (), s32[]{:S(2)}) async-start(), calls=%async_computation.27 | async-start | bytes 3932160 | tf_op jit(solution)/shard_map/all_gather | solution.py:40
  237.5 251.5 %copy-start.8 = (f32[192,2048]{1,0:T(8,128)}, f32[192,2048]{1,0:T(8,128)S(1)}, u32[]{:S(2)}) copy-start(f32[192,2048]{1,0:T(8,128)S(1)} %get-tuple-element.560) | copy-start | bytes 4718596
  239.2 176.3 %all-gather.49.cloned.1.call-start = ((), (), s32[]{:S(2)}) async-start(), calls=%async_computation.55 | async-start | bytes 9437184 | tf_op jit(solution)/shard_map/all_gather | solution.py:130
  242.3 246.7 %reduce-scatter.27.cloned.1.call-start = ((), (), s32[]{:S(2)}) async-start(), calls=%async_computation.28 | async-start | bytes 3932160 | tf_op jit(solution)/shard_map/reduce_scatter | solution.py:48
  242.8 172.7 %copy-start.101 = (f32[1,2048]{1,0:T(1,128)}, f32[1,2048]{1,0:T(1,128)S(1)}, u32[]{:S(2)}) copy-start(f32[1,2048]{1,0:T(1,128)S(1)} %get-tuple-element.586) | copy-start | bytes 24580
  242.8 714.0 %copy-start.104 = (f32[1,2048]{1,0:T(1,128)}, f32[1,2048]{1,0:T(1,128)S(1)}, u32[]{:S(2)}) copy-start(f32[1,2048]{1,0:T(1,128)S(1)} %get-tuple-element.585) | copy-start | bytes 24580
  428.6 90.3 %all-gather.51.cloned.1.call-start = ((), (), s32[]{:S(2)}) async-start(), calls=%async_computation.56 | async-start | bytes 2359296 | tf_op jit(solution)/shard_map/all_gather | solution.py:126
  429.3 155.0 %all-gather.31.cloned.1.call-start = ((), (), s32[]{:S(2)}) async-start(), calls=%async_computation.29 | async-start | bytes 3932160 | tf_op jit(solution)/shard_map/all_gather | solution.py:40
  490.5 218.6 %copy-start.2 = (f32[192,2048]{1,0:T(8,128)}, f32[192,2048]{1,0:T(8,128)S(1)}, u32[]{:S(2)}) copy-start(f32[192,2048]{1,0:T(8,128)S(1)} %get-tuple-element.558) | copy-start | bytes 4718596
  490.5 93.9 %copy-start.107 = (f32[1,512]{1,0:T(1,128)S(1)}, f32[1,512]{1,0:T(1,128)}, u32[]{:S(2)}) copy-start(f32[1,512]{1,0:T(1,128)} %get-tuple-element.597) | copy-start | bytes 6148
  490.8 98.8 %copy-start.98 = (f32[192]{0:T(256)}, f32[192]{0:T(256)S(1)}, u32[]{:S(2)}) copy-start(f32[192]{0:T(256)S(1)} %multiply_reduce_fusion.3) | copy-start | bytes 2308
  490.9 98.8 %copy-start.90 = (f32[192]{0:T(256)}, f32[192]{0:T(256)S(1)}, u32[]{:S(2)}) copy-start(f32[192]{0:T(256)S(1)} %fusion.162) | copy-start | bytes 2308
  492.2 152.5 %all-gather.53.cloned.1.call-start = ((), (), s32[]{:S(2)}) async-start(), calls=%async_computation.57 | async-start | bytes 2359296 | tf_op jit(solution)/shard_map/all_gather | solution.py:128
  492.9 216.2 %reduce-scatter.29.cloned.1.call-start = ((), (), s32[]{:S(2)}) async-start(), calls=%async_computation.30 | async-start | bytes 3932160 | tf_op jit(solution)/shard_map/reduce_scatter | solution.py:48
  504.0 87.2 %copy-start.42 = (bf16[1,2048,64]{1,2,0:T(8,128)(2,1)}, bf16[1,2048,64]{1,2,0:T(8,128)(2,1)S(1)}, u32[]{:S(2)}) copy-start(bf16[1,2048,64]{1,2,0:T(8,128)(2,1)S(1)} %all-gather.6) | copy-start | bytes 786436
  650.4 119.8 %all-gather.55.cloned.1.call-start = ((), (), s32[]{:S(2)}) async-start(), calls=%async_computation.58 | async-start | bytes 9437184 | tf_op jit(solution)/shard_map/all_gather | solution.py:129
  651.2 184.6 %all-gather.33.cloned.1.call-start = ((), (), s32[]{:S(2)}) async-start(), calls=%async_computation.31 | async-start | bytes 3932160 | tf_op jit(solution)/shard_map/all_gather | solution.py:40
  710.5 334.4 %copy-start.6 = (f32[192,2048]{1,0:T(8,128)}, f32[192,2048]{1,0:T(8,128)S(1)}, u32[]{:S(2)}) copy-start(f32[192,2048]{1,0:T(8,128)S(1)} %get-tuple-element.556) | copy-start | bytes 4718596
  712.1 187.8 %all-gather.35.cloned.1.call-start = ((), (), s32[]{:S(2)}) async-start(), calls=%async_computation.33 | async-start | bytes 3932160 | tf_op jit(solution)/shard_map/all_gather | solution.py:44
  737.1 308.3 %copy-start.15 = (f32[192,2048]{1,0:T(8,128)}, f32[192,2048]{1,0:T(8,128)S(1)}, u32[]{:S(2)}) copy-start(f32[192,2048]{1,0:T(8,128)S(1)} %get-tuple-element.605) | copy-start | bytes 4718596
  737.2 219.7 %all-gather.57.cloned.1.call-start = ((), (), s32[]{:S(2)}) async-start(), calls=%async_computation.59 | async-start | bytes 9437184 | tf_op jit(solution)/shard_map/all_gather | solution.py:130
  737.7 304.7 %reduce-scatter.33.cloned.1.call-start = ((), (), s32[]{:S(2)}) async-start(), calls=%async_computation.34 | async-start | bytes 3932160 | tf_op jit(solution)/shard_map/reduce_scatter | solution.py:58
  982.0 129.1 %all-gather.37.cloned.1.call-start = ((), (), s32[]{:S(2)}) async-start(), calls=%async_computation.35 | async-start | bytes 3932160 | tf_op jit(solution)/shard_map/all_gather | solution.py:44
  1047.5 136.2 %reduce-scatter.61.cloned.1.call-start = ((), (), s32[]{:S(2)}) async-start(), calls=%async_computation.60 | async-start | bytes 491520
  1164.3 83.6 %reduce-scatter.35.cloned.1.call-start = ((), (), s32[]{:S(2)}) async-start(), calls=%async_computation.36 | async-start | bytes 3932160 | tf_op jit(solution)/shard_map/reduce_scatter | solution.py:58
  1189.2 63.6 %copy-start.16 = (f32[192,2048]{1,0:T(8,128)S(1)}, f32[192,2048]{1,0:T(8,128)}, u32[]{:S(2)}) copy-start(f32[192,2048]{1,0:T(8,128)} %copy-done.15) | copy-start | bytes 4718596
  1189.3 130.1 %all-gather.39.cloned.1.call-start = ((), (), s32[]{:S(2)}) async-start(), calls=%async_computation.37 | async-start | bytes 3932160 | tf_op jit(solution)/shard_map/all_gather | solution.py:44
  1252.9 66.5 %copy-start.102 = (f32[1,2048]{1,0:T(1,128)S(1)}, f32[1,2048]{1,0:T(1,128)}, u32[]{:S(2)}) copy-start(f32[1,2048]{1,0:T(1,128)} %copy-done.101) | copy-start | bytes 24580
  1255.7 149.4 %reduce-scatter.37.cloned.1.call-start = ((), (), s32[]{:S(2)}) async-start(), calls=%async_computation.38 | async-start | bytes 3932160 | tf_op jit(solution)/shard_map/reduce_scatter | solution.py:58
  1346.0 128.7 %all-gather.41.cloned.1.call-start = ((), (), s32[]{:S(2)}) async-start(), calls=%async_computation.39 | async-start | bytes 3932160 | tf_op jit(solution)/shard_map/all_gather | solution.py:44
  1411.1 131.8 %reduce-scatter.63.cloned.1.call-start = ((), (), s32[]{:S(2)}) async-start(), calls=%async_computation.61 | async-start | bytes 491520
  1523.5 97.0 %reduce-scatter.31.cloned.1.call-start = ((), (), s32[]{:S(2)}) async-start(), calls=%async_computation.32 | async-start | bytes 3932160 | tf_op jit(solution)/shard_map/reduce_scatter | solution.py:48
  1536.7 191.2 %all-reduce.7.cloned.1.call-start = ((), (), s32[]{:S(2)}) async-start(), calls=%async_computation.49 | async-start | bytes 131072 | tf_op jit(solution)/shard_map/psum | solution.py:310
  1538.1 227.1 %reduce-scatter.47.cloned.1.call-start = ((), (), s32[]{:S(2)}) async-start(), calls=%async_computation.44 | async-start | bytes 294912 | tf_op jit(solution)/shard_map/reduce_scatter | solution.py:279
  1541.4 260.8 %reduce-scatter.45.cloned.1.call-start = ((), (), s32[]{:S(2)}) async-start(), calls=%async_computation.43 | async-start | bytes 294912 | tf_op jit(solution)/shard_map/reduce_scatter | solution.py:279
  1545.2 331.8 %reduce-scatter.59.cloned.1.call-start = ((), (), s32[]{:S(2)}) async-start(), calls=%async_computation.51 | async-start | bytes 9437184 | tf_op jit(solution)/shard_map/reduce_scatter | solution.py:288
  1558.0 393.9 %reduce-scatter.57.cloned.1.call-start = ((), (), s32[]{:S(2)}) async-start(), calls=%async_computation.50 | async-start | bytes 9437184 | tf_op jit(solution)/shard_map/reduce_scatter | solution.py:288
  1571.3 443.8 %reduce-scatter.39.cloned.1.call-start = ((), (), s32[]{:S(2)}) async-start(), calls=%async_computation.40 | async-start | bytes 3932160 | tf_op jit(solution)/shard_map/reduce_scatter | solution.py:58
  1578.7 511.2 %reduce-scatter.55.cloned.1.call-start = ((), (), s32[]{:S(2)}) async-start(), calls=%async_computation.48 | async-start | bytes 9437184 | tf_op jit(solution)/shard_map/reduce_scatter | solution.py:285
  1591.5 573.4 %reduce-scatter.53.cloned.1.call-start = ((), (), s32[]{:S(2)}) async-start(), calls=%async_computation.47 | async-start | bytes 9437184 | tf_op jit(solution)/shard_map/reduce_scatter | solution.py:285
  1604.2 605.2 %reduce-scatter.51.cloned.1.call-start = ((), (), s32[]{:S(2)}) async-start(), calls=%async_computation.46 | async-start | bytes 2359296 | tf_op jit(solution)/shard_map/reduce_scatter | solution.py:282
  1610.4 643.9 %reduce-scatter.49.cloned.1.call-start = ((), (), s32[]{:S(2)}) async-start(), calls=%async_computation.45 | async-start | bytes 2359296 | tf_op jit(solution)/shard_map/reduce_scatter | solution.py:282
  1616.0 682.8 %reduce-scatter.43.cloned.1.call-start = ((), (), s32[]{:S(2)}) async-start(), calls=%async_computation.42 | async-start | bytes 2359296 | tf_op jit(solution)/shard_map/reduce_scatter | solution.py:276
  1624.3 106.3 %copy-start.11 = (bf16[768,2048]{1,0:T(8,128)(2,1)S(1)}, bf16[768,2048]{1,0:T(8,128)(2,1)}, u32[]{:S(2)}) copy-start(bf16[768,2048]{1,0:T(8,128)(2,1)} %all-gather.27.cloned.1.call-done) | copy-start | bytes 9437188
  1624.3 17.1 all-to-all-start.2
  1628.8 714.8 %reduce-scatter.41.cloned.1.call-start = ((), (), s32[]{:S(2)}) async-start(), calls=%async_computation.41 | async-start | bytes 2359296 | tf_op jit(solution)/shard_map/reduce_scatter | solution.py:276
  1952.0 63.2 %copy-start.5 = (f32[192,2048]{1,0:T(8,128)S(1)}, f32[192,2048]{1,0:T(8,128)}, u32[]{:S(2)}) copy-start(f32[192,2048]{1,0:T(8,128)} %copy-done.4) | copy-start | bytes 4718596
  1952.0 63.2 %copy-start.55 = (f32[1,2048]{1,0:T(1,128)S(1)}, f32[1,2048]{1,0:T(1,128)}, u32[]{:S(2)}) copy-start(f32[1,2048]{1,0:T(1,128)} %copy-done.54) | copy-start | bytes 24580
  1952.0 63.2 %copy-start.62 = (f32[192]{0:T(256)S(1)}, f32[192]{0:T(256)}, u32[]{:S(2)}) copy-start(f32[192]{0:T(256)} %copy-done.61) | copy-start | bytes 2308
  2020.8 457.8 %all-to-all-start.4 = ((bf16[8,24,2048]{2,1,0:T(8,128)(2,1)}), bf16[8,24,2048]{2,1,0:T(8,128)(2,1)S(1)}, u32[]{:S(2)}, u32[]{:S(2)}) async-start(bf16[8,24,2048]{2,1,0:T(8,128)(2,1)} %bitcast.336), calls=%async_computation.12 | async-start | bytes 1572864 | tf_op jit(solution)/shard_map/all_to_all | solution.py:333
  2024.5 451.7 %all-reduce.9.cloned.1.call-start = ((), (), s32[]{:S(2)}) async-start(), calls=%async_computation.62 | async-start | bytes 233472 | tf_op jit(solution)/shard_map/psum | solution.py:310
  2164.9 91.6 %copy-start.69 = (f32[2048]{0:T(1024)S(1)}, f32[2048]{0:T(1024)}, u32[]{:S(2)}) copy-start(f32[2048]{0:T(1024)} %get-tuple-element.464) | copy-start | bytes 24580
  2164.9 91.6 %copy-start.70 = (f32[2048]{0:T(1024)S(1)}, f32[2048]{0:T(1024)}, u32[]{:S(2)}) copy-start(f32[2048]{0:T(1024)} %get-tuple-element.454) | copy-start | bytes 24580
  2254.4 233.5 %copy-start.1 = (bf16[192,2048]{1,0:T(8,128)(2,1)S(1)}, bf16[192,2048]{1,0:T(8,128)(2,1)}, u32[]{:S(2)}) copy-start(bf16[192,2048]{1,0:T(8,128)(2,1)} %param.26) | copy-start | bytes 2359300
  (114 other events, 1216.0 us)
Sparse Core Ops, SparseCore 0:
  38.4 62.8 all-gather.26
  103.8 26.5 all-gather.42
  132.8 28.1 all-gather.44
  175.9 60.1 reduce-scatter.24
  238.4 54.4 all-gather.46
  294.9 63.4 all-gather.28
  360.9 54.5 all-gather.48
  428.7 60.2 reduce-scatter.26
  490.9 27.9 all-gather.50
  520.9 63.4 all-gather.30
  586.3 26.8 all-gather.52
  650.5 58.4 reduce-scatter.28
  710.9 59.2 all-gather.54
  772.2 63.4 all-gather.32
  837.7 62.1 all-gather.34
  902.2 54.5 all-gather.56
  982.1 60.2 reduce-scatter.32
  1047.6 63.5 all-gather.36
  1164.4 19.2 reduce-scatter.60
  1189.4 58.5 reduce-scatter.34
  1255.8 63.5 all-gather.38
  1346.2 58.8 reduce-scatter.36
  1411.2 63.5 all-gather.40
  1523.6 19.2 reduce-scatter.62
  1545.7 58.5 reduce-scatter.30
  1610.3 117.5 all-reduce.6
  1730.8 34.3 reduce-scatter.46
  1768.5 33.5 reduce-scatter.44
  1805.6 71.2 reduce-scatter.58
  1880.6 71.2 reduce-scatter.56
  1954.8 60.2 reduce-scatter.38
  2018.6 71.2 reduce-scatter.54
  2093.6 71.2 reduce-scatter.52
  2168.2 41.2 reduce-scatter.50
  2213.1 41.2 reduce-scatter.48
  2257.5 41.2 reduce-scatter.42
  2302.2 41.2 reduce-scatter.40
  2351.1 124.9 all-reduce.8
where the time goes:
time: 2510 us; the launch traced here: 2490 us
  waiting for transfers between devices  1890 us (75%)
  matrix products  350 us (14%)
  other arithmetic  79.2 us (3%)
  blocking collectives  72.6 us (3%)
  local copies, waits for them, and re-layouts  65.7 us (3%)
    all_gather x4, waiting for transfers between devices, rows_gather(): return lax.all_gather(values, 'tensor', axis=0, tiled=True)  247 us
    all_gather x4, waiting for transfers between devices, grad_gather(): return lax.all_gather(values, 'tensor', axis=0, tiled=True)  242 us
    reduce_scatter x4, waiting for transfers between devices, grad_scatter(): lax.psum_scatter(running.astype(jnp.bfloat16), 'tensor', scatter_dimensio...  237 us
    psum x2, waiting for transfers between devices, local(): lax.psum((smalls[0], smalls[1], smalls[2], smalls[3], smalls[4], smalls[5...  211 us
    reduce_scatter x4, waiting for transfers between devices, rows_scatter(): lax.psum_scatter(matmul(left, right).astype(jnp.bfloat16), 'tensor', scat...  174 us
    reduce_scatter x2, waiting for transfers between devices, local(): lax.psum_scatter(down_grad.astype(jnp.bfloat16), 'dp', scatter_dimension=...  148 us
    reduce_scatter x2, waiting for transfers between devices, local(): lax.psum_scatter(up_grad.astype(jnp.bfloat16), 'dp', scatter_dimension=0,...  140 us
    dot_general x34, matrix products, contract_cols(): lax.dot_general(left, right, (((1,), (1,)), ((), ())), preferred_element_...  118 us
  transfers between devices with their start and end apart: 42, of which 38 were waited for; matrix products, arithmetic and copies ran while one was open for 11% of the time, Pallas kernels for 0%

commit v1 on v0

v1 whole, which is shorter than its diff:
```python
import jax
import jax.numpy as jnp
from jax import lax
from jax.experimental import pallas as pl
from jax.experimental.pallas import tpu as pltpu
from jax.sharding import PartitionSpec as P

HEAD = 128
EPSILON = 1e-05
BF16 = jnp.bfloat16
F32 = jnp.float32


def layer_norm(values, scales, offsets):
    row_mean = jnp.mean(values, axis=-1, keepdims=True)
    centred = values - row_mean
    row_var = jnp.mean(centred * centred, axis=-1, keepdims=True)
    return centred * lax.rsqrt(row_var + EPSILON) * scales + offsets


def gelu_tanh(values):
    return jax.nn.gelu(values, approximate=True)


def matmul(left, right):
    return jnp.dot(left, right, preferred_element_type=F32)


def contract_rows(left, right):
    return lax.dot_general(left, right, (((0,), (0,)), ((), ())), preferred_element_type=F32)


def contract_cols(left, right):
    return lax.dot_general(left, right, (((1,), (1,)), ((), ())), preferred_element_type=F32)


def after(values, *others):
    return lax.optimization_barrier((values, others))[0]


def flip(values, bit):
    count = lax.axis_size("dp")
    return lax.ppermute(values, "dp", [(i, i ^ bit) for i in range(count)])


def turn(values, step):
    count = lax.axis_size("tensor")
    return lax.ppermute(values, "tensor", [((i + step) % count, i) for i in range(count)])


def plane_bits():
    count = lax.axis_size("dp")
    return [1 << k for k in range(1, count.bit_length() - 1)]


def slot_order():
    count = lax.axis_size("dp")
    evens = list(range(0, count, 2))
    return evens + [r ^ 1 for r in evens]


def join_rows(arrays):
    return arrays[0] if len(arrays) == 1 else jnp.concatenate(arrays, axis=0)


def blocks_of(parts, wanted):
    runs = []
    where = {}
    for array, blocks in parts:
        rows = array.shape[0] // len(blocks)
        for i, block in enumerate(blocks):
            where[block] = (array, i * rows, rows)
    for block in wanted:
        array, start, rows = where[block]
        if runs and runs[-1][0] is array and runs[-1][2] == start:
            runs[-1][2] += rows
        else:
            runs.append([array, start, start + rows])
    return join_rows([lax.slice_in_dim(array, low, high) for array, low, high in runs])


class Gather:
    def __init__(self, first, second):
        bits = plane_bits()
        self.members = [
            [order, [(array, [0])]]
            for group, order in ((first, bits), (second, bits[::-1]))
            for array in group
        ]
        self.taken = 0

    def send(self, *gate):
        for member in self.members:
            order, parts = member
            bit = order[self.taken]
            blocks = [block for _, part in parts for block in part]
            whole = join_rows([array for array, _ in parts])
            come = flip(after(whole, *gate) if gate else whole, bit)
            member[1] = [(whole, blocks), (come, [block | bit for block in blocks])]
        self.taken += 1
        return self

    def settle(self, *late):
        for member in self.members:
            own, (come, blocks) = member[1]
            member[1] = [own, (after(come, *late), blocks)]
        return self

    def finish(self, *gate):
        while self.taken < len(plane_bits()):
            self.send(*gate)
        return [
            parts + [(flip(array, 1), [block | 1 for block in blocks]) for array, blocks in parts]
            for _, parts in self.members
        ]


class Scatter:
    def __init__(self, first, second):
        bits = plane_bits()
        evens = list(range(0, lax.axis_size("dp"), 2))
        self.members = [
            [order, half, evens]
            for group, order in ((first, bits), (second, bits[::-1]))
            for half in group
        ]
        self.taken = 0
        self.come = None

    def send(self, *gate):
        self.come = []
        for order, half, blocks in self.members:
            sent = [block for block in blocks if block & order[self.taken]]
            piece = blocks_of([(half, blocks)], sent)
            piece = after(piece, *gate) if gate else piece
            self.come.append(flip(piece, order[self.taken]))
        self.taken += 1
        return self

    def settle(self, *late):
        last = self.taken == len(plane_bits())
        for member, come in zip(self.members, self.come):
            order, half, blocks = member
            keep = [block for block in blocks if not block & order[self.taken - 1]]
            if late:
                come = after(come, *late)
            total = blocks_of([(half, blocks)], keep).astype(F32) + come.astype(F32)
            member[1:] = [total if last else total.astype(BF16), keep]
        self.come = None
        return self

    def now(self):
        return [half for _, half, _ in self.members]

    def finish(self, *late):
        if self.come:
            self.settle(*late)
        while self.taken < len(plane_bits()):
            self.send()
            self.settle(*late)
        return [half.astype(F32) for _, half, _ in self.members]


def gradient_half(features, values):
    half = features.shape[1] // 2
    far = contract_rows(features[:, half:], values).astype(BF16)
    near = contract_rows(features[:, :half], values) + flip(far, 1).astype(F32)
    return near.astype(BF16)


def plain_product(total):
    return (total,)


def round_product(total):
    return (total.astype(BF16),)


def gelu_both(total, bias):
    value = total + bias
    return value, gelu_tanh(value).astype(BF16)


def gelu_slope(values):
    factor = 0.7978845608028654
    square = values * values
    wave = jnp.tanh(factor * (values + 0.044715 * (square * values)))
    return 0.5 * (1.0 + wave) + (0.5 * factor) * values * (1.0 - wave * wave) * (
        1.0 + (3.0 * 0.044715) * square
    )


def gelu_and_back(total, bias, act_grad):
    value = total + bias
    return gelu_tanh(value).astype(BF16), (act_grad * gelu_slope(value)).astype(BF16)


def gelu_back(total, value):
    return ((total * gelu_slope(value)).astype(BF16),)


def times(left, parts, finish, extras, types):
    rows, depth = left.shape
    columns = parts[0][0].shape[1]
    height = depth // lax.axis_size("dp")
    place = {block: i for i, block in enumerate(slot_order())}
    if height % 128:
        return finish(matmul(left, blocks_of(parts, slot_order())), *extras)
    tile = next(size for size in (768, 640, 512, 384, 256, 128, columns) if columns % size == 0)
    spots = [[place[block] * height for block in blocks] for _, blocks in parts]

    def kernel(left_ref, *refs):
        part_refs = refs[: len(parts)]
        extra_refs = refs[len(parts) : len(parts) + len(extras)]
        total = None
        for ref, starts in zip(part_refs, spots):
            for i, start in enumerate(starts):
                piece = matmul(
                    left_ref[:, start : start + height], ref[i * height : (i + 1) * height, :]
                )
                total = piece if total is None else total + piece
        values = finish(total, *[ref[...] for ref in extra_refs])
        for ref, value in zip(refs[len(parts) + len(extras) :], values):
            ref[...] = value

    return pl.pallas_call(
        kernel,
        grid=(columns // tile,),
        in_specs=[pl.BlockSpec((rows, depth), lambda j: (0, 0))]
        + [pl.BlockSpec((array.shape[0], tile), lambda j: (0, j)) for array, _ in parts]
        + [pl.BlockSpec((extra.shape[0], tile), lambda j: (0, j)) for extra in extras],
        out_specs=[pl.BlockSpec((rows, tile), lambda j: (0, j)) for _ in types],
        out_shape=[jax.ShapeDtypeStruct((rows, columns), kind) for kind in types],
        cost_estimate=pl.CostEstimate(
            flops=2 * rows * depth * columns,
            transcendentals=rows * columns if extras else 0,
            bytes_accessed=2 * depth * (rows + columns) + 6 * rows * columns,
        ),
        name="times",
    )(left, *[array for array, _ in parts], *extras)


def times_turned(left, parts, kind):
    rows, depth = left.shape
    count = lax.axis_size("dp")
    height = sum(array.shape[0] for array, _ in parts) // count
    place = {block: i for i, block in enumerate(slot_order())}
    if height % 128:
        return contract_cols(left, blocks_of(parts, slot_order())).astype(kind)
    tile = 256 if rows % 256 == 0 else rows
    spots = [[place[block] * height for block in blocks] for _, blocks in parts]

    def kernel(left_ref, *refs):
        for ref, starts in zip(refs, spots):
            for i, start in enumerate(starts):
                piece = contract_cols(left_ref[...], ref[i * height : (i + 1) * height, :])
                refs[-1][:, start : start + height] = piece.astype(kind)

    whole = [
        pl.BlockSpec(array.shape, lambda i: (0, 0), pipeline_mode=pl.Buffered(1))
        for array, _ in parts
    ]
    return pl.pallas_call(
        kernel,
        grid=(rows // tile,),
        in_specs=[pl.BlockSpec((tile, depth), lambda i: (i, 0))] + whole,
        out_specs=pl.BlockSpec((tile, count * height), lambda i: (i, 0)),
        out_shape=jax.ShapeDtypeStruct((rows, count * height), kind),
        cost_estimate=pl.CostEstimate(
            flops=2 * rows * depth * count * height,
            transcendentals=0,
            bytes_accessed=2 * depth * (rows + count * height) + 4 * rows * count * height,
        ),
        name="times_turned",
    )(left, *[array for array, _ in parts])


def arrays_of(*weights):
    return [array for parts in weights for array, _ in parts]


def tensor_slots(values):
    return [values] + [turn(values, k) for k in range(1, lax.axis_size("tensor"))]


def tensor_rows(values):
    return lax.all_gather(values, "tensor", axis=0, tiled=True)


def tensor_sum(values):
    return lax.psum_scatter(values, "tensor", scatter_dimension=0, tiled=True)


def sum_columns(whole, count):
    width = whole.shape[1] // count
    whole = whole.astype(BF16)
    pieces = [whole[:, k * width : (k + 1) * width] for k in range(count)]
    return tensor_sum(jnp.concatenate(pieces, axis=0)).astype(F32)


def sum_query(whole, width, query_cols, pair_cols):
    count = lax.axis_size("tensor")
    rows = whole.shape[0]
    whole = whole.astype(BF16)
    pieces = []
    for k in range(count):
        pieces.append(whole[:, k * query_cols : (k + 1) * query_cols])
        pair = whole[:, width + k * pair_cols : width + (k + 1) * pair_cols]
        pieces.append(pair.reshape(rows * pair_cols // query_cols, query_cols))
    total = tensor_sum(jnp.concatenate(pieces, axis=0)).astype(F32)
    return total[:rows], total[rows:].reshape(rows, pair_cols)


def copy_block(table, source, target):
    target[...] = source[...]


def reorder(values, table):
    rows, columns = values.shape
    count = table.shape[0]
    width = columns // count
    if width % 128:
        return jnp.take(values.reshape(rows, count, width), table, axis=1).reshape(rows, columns)
    return pl.pallas_call(
        copy_block,
        grid_spec=pltpu.PrefetchScalarGridSpec(
            num_scalar_prefetch=1,
            grid=(count,),
            in_specs=[pl.BlockSpec((rows, width), lambda j, table: (0, table[j]))],
            out_specs=pl.BlockSpec((rows, width), lambda j, table: (0, j)),
        ),
        out_shape=jax.ShapeDtypeStruct(values.shape, values.dtype),
        name="reorder",
    )(table, values)


def stack_heads(block):
    return jnp.concatenate([block[:, :HEAD], block[:, HEAD:]], axis=0)


def attend_kernel(scale, query_ref, key_ref, value_t_ref, bias_ref, out_ref, log_ref):
    rows = query_ref.shape[0]
    queries = stack_heads(query_ref[...])
    scores = contract_cols(key_ref[...], queries) * scale + bias_ref[...]
    top = jnp.max(scores, axis=0, keepdims=True)
    exps = jnp.exp(scores - top)
    total = jnp.sum(exps, axis=0, keepdims=True)
    probs = (exps * (1.0 / total)).astype(BF16)
    mixed = matmul(value_t_ref[...], probs).T.astype(BF16)
    out_ref[:, :HEAD] = mixed[:rows]
    out_ref[:, HEAD:] = mixed[rows:]
    log_ref[0] = top + jnp.log(total)


def attend(queries, key_rows, value_t, bias, scale):
    rows, columns = queries.shape
    pairs = columns // (2 * HEAD)
    keys = key_rows.shape[0]

    def kernel(*refs):
        attend_kernel(scale, *refs)

    return pl.pallas_call(
        kernel,
        grid=(pairs,),
        in_specs=[
            pl.BlockSpec((rows, 2 * HEAD), lambda i: (0, i)),
            pl.BlockSpec((keys, HEAD), lambda i: (0, 0)),
            pl.BlockSpec((HEAD, keys), lambda i: (0, 0)),
            pl.BlockSpec((keys, 2 * rows), lambda i: (0, 0)),
        ],
        out_specs=[
            pl.BlockSpec((rows, 2 * HEAD), lambda i: (0, i)),
            pl.BlockSpec((1, 1, 2 * rows), lambda i: (i, 0, 0)),
        ],
        out_shape=[
            jax.ShapeDtypeStruct((rows, columns), BF16),
            jax.ShapeDtypeStruct((pairs, 1, 2 * rows), F32),
        ],
        cost_estimate=pl.CostEstimate(
            flops=4 * rows * keys * columns,
            transcendentals=rows * keys * columns // HEAD,
            bytes_accessed=4 * rows * columns + 8 * keys * rows,
        ),
        name="attend",
    )(queries, key_rows, value_t, bias)


def attend_back_kernel(
    scale, query_ref, dout_ref, key_ref, value_ref, key_t_ref, bias_ref, log_ref, grad_ref, pair_ref
):
    rows = query_ref.shape[0]

    @pl.when(pl.program_id(0) == 0)
    def _():
        pair_ref[...] = jnp.zeros_like(pair_ref)

    queries = stack_heads(query_ref[...])
    douts = stack_heads(dout_ref[...])
    scores = contract_cols(key_ref[...], queries) * scale + bias_ref[...]
    probs = jnp.exp(scores - log_ref[0])
    prob_grad = contract_cols(value_ref[...], douts)
    inner = jnp.sum(probs * prob_grad, axis=0, keepdims=True)
    score_grad = (probs * (prob_grad - inner) * scale).astype(BF16)
    pair_ref[:, :HEAD] += matmul(score_grad, queries)
    pair_ref[:, HEAD:] += matmul(probs.astype(BF16), douts)
    query_grad = matmul(key_t_ref[...], score_grad).T.astype(BF16)
    grad_ref[:, :HEAD] = query_grad[:rows]
    grad_ref[:, HEAD:] = query_grad[rows:]


def attend_back(queries, douts, key_rows, value_rows, key_t, bias, log_totals, scale):
    rows, columns = queries.shape
    pairs = columns // (2 * HEAD)
    keys = key_rows.shape[0]

    def kernel(*refs):
        attend_back_kernel(scale, *refs)

    return pl.pallas_call(
        kernel,
        grid=(pairs,),
        in_specs=[
            pl.BlockSpec((rows, 2 * HEAD), lambda i: (0, i)),
            pl.BlockSpec((rows, 2 * HEAD), lambda i: (0, i)),
            pl.BlockSpec((keys, HEAD), lambda i: (0, 0)),
            pl.BlockSpec((keys, HEAD), lambda i: (0, 0)),
            pl.BlockSpec((HEAD, keys), lambda i: (0, 0)),
            pl.BlockSpec((keys, 2 * rows), lambda i: (0, 0)),
            pl.BlockSpec((1, 1, 2 * rows), lambda i: (i, 0, 0)),
        ],
        out_specs=[
            pl.BlockSpec((rows, 2 * HEAD), lambda i: (0, i)),
            pl.BlockSpec((keys, 2 * HEAD), lambda i: (0, 0)),
        ],
        out_shape=[
            jax.ShapeDtypeStruct((rows, columns), BF16),
            jax.ShapeDtypeStruct((keys, 2 * HEAD), F32),
        ],
        cost_estimate=pl.CostEstimate(
            flops=10 * rows * keys * columns,
            transcendentals=rows * keys * columns // HEAD,
            bytes_accessed=6 * rows * columns + 12 * keys * rows,
        ),
        name="attend_back",
    )(queries, douts, key_rows, value_rows, key_t, bias, log_totals)


def local(
    tokens,
    cotangent,
    deal,
    segment,
    norm1_gain,
    norm1_shift,
    query_weight,
    query_bias,
    kv_weight,
    value_bias,
    out_weight,
    out_bias,
    norm2_gain,
    norm2_shift,
    up_weight,
    up_bias,
    down_weight,
    down_bias,
):
    local_rows, width = tokens.shape
    dp_count = lax.axis_size("dp")
    tensor_count = lax.axis_size("tensor")
    dp_rank = lax.axis_index("dp")
    tensor_rank = lax.axis_index("tensor")
    slot_rows = local_rows // dp_count
    layer_total = query_weight.shape[0]
    group_rows = local_rows * tensor_count
    query_cols = query_weight.shape[2]
    pair_cols = kv_weight.shape[2]
    score_scale = HEAD ** (-0.5)
    order = slot_order()
    to_slots = jnp.asarray(order, jnp.int32) ^ dp_rank
    place_of = [order.index(r) for r in range(dp_count)]
    from_slots = jnp.take(
        jnp.asarray(place_of, jnp.int32), jnp.arange(dp_count, dtype=jnp.int32) ^ dp_rank
    )

    last = layer_total - 1
    split = width // 2
    cut = tensor_count // 2
    bias_slots = jnp.roll(
        jnp.concatenate(tensor_slots(query_bias), axis=1), tensor_rank * query_cols, axis=1
    )
    kv_full = jnp.roll(
        jnp.concatenate(tensor_slots(kv_weight), axis=2), tensor_rank * pair_cols, axis=2
    )
    depth = query_weight.shape[1]

    def columns(rows, *more):
        count = rows.shape[0] // depth
        pieces = [rows[k * depth : (k + 1) * depth] for k in range(count)]
        return jnp.concatenate(pieces + list(more), axis=1)

    out_turned = [out_weight[l].T for l in range(layer_total)]
    down_turned = [down_weight[l].T for l in range(layer_total)]
    query_rows = tensor_rows(query_weight[0])
    out_rows = tensor_rows(after(out_turned[0], query_rows))
    cut_rows = cut * depth
    ff_gather = Gather([up_weight[0]], [down_turned[0]]).send()
    query_gather = Gather(
        [columns(query_rows[:cut_rows])], [columns(query_rows[cut_rows:], kv_full[0])]
    )
    w_query = query_gather.finish()
    out_gather = Gather([columns(out_rows[:cut_rows])], [columns(out_rows[cut_rows:])])
    w_out = out_gather.finish()
    ff_gather.settle()

    target_dev = deal // local_rows // tensor_count
    target_row = deal % local_rows
    dev_ids = jnp.arange(dp_count, dtype=jnp.int32)
    dev_match = (target_dev[:, None] == dev_ids[None, :]).astype(jnp.int32)
    earlier = jnp.cumsum(dev_match, axis=0) - dev_match
    slot_of = target_dev * slot_rows + jnp.sum(earlier * dev_match, axis=1)
    row_ids = jnp.arange(local_rows, dtype=jnp.int32)
    send_table = (row_ids[:, None] == slot_of[None, :]).astype(BF16)
    place_cols = jnp.broadcast_to(target_row.astype(BF16)[:, None], (local_rows, HEAD))
    tokens_sent = matmul(send_table, jnp.concatenate([tokens, place_cols], axis=1)).astype(BF16)
    tokens_come = lax.all_to_all(tokens_sent, "dp", split_axis=0, concat_axis=0, tiled=True)
    tangent_sent = matmul(send_table, cotangent).astype(BF16)
    tangent_come = lax.all_to_all(tangent_sent, "dp", split_axis=0, concat_axis=0, tiled=True)
    arrived_place = tokens_come[:, width].astype(jnp.int32)
    place_table = (row_ids[:, None] == arrived_place[None, :]).astype(BF16)
    stream = reorder(matmul(place_table, tokens_come[:, :width]).astype(BF16), to_slots).astype(F32)
    last_branch = reorder(matmul(place_table, tangent_come).astype(BF16), to_slots)
    tangent = last_branch.astype(F32)
    stream = after(stream, last_branch)

    vectors = jnp.concatenate(
        [norm1_gain, norm1_shift, out_bias, norm2_gain, norm2_shift, down_bias], axis=0
    )
    vectors = reorder(vectors, to_slots)
    gain_one, shift_one, bias_out, gain_two, shift_two, bias_down = [
        vectors[i * layer_total : (i + 1) * layer_total] for i in range(6)
    ]

    places = jnp.arange(group_rows, dtype=jnp.int32)
    key_places = (places + tensor_rank * local_rows) % group_rows
    key_labels = jnp.roll(segment, -tensor_rank * local_rows)
    allowed = (key_places[:, None] <= key_places[None, :local_rows]) & (
        key_labels[:, None] == key_labels[None, :local_rows]
    )
    score_bias = jnp.where(allowed, 0.0, -1e30).astype(F32)
    score_bias = jnp.concatenate([score_bias, score_bias], axis=1)

    def product(left, weights):
        pieces = [times(left, parts, plain_product, (), (F32,))[0] for parts in weights]
        return pieces[0] if len(pieces) == 1 else jnp.concatenate(pieces, axis=1)

    def product_turned(left, weights):
        total, start = None, 0
        for parts in weights:
            size = parts[0][0].shape[1]
            piece = times_turned(left[:, start : start + size], parts, F32)
            total = piece if total is None else total + piece
            start += size
        return total

    saved = []
    for l in range(layer_total):
        if l < last:
            query_rows = tensor_rows(after(query_weight[l + 1], out_rows))
            out_rows = tensor_rows(after(out_turned[l + 1], query_rows))
        normed = layer_norm(stream, gain_one[l], shift_one[l]).astype(BF16)
        projected = product(normed, w_query)
        pair_bias = jnp.concatenate([jnp.zeros((HEAD,), F32), value_bias[l]])
        pair_own = (projected[:, width:] + pair_bias).astype(BF16)
        queries = (projected[:, :width] + bias_slots[l]).astype(BF16)
        pair_all = jnp.concatenate(tensor_slots(pair_own))
        pair_t = pair_all.T
        mixed, log_totals = attend(
            queries, pair_all[:, :HEAD], pair_t[HEAD:], score_bias, score_scale
        )
        w_up, w_down = ff_gather.settle(mixed).finish(mixed)
        hidden_state = stream + product_turned(mixed, w_out) + bias_out[l]
        normed_two = layer_norm(hidden_state, gain_two[l], shift_two[l]).astype(BF16)
        normed_two_all = tensor_rows(normed_two)
        normed_two_all = after(normed_two_all, *arrays_of(w_up, w_down))
        if l == last:
            if last == 0:
                branch_all = tensor_rows(last_branch)
            act_grad = times(branch_all, w_down, plain_product, (), (F32,))[0]
            normed_two_all = after(normed_two_all, act_grad)
            activation, pre_grad = times(
                normed_two_all, w_up, gelu_and_back, (up_bias[l][None], act_grad), (BF16, BF16)
            )
            pre_gelu = None
        else:
            pre_gelu, activation = times(
                normed_two_all, w_up, gelu_both, (up_bias[l][None],), (F32, BF16)
            )
        saved.append(
            (
                stream,
                normed,
                queries,
                pair_all,
                pair_t,
                log_totals,
                mixed,
                hidden_state,
                normed_two_all,
                pre_gelu,
                activation,
                w_query,
                w_out,
                w_up,
                w_down,
            )
        )
        if l < last:
            attn_gather = Gather([columns(query_rows, kv_full[l + 1])], [columns(out_rows)])
            attn_gather.send(normed_two_all)
            down_part = times_turned(activation, w_down, BF16)
            down_sum = tensor_sum(down_part)
            w_query, w_out = [[parts] for parts in attn_gather.settle(down_part).finish(down_part)]
            down_sum = after(down_sum, *arrays_of(*w_query, *w_out))
            if l == last - 1:
                branch_all = tensor_rows(after(last_branch, down_sum))
            stream = hidden_state + down_sum.astype(F32) + bias_down[l]
            ff_gather = Gather([up_weight[l + 1]], [down_turned[l + 1]]).send(down_sum)

    reduced = [None] * layer_total
    vector_grads = [None] * layer_total
    query_bias_grads = [None] * layer_total
    value_bias_grads = [None] * layer_total
    up_bias_grads = [None] * layer_total
    later = None
    for l in reversed(range(layer_total)):
        (
            stream_in,
            normed,
            queries,
            pair_all,
            pair_t,
            log_totals,
            mixed,
            hidden_state,
            normed_two_all,
            pre_gelu,
            activation,
            w_query,
            w_out,
            w_up,
            w_down,
        ) = saved[l]
        branch_grad = tangent.astype(BF16)
        if l < last:
            branch_all = tensor_rows(branch_grad)
            above, both_above, normed_above, attn_above, mixed_above, ff_scatter = later
            ff_scatter.settle(branch_grad).send()
            both_late, attn_late = after((both_above, attn_above), branch_grad)
            attn_scatter = Scatter(
                [gradient_half(normed_above, both_late)], [gradient_half(attn_late, mixed_above)]
            )
            attn_scatter.send()
            branch_all = after(branch_all, *ff_scatter.now(), *attn_scatter.now())
            pre_grad = times(branch_all, w_down, gelu_back, (pre_gelu,), (BF16,))[0]
        normed_part = times_turned(pre_grad, w_up, BF16)
        normed_two_grad = tensor_sum(normed_part)
        if l < last:
            up_grad, down_grad = ff_scatter.finish(normed_part)
            reduced[above] = (up_grad, down_grad.T)
            attn_scatter.settle(normed_part).send()
        pre_late, branch_late = after((pre_grad, branch_all), normed_part)
        down_bias_part = jnp.sum(after(branch_grad, normed_part).astype(F32), axis=0)
        up_bias_grads[l] = jnp.sum(pre_late.astype(F32), axis=0)
        ff_scatter = Scatter(
            [gradient_half(normed_two_all, pre_late)], [gradient_half(branch_late, activation)]
        )
        ff_scatter.send()
        beside = ff_scatter.now()
        if l == last:
            final_part = times_turned(after(activation, *beside), w_down, BF16)
            beside = beside + [final_part]
        else:
            beside = beside + attn_scatter.now()
        normed_two_grad = after(normed_two_grad, *beside)
        if l == last:
            final_sum = tensor_sum(after(final_part, normed_two_grad))
        hidden_part, gain_two_part, shift_two_part = jax.vjp(
            layer_norm, hidden_state, gain_two[l], shift_two[l]
        )[1](normed_two_grad.astype(F32))
        hidden_grad = tangent + hidden_part
        attn_grad = hidden_grad.astype(BF16)
        out_bias_part = jnp.sum(attn_grad.astype(F32), axis=0)
        mixed_grad = product(attn_grad, w_out).astype(BF16)
        if l == 0:
            ff_scatter.settle(attn_grad).send()
            attn_late = after(attn_grad, mixed_grad)
            out_scatter = Scatter(
                [gradient_half(attn_late, mixed[:, :split])],
                [gradient_half(attn_late, mixed[:, split:])],
            ).send()
            mixed_grad = after(mixed_grad, *ff_scatter.now(), *out_scatter.now())
        query_grad, pair_part = attend_back(
            queries,
            mixed_grad,
            pair_all[:, :HEAD],
            pair_all[:, HEAD:],
            pair_t[:HEAD],
            score_bias,
            log_totals,
            score_scale,
        )
        pair_grad = pair_part[:local_rows]
        for k in range(1, tensor_count):
            piece = pair_part[k * local_rows : (k + 1) * local_rows].astype(BF16)
            pair_grad = pair_grad + turn(piece, tensor_count - k).astype(F32)
        pair_grad = pair_grad.astype(BF16)
        query_bias_grads[l] = jnp.sum(query_grad.astype(F32), axis=0)
        value_bias_grads[l] = jnp.sum(pair_grad[:, HEAD:].astype(F32), axis=0)
        both_grad = jnp.concatenate([query_grad, pair_grad], axis=1)
        if l == 0 and last > 0:
            both_whole, out_whole = attn_scatter.finish(query_grad)
            out_grad = sum_columns(out_whole, tensor_count).T
            query_w_grad, kv_grad = sum_query(both_whole, width, query_cols, pair_cols)
            reduced[above] = (query_w_grad, kv_grad, out_grad) + reduced[above]
        normed_grad = product_turned(both_grad, w_query)
        stream_part, gain_one_part, shift_one_part = jax.vjp(
            layer_norm, stream_in, gain_one[l], shift_one[l]
        )[1](normed_grad)
        tangent = hidden_grad + stream_part
        later = (l, both_grad, normed, attn_grad, mixed, ff_scatter)
        vector_grads[l] = [
            gain_one_part,
            shift_one_part,
            out_bias_part,
            gain_two_part,
            shift_two_part,
            down_bias_part,
        ]
    out_scatter.settle(both_grad).send()
    both_scatter = Scatter(
        [gradient_half(normed, both_grad[:, :split])], [gradient_half(normed, both_grad[:, split:])]
    ).send()
    up_grad, down_grad = ff_scatter.finish(both_grad)
    out_grad = sum_columns(jnp.concatenate(out_scatter.finish(), axis=1), tensor_count).T
    both_whole = jnp.concatenate(both_scatter.finish(), axis=1)
    query_w_grad, kv_grad = sum_query(both_whole, width, query_cols, pair_cols)
    reduced[0] = (query_w_grad, kv_grad, out_grad, up_grad, down_grad.T)
    final_sum = after(final_sum, normed_two_grad)
    layer_out = (saved[last][7] + final_sum.astype(F32) + bias_down[last]).astype(BF16)

    stacked = jnp.stack([vector_grads[l][m] for m in range(6) for l in range(layer_total)])
    stacked = reorder(stacked, from_slots)
    query_rows = jnp.stack(query_bias_grads)
    value_rows = jnp.pad(jnp.stack(value_bias_grads), ((0, 0), (0, width - HEAD)))
    smalls = jnp.concatenate([stacked, query_rows, value_rows], axis=0)
    small_count = smalls.shape[0]
    smalls = jnp.concatenate([smalls, jnp.stack(up_bias_grads)], axis=0)
    for k in range(dp_count.bit_length() - 1):
        smalls = smalls + flip(smalls, 1 << k)
    up_bias_grad = smalls[small_count:]
    smalls = smalls[:small_count]
    total = smalls
    if tensor_count & (tensor_count - 1) == 0:
        for k in range(tensor_count.bit_length() - 1):
            total = total + lax.ppermute(
                total, "tensor", [(i, i ^ (1 << k)) for i in range(tensor_count)]
            )
    else:
        total = lax.psum(total, "tensor")
    vector_sums = [total[m * layer_total : (m + 1) * layer_total] for m in range(8)]
    query_bias_grad = lax.dynamic_slice_in_dim(
        vector_sums[6], tensor_rank * query_cols, query_cols, 1
    )
    value_bias_grad = vector_sums[7][:, :HEAD]

    out_slots = contract_rows(place_table, reorder(layer_out, from_slots)).astype(BF16)
    grad_slots = contract_rows(place_table, reorder(tangent.astype(BF16), from_slots)).astype(BF16)
    out_back = lax.all_to_all(out_slots, "dp", split_axis=0, concat_axis=0, tiled=True)
    grad_back = lax.all_to_all(grad_slots, "dp", split_axis=0, concat_axis=0, tiled=True)
    layer_rows = contract_rows(send_table, out_back).astype(BF16)
    token_rows = contract_rows(send_table, grad_back).astype(BF16)
    summed = [jnp.stack([reduced[l][m] for l in range(layer_total)]) for m in range(5)]
    return (
        layer_rows,
        token_rows,
        vector_sums[0],
        vector_sums[1],
        summed[0],
        query_bias_grad,
        summed[1],
        value_bias_grad,
        summed[2],
        vector_sums[2],
        vector_sums[3],
        vector_sums[4],
        summed[3],
        up_bias_grad,
        summed[4],
        vector_sums[5],
    )


def solution(mesh):
    rows = P(("dp", "tensor"), None)
    in_specs = (
        rows,
        rows,
        P(("dp", "tensor")),
        P("dp"),
        P(),
        P(),
        P(None, "dp", "tensor"),
        P(None, "tensor"),
        P(None, "dp", "tensor"),
        P(),
        P(None, "tensor", "dp"),
        P(),
        P(),
        P(),
        P(None, "dp", "tensor"),
        P(None, "tensor"),
        P(None, "tensor", "dp"),
        P(),
    )
    out_specs = (
        rows,
        rows,
        P(),
        P(),
        P(None, "dp", "tensor"),
        P(None, "tensor"),
        P(None, "dp", "tensor"),
        P(),
        P(None, "tensor", "dp"),
        P(),
        P(),
        P(),
        P(None, "dp", "tensor"),
        P(None, "tensor"),
        P(None, "tensor", "dp"),
        P(),
    )
    return jax.shard_map(local, mesh=mesh, in_specs=in_specs, out_specs=out_specs, check_vma=False)
```

time: 2510 us -> 1260 us (0.50)
  waiting for transfers between devices: 1890 us -> 532 us
  Pallas kernels: 0 us -> 248 us
  matrix products: 350 us -> 114 us
  starting transfers between devices: 20.6 us -> 105 us
  blocking collectives: 72.6 us -> 0 us
  other arithmetic: 79.2 us -> 127 us
  local copies, waits for them, and re-layouts: 65.7 us -> 105 us
    reduce_scatter x18 -> x8, waiting for transfers between devices: 936 us -> 21.7 us  [tensor_sum(): return lax.psum_scatter(values, 'tensor', scatter_dimension=0, tiled=True)]
    all_gather x16 -> x8, waiting for transfers between devices: 700 us -> 46.4 us  [tensor_rows(): return lax.all_gather(values, 'tensor', axis=0, tiled=True)]
    ppermute x0 -> x93, waiting for transfers between devices: none -> 440 us  [the longest x73 397 us: flip(): return lax.ppermute(values, 'dp', [(i, i ^ bit) for i in range(count)])]
    pallas_call x0 -> x30, Pallas kernels: none -> 248 us  [the longest x10 85.5 us: times(): pl.pallas_call(kernel, grid=(columns // tile,), in_specs=[pl.BlockSpec((r...]
    dot_general x64 -> x4, matrix products: 233 us -> 7.29 us  [matmul(): return jnp.dot(left, right, preferred_element_type=F32)]
    psum x2 -> x0, waiting for transfers between devices: 211 us -> none  [local(): lax.psum((smalls[0], smalls[1], smalls[2], smalls[3], smalls[4], smalls[5...]
    ppermute x0 -> x93, starting transfers between devices: none -> 86.3 us  [the longest x73 53.3 us: flip(): return lax.ppermute(values, 'dp', [(i, i ^ bit) for i in range(count)])]
    all_gather x4 -> x0, blocking collectives: 49.9 us -> none  [the longest x2 30.1 us: local(): pair_all = lax.all_gather(pair_local, 'tensor', axis=1, tiled=True)]
  transfers between devices with their start and end apart: 42 -> 113, of which waited for: 38 -> 44; matrix products, arithmetic and copies ran while one was open for 11% -> 23% of each run, Pallas kernels for 0% -> 10%
where the time goes in v1:
time: 1260 us; the launch traced here: 1250 us
  waiting for transfers between devices  532 us (42%)
  Pallas kernels  248 us (20%)
  other arithmetic  127 us (10%)
  matrix products  114 us (9%)
  local copies, waits for them, and re-layouts  105 us (8%)
  starting transfers between devices  105 us (8%)
  between operations  16.3 us (1%)
    ppermute x73, waiting for transfers between devices, flip(): return lax.ppermute(values, 'dp', [(i, i ^ bit) for i in range(count)])  397 us
    dot_general x24, matrix products, contract_rows(): lax.dot_general(left, right, (((0,), (0,)), ((), ())), preferred_element_...  107 us
    pallas_call x10, Pallas kernels, times(): pl.pallas_call(kernel, grid=(columns // tile,), in_specs=[pl.BlockSpec((r...  85.5 us
    pallas_call x10, Pallas kernels, times_turned(): pl.pallas_call(kernel, grid=(rows // tile,), in_specs=[pl.BlockSpec((tile...  84.5 us
    ppermute x73, starting transfers between devices, flip(): return lax.ppermute(values, 'dp', [(i, i ^ bit) for i in range(count)])  53.3 us
    all_gather x8, waiting for transfers between devices, tensor_rows(): return lax.all_gather(values, 'tensor', axis=0, tiled=True)  46.4 us
    unnamed x315, local copies, waits for them, and re-layouts  43.7 us
    ppermute x18, starting transfers between devices, turn(): lax.ppermute(values, 'tensor', [((i + step) % count, i) for i in range(co...  32.9 us
  transfers between devices with their start and end apart: 113, of which 44 were waited for; matrix products, arithmetic and copies ran while one was open for 23% of the time, Pallas kernels for 10%

profile of v1, /device:TPU:0, one launch (start us, length us, event | category | flops | bytes accessed | tf_op | source)
XLA Modules:
  0.0 1248.4 jit_solution(896607889421499010)
XLA Ops:
  32.4 4.8 reorder.8
  47.6 5.4 collective-permute-done.4
  58.5 12.7 %collective-permute-done.7 = bf16[256,1280]{1,0:T(8,128)(2,1)S(1)} collective-permute-done((bf16[256,1280]{1,0:T(8,128)(2,1)S(1)}, bf16[256,1280]{1,0:T(8,128)(2,1)S(1)}, u32[]{:S(2)}, u32[]{:S(2)}) %collective-permute-start.7) | collective-permute-done | bytes 655392 | tf_op jit(solution)/shard_map/ppermute | solution.py:43
  86.2 23.9 %all-to-all-done.1 = bf16[8,24,2048]{2,1,0:T(8,128)(2,1)S(1)} async-done(((bf16[8,24,2048]{2,1,0:T(8,128)(2,1)}), bf16[8,24,2048]{2,1,0:T(8,128)(2,1)S(1)}, u32[]{:S(2)}, u32[]{:S(2)}) %all-to-all-start.1) | async-done | bytes 786464 | tf_op jit(solution)/shard_map/all_to_all | solution.py:529
  111.3 5.7 reorder.6
  118.3 5.8 reorder.7
  128.6 10.4 collective-permute-done.17
  147.4 4.9 times.11
  165.3 7.3 collective-permute-done.15
  175.8 9.9 attend.2
  188.7 5.0 times_turned.11
  193.7 5.0 times_turned.10
  202.5 10.6 collective-permute-done.29
  222.0 44.5 %collective-permute-done.30.refs_1_ = bf16[512,2048]{1,0:T(8,128)(2,1)} collective-permute-done((bf16[512,2048]{1,0:T(8,128)(2,1)}, bf16[512,2048]{1,0:T(8,128)(2,1)}, u32[]{:S(2)}, u32[]{:S(2)}) %collective-permute-start.30) | collective-permute-done | bytes 2097184 | tf_op jit(solution)/shard_map/ppermute | solution.py:43
  274.9 13.4 %times.12 = (f32[768,2048]{1,0:T(8,128)}, bf16[768,2048]{1,0:T(8,128)(2,1)}) custom-call(bf16[768,2048]{1,0:T(8,128)(2,1)} %all-gather.12.cloned.1.call-done.left_ref, bf16[512,2048]{1,0:T(8,128)(2,1)} %pad_maximum_fusion.4.refs_0_, bf16[512,2048]{1,0:T(8,128)(2,1)} %collective-permute-done.26.refs_1_, bf16[512,2048]{1,0:T(8,128)(2,1)} %collective-permute-done.27.refs_2_, ...), custom_call_target="tpu_custom_call" | custom-call | flops 6442450944 | bytes 20971520 | tf_op jit(solution)/shard_map/times/pallas_call | solution.py:226
  288.3 11.9 times_turned.12
  308.0 22.5 %collective-permute-done.37 = bf16[256,2048]{1,0:T(8,128)(2,1)S(1)} collective-permute-done((bf16[256,2048]{1,0:T(8,128)(2,1)S(1)}, bf16[256,2048]{1,0:T(8,128)(2,1)S(1)}, u32[]{:S(2)}, u32[]{:S(2)}) %collective-permute-start.37) | collective-permute-done | bytes 1048608 | tf_op jit(solution)/shard_map/ppermute | solution.py:43
  332.3 47.5 %collective-permute-done.34.refs_1_ = bf16[512,2304]{1,0:T(8,128)(2,1)S(1)} collective-permute-done((bf16[512,2304]{1,0:T(8,128)(2,1)S(1)}, bf16[512,2304]{1,0:T(8,128)(2,1)S(1)}, u32[]{:S(2)}, u32[]{:S(2)}) %collective-permute-start.34) | collective-permute-done | bytes 2359328 | tf_op jit(solution)/shard_map/ppermute | solution.py:43
  380.4 6.6 collective-permute-done.39.refs_2_
  394.7 7.0 times.13
  402.9 7.5 collective-permute-start.43
  421.6 9.9 attend.3
  431.5 7.7 times_turned.13
  448.1 22.1 %collective-permute-done.48 = bf16[256,2048]{1,0:T(8,128)(2,1)} collective-permute-done((bf16[256,2048]{1,0:T(8,128)(2,1)}, bf16[256,2048]{1,0:T(8,128)(2,1)}, u32[]{:S(2)}, u32[]{:S(2)}) %collective-permute-start.48) | collective-permute-done | bytes 1048608 | tf_op jit(solution)/shard_map/ppermute | solution.py:43
  477.4 43.5 %collective-permute-done.45.refs_1_ = bf16[512,2048]{1,0:T(8,128)(2,1)} collective-permute-done((bf16[512,2048]{1,0:T(8,128)(2,1)S(1)}, bf16[512,2048]{1,0:T(8,128)(2,1)}, u32[]{:S(2)}, u32[]{:S(2)}) %collective-permute-start.45) | collective-permute-done | bytes 2097184 | tf_op jit(solution)/shard_map/ppermute | solution.py:43
  528.5 44.0 %all-gather.20.cloned.1.call-done.left_ref = bf16[768,2048]{1,0:T(8,128)(2,1)} async-done(((bf16[192,2048]{1,0:T(8,128)(2,1)}), bf16[768,2048]{1,0:T(8,128)(2,1)}) %all-gather.20.cloned.1.call-update) | async-done | bytes 3145744 | tf_op jit(solution)/shard_map/all_gather | solution.py:287
  572.4 11.7 times.14.refs_5_
  584.1 15.5 %times.15 = (bf16[768,2048]{1,0:T(8,128)(2,1)}, bf16[768,2048]{1,0:T(8,128)(2,1)}) custom-call(bf16[768,2048]{1,0:T(8,128)(2,1)} %all-gather.18.cloned.1.call-done.left_ref, bf16[512,2048]{1,0:T(8,128)(2,1)} %copy-done.74, bf16[512,2048]{1,0:T(8,128)(2,1)} %collective-permute-done.45.refs_1_, bf16[512,2048]{1,0:T(8,128)(2,1)} %copy-done.134, ...), custom_call_target="tpu_custom_call" | custom-call | flops 6442450944 | bytes 20971520 | tf_op jit(solution)/shard_map/times/pallas_call | solution.py:226
  599.6 11.9 times_turned.14
  611.6 7.9 convolution_convert_fusion.6
  619.7 7.8 convolution_convert_fusion.5
  628.8 9.3 add_convert_fusion.5
  638.1 6.9 add_convert_fusion.4
  645.0 12.0 times_turned.15
  657.0 21.7 %reduce-scatter.11.cloned.1.call-done = bf16[192,2048]{1,0:T(8,128)(2,1)} async-done(((bf16[768,2048]{1,0:T(8,128)(2,1)}), bf16[192,2048]{1,0:T(8,128)(2,1)}) %reduce-scatter.11.cloned.1.call-update) | async-done | bytes 786448 | tf_op jit(solution)/shard_map/reduce_scatter | solution.py:291
  683.4 6.6 times.16
  692.6 12.6 %attend_back.2 = (bf16[192,2048]{1,0:T(8,128)(2,1)}, f32[768,256]{1,0:T(8,128)}) custom-call(bf16[192,2048]{1,0:T(8,128)(2,1)} %fusion.8.refs_0_, bf16[192,2048]{1,0:T(8,128)(2,1)} %convert_element_type.450.refs_1_, bf16[768,128]{1,0:T(8,128)(2,1)} %copy.89.refs_1_.refs_2_, bf16[768,128]{1,0:T(8,128)(2,1)} %copy.92.refs_3_, ...), custom_call_target="tpu_custom_call" | custom-call | flops 3019898880 | bytes 4128768 | tf_op jit(solution)/shard_map/attend_back/pallas_call | solution.py:420
  720.9 8.4 times_turned.16
  735.5 4.8 convolution_convert_fusion
  751.2 44.0 %collective-permute-done.57 = bf16[512,2048]{1,0:T(8,128)(2,1)S(1)} collective-permute-done((bf16[512,2048]{1,0:T(8,128)(2,1)S(1)}, bf16[512,2048]{1,0:T(8,128)(2,1)S(1)}, u32[]{:S(2)}, u32[]{:S(2)}) %collective-permute-start.57) | collective-permute-done | bytes 2097184 | tf_op jit(solution)/shard_map/ppermute | solution.py:43
  801.9 5.6 add_convert_fusion.3
  807.4 6.0 add_convert_fusion
  813.4 14.1 %times.17.left_ref = bf16[768,2048]{1,0:T(8,128)(2,1)} custom-call(bf16[768,2048]{1,0:T(8,128)(2,1)} %all-gather.22.cloned.1.call-done.left_ref, bf16[512,2048]{1,0:T(8,128)(2,1)} %pad_maximum_fusion.5.refs_0_, bf16[512,2048]{1,0:T(8,128)(2,1)} %collective-permute-done.30.refs_1_, bf16[512,2048]{1,0:T(8,128)(2,1)} %collective-permute-done.31.refs_2_, ...), custom_call_target="tpu_custom_call" | custom-call | flops 6442450944 | bytes 20971520 | tf_op jit(solution)/shard_map/times/pallas_call | solution.py:226
  827.6 11.9 times_turned.17
  854.1 7.0 convolution_convert_fusion.4
  861.5 14.4 %collective-permute-done.92 = bf16[256,2048]{1,0:T(8,128)(2,1)S(1)} collective-permute-done((bf16[256,2048]{1,0:T(8,128)(2,1)S(1)}, bf16[256,2048]{1,0:T(8,128)(2,1)S(1)}, u32[]{:S(2)}, u32[]{:S(2)}) %collective-permute-start.92) | collective-permute-done | bytes 1048608 | tf_op jit(solution)/shard_map/ppermute | solution.py:43
  877.5 7.9 convolution_convert_fusion.3
  890.4 29.2 %collective-permute-done.64 = bf16[512,2048]{1,0:T(8,128)(2,1)S(1)} collective-permute-done((bf16[512,2048]{1,0:T(8,128)(2,1)S(1)}, bf16[512,2048]{1,0:T(8,128)(2,1)S(1)}, u32[]{:S(2)}, u32[]{:S(2)}) %collective-permute-start.64) | collective-permute-done | bytes 2097184 | tf_op jit(solution)/shard_map/ppermute | solution.py:43
  923.1 7.2 collective-permute-done.63
  942.1 5.6 add_convert_fusion.1
  975.6 5.8 reorder.9
  988.1 5.8 collective-permute-done.66
  1013.5 12.8 %attend_back.3 = (bf16[192,2048]{1,0:T(8,128)(2,1)}, f32[768,256]{1,0:T(8,128)}) custom-call(bf16[192,2048]{1,0:T(8,128)(2,1)} %fusion.10.refs_0_, bf16[192,2048]{1,0:T(8,128)(2,1)} %pad_maximum_fusion.25.refs_1_, bf16[768,128]{1,0:T(8,128)(2,1)} %copy.84.refs_1_.refs_2_, bf16[768,128]{1,0:T(8,128)(2,1)} %copy.94.refs_3_, ...), custom_call_target="tpu_custom_call" | custom-call | flops 3019898880 | bytes 4128768 | tf_op jit(solution)/shard_map/attend_back/pallas_call | solution.py:420
  1057.7 5.0 times_turned.18
  1064.1 5.6 collective-permute-done.70
  1073.0 5.8 times_turned.19
  1084.7 5.8 reorder.10
  1099.0 4.8 reorder.11
  1119.6 12.4 collective-permute-done.91
  1137.3 5.8 collective-permute-done.87
  1143.3 22.3 %collective-permute-done.78 = bf16[512,1024]{1,0:T(8,128)(2,1)S(1)} collective-permute-done((bf16[512,1024]{1,0:T(8,128)(2,1)S(1)}, bf16[512,1024]{1,0:T(8,128)(2,1)S(1)}, u32[]{:S(2)}, u32[]{:S(2)}) %collective-permute-start.78) | collective-permute-done | bytes 1048608 | tf_op jit(solution)/shard_map/ppermute | solution.py:43
  1170.5 8.7 collective-permute-done.79
  1210.6 5.4 copy.97
  1222.8 8.8 collective-permute-done.76
  (777 shorter events, 428.0 us)
Async XLA Ops:
  7.2 46.4 %all-gather.24.cloned.1.call-start = ((), (), s32[]{:S(2)}) async-start(), calls=%async_computation.27 | async-start | bytes 1310720 | tf_op jit(solution)/shard_map/all_gather | solution.py:287
  7.2 40.3 %collective-permute-start.12 = (f32[2,512]{1,0:T(2,128)}, f32[2,512]{1,0:T(2,128)S(1)}, u32[]{:S(2)}, u32[]{:S(2)}) collective-permute-start(f32[2,512]{1,0:T(2,128)} %param.27), channel_id=1, source_target_pairs={{2,0},{3,1},{0,2},{1,3},{6,4},{7,5},{4,6},{5,7},{10,8},{11,9},{8,1... | collective-permute-start | bytes 12296 | tf_op jit(solution)/shard_map/ppermute | solution.py:48
  11.3 35.9 %collective-permute-start.11 = (f32[2,512]{1,0:T(2,128)}, f32[2,512]{1,0:T(2,128)S(1)}, u32[]{:S(2)}, u32[]{:S(2)}) collective-permute-start(f32[2,512]{1,0:T(2,128)} %param.27), channel_id=1, source_target_pairs={{1,0},{2,1},{3,2},{0,3},{5,4},{6,5},{7,6},{4,7},{9,8},{10,9},{11,1... | collective-permute-start | bytes 12296 | tf_op jit(solution)/shard_map/ppermute | solution.py:48
  12.7 34.9 %collective-permute-start.13 = (f32[2,512]{1,0:T(2,128)}, f32[2,512]{1,0:T(2,128)S(1)}, u32[]{:S(2)}, u32[]{:S(2)}) collective-permute-start(f32[2,512]{1,0:T(2,128)} %param.27), channel_id=1, source_target_pairs={{3,0},{0,1},{1,2},{2,3},{7,4},{4,5},{5,6},{6,7},{11,8},{8,9},{9,10... | collective-permute-start | bytes 12296 | tf_op jit(solution)/shard_map/ppermute | solution.py:48
  14.3 33.3 %collective-permute-start.6 = (bf16[2,256,64]{2,1,0:T(8,128)(2,1)S(1)}, bf16[2,256,64]{2,1,0:T(8,128)(2,1)S(1)}, u32[]{:S(2)}, u32[]{:S(2)}) collective-permute-start(bf16[2,256,64]{2,1,0:T(8,128)(2,1)S(1)} %copy.81), channel_id=1, source_target_pairs={{3,0},{0,1},{1,2},{2,3},{7,4},{4,5},{5,6},{6,7},{11,8},{8,9},{9,10... | collective-permute-start | bytes 196616 | tf_op jit(solution)/shard_map/ppermute | solution.py:48
  24.3 48.6 %all-to-all-start = ((bf16[8,24,2176]{2,1,0:T(8,128)(2,1)}), bf16[8,24,2176]{2,1,0:T(8,128)(2,1)}, u32[]{:S(2)}, u32[]{:S(2)}) async-start(bf16[8,24,2176]{2,1,0:T(8,128)(2,1)} %bitcast.3), calls=%async_computation | async-start | bytes 1671168 | tf_op jit(solution)/shard_map/all_to_all | solution.py:527
  28.7 55.1 %all-gather.10.cloned.1.call-start = ((), (), s32[]{:S(2)}) async-start(), calls=%async_computation.12 | async-start | bytes 1310720 | tf_op jit(solution)/shard_map/all_gather | solution.py:287
  71.3 53.0 %collective-permute-start.8 = (bf16[512,1280]{1,0:T(8,128)(2,1)S(1)}, bf16[512,1280]{1,0:T(8,128)(2,1)}, u32[]{:S(2)}, u32[]{:S(2)}) collective-permute-start(bf16[512,1280]{1,0:T(8,128)(2,1)S(1)} %pad_maximum_fusion.12.refs_0_), channel_id=1, source_target_pairs={{0,8},{4,12},{8,0},{12,4},{16,24},{20,28},{24,16},{28,20},{1,9},{5... | collective-permute-start | bytes 3932168 | tf_op jit(solution)/shard_map/ppermute | solution.py:43
  72.9 37.2 %all-to-all-start.1 = ((bf16[8,24,2048]{2,1,0:T(8,128)(2,1)}), bf16[8,24,2048]{2,1,0:T(8,128)(2,1)S(1)}, u32[]{:S(2)}, u32[]{:S(2)}) async-start(bf16[8,24,2048]{2,1,0:T(8,128)(2,1)} %bitcast.6), calls=%async_computation.1 | async-start | bytes 1572864 | tf_op jit(solution)/shard_map/all_to_all | solution.py:529
  76.4 192.1 %all-gather.14.cloned.1.call-start = ((), (), s32[]{:S(2)}) async-start(), calls=%async_computation.15 | async-start | bytes 1310720 | tf_op jit(solution)/shard_map/all_gather | solution.py:287
  79.5 46.0 %collective-permute-start.1 = (bf16[512,1024]{1,0:T(8,128)(2,1)}, bf16[512,1024]{1,0:T(8,128)(2,1)}, u32[]{:S(2)}, u32[]{:S(2)}) collective-permute-start(bf16[512,1024]{1,0:T(8,128)(2,1)} %pad_maximum_fusion.15.refs_0_), channel_id=1, source_target_pairs={{0,16},{4,20},{8,24},{12,28},{16,0},{20,4},{24,8},{28,12},{1,17},{... | collective-permute-start | bytes 3145736 | tf_op jit(solution)/shard_map/ppermute | solution.py:43
  86.0 38.9 %collective-permute-start.21 = (bf16[256,1024]{1,0:T(8,128)(2,1)}, bf16[256,1024]{1,0:T(8,128)(2,1)}, u32[]{:S(2)}, u32[]{:S(2)}) collective-permute-start(bf16[256,1024]{1,0:T(8,128)(2,1)} %pad_maximum_fusion.29), channel_id=1, source_target_pairs={{0,16},{4,20},{8,24},{12,28},{16,0},{20,4},{24,8},{28,12},{1,17},{... | collective-permute-start | bytes 1572872 | tf_op jit(solution)/shard_map/ppermute | solution.py:43
  86.2 54.3 %collective-permute-start.2 = (bf16[512,1024]{1,0:T(8,128)(2,1)}, bf16[512,1024]{1,0:T(8,128)(2,1)}, u32[]{:S(2)}, u32[]{:S(2)}) collective-permute-start(bf16[512,1024]{1,0:T(8,128)(2,1)} %pad_maximum_fusion.15.refs_0_), channel_id=1, source_target_pairs={{0,4},{4,0},{8,12},{12,8},{16,20},{20,16},{24,28},{28,24},{1,5},{5... | collective-permute-start | bytes 3145736 | tf_op jit(solution)/shard_map/ppermute | solution.py:43
  143.2 130.8 %all-gather.12.cloned.1.call-start = ((), (), s32[]{:S(2)}) async-start(), calls=%async_computation.13 | async-start | bytes 3932160 | tf_op jit(solution)/shard_map/all_gather | solution.py:287
  163.5 39.0 %collective-permute-start.25 = (bf16[256,2048]{1,0:T(8,128)(2,1)}, bf16[256,2048]{1,0:T(8,128)(2,1)}, u32[]{:S(2)}, u32[]{:S(2)}) collective-permute-start(bf16[256,2048]{1,0:T(8,128)(2,1)} %get-tuple-element.254), channel_id=1, source_target_pairs={{0,8},{4,12},{8,0},{12,4},{16,24},{20,28},{24,16},{28,20},{1,9},{5... | collective-permute-start | bytes 3145736 | tf_op jit(solution)/shard_map/ppermute | solution.py:43
  202.5 100.5 %all-gather.16.cloned.1.call-start = ((), (), s32[]{:S(2)}) async-start(), calls=%async_computation.16 | async-start | bytes 1310720 | tf_op jit(solution)/shard_map/all_gather | solution.py:287
  219.5 47.1 %collective-permute-start.30 = (bf16[512,2048]{1,0:T(8,128)(2,1)}, bf16[512,2048]{1,0:T(8,128)(2,1)}, u32[]{:S(2)}, u32[]{:S(2)}) collective-permute-start(bf16[512,2048]{1,0:T(8,128)(2,1)} %pad_maximum_fusion.5.refs_0_), channel_id=1, source_target_pairs={{0,8},{4,12},{8,0},{12,4},{16,24},{20,28},{24,16},{28,20},{1,9},{5... | collective-permute-start | bytes 6291464 | tf_op jit(solution)/shard_map/ppermute | solution.py:43
  220.3 46.7 %collective-permute-start.26 = (bf16[512,2048]{1,0:T(8,128)(2,1)}, bf16[512,2048]{1,0:T(8,128)(2,1)}, u32[]{:S(2)}, u32[]{:S(2)}) collective-permute-start(bf16[512,2048]{1,0:T(8,128)(2,1)} %pad_maximum_fusion.4.refs_0_), channel_id=1, source_target_pairs={{0,16},{4,20},{8,24},{12,28},{16,0},{20,4},{24,8},{28,12},{1,17},{... | collective-permute-start | bytes 6291464 | tf_op jit(solution)/shard_map/ppermute | solution.py:43
  221.5 52.0 %collective-permute-start.31 = (bf16[512,2048]{1,0:T(8,128)(2,1)}, bf16[512,2048]{1,0:T(8,128)(2,1)}, u32[]{:S(2)}, u32[]{:S(2)}) collective-permute-start(bf16[512,2048]{1,0:T(8,128)(2,1)} %pad_maximum_fusion.5.refs_0_), channel_id=1, source_target_pairs={{0,4},{4,0},{8,12},{12,8},{16,20},{20,16},{24,28},{28,24},{1,5},{5... | collective-permute-start | bytes 6291464 | tf_op jit(solution)/shard_map/ppermute | solution.py:43
  221.5 52.0 %collective-permute-start.27 = (bf16[512,2048]{1,0:T(8,128)(2,1)}, bf16[512,2048]{1,0:T(8,128)(2,1)}, u32[]{:S(2)}, u32[]{:S(2)}) collective-permute-start(bf16[512,2048]{1,0:T(8,128)(2,1)} %pad_maximum_fusion.4.refs_0_), channel_id=1, source_target_pairs={{0,4},{4,0},{8,12},{12,8},{16,20},{20,16},{24,28},{28,24},{1,5},{5... | collective-permute-start | bytes 6291464 | tf_op jit(solution)/shard_map/ppermute | solution.py:43
  268.6 123.1 %reduce-scatter.9.cloned.1.call-start = ((), (), s32[]{:S(2)}) async-start(), calls=%async_computation.14 | async-start | bytes 3932160 | tf_op jit(solution)/shard_map/reduce_scatter | solution.py:291
  274.1 31.9 %collective-permute-start.33 = (bf16[256,2304]{1,0:T(8,128)(2,1)S(1)}, bf16[256,2304]{1,0:T(8,128)(2,1)}, u32[]{:S(2)}, u32[]{:S(2)}) collective-permute-start(bf16[256,2304]{1,0:T(8,128)(2,1)S(1)} %fusion.56), channel_id=1, source_target_pairs={{0,8},{4,12},{8,0},{12,4},{16,24},{20,28},{24,16},{28,20},{1,9},{5... | collective-permute-start | bytes 3538952 | tf_op jit(solution)/shard_map/ppermute | solution.py:43
  300.3 223.2 %all-gather.18.cloned.1.call-start = ((), (), s32[]{:S(2)}) async-start(), calls=%async_computation.17 | async-start | bytes 3932160 | tf_op jit(solution)/shard_map/all_gather | solution.py:287
  307.4 72.4 %collective-permute-start.34 = (bf16[512,2304]{1,0:T(8,128)(2,1)S(1)}, bf16[512,2304]{1,0:T(8,128)(2,1)S(1)}, u32[]{:S(2)}, u32[]{:S(2)}) collective-permute-start(bf16[512,2304]{1,0:T(8,128)(2,1)S(1)} %pad_maximum_fusion.2.refs_0_), channel_id=1, source_target_pairs={{0,16},{4,20},{8,24},{12,28},{16,0},{20,4},{24,8},{28,12},{1,17},{... | collective-permute-start | bytes 7077896 | tf_op jit(solution)/shard_map/ppermute | solution.py:43
  330.8 49.5 %collective-permute-start.38 = (bf16[512,2048]{1,0:T(8,128)(2,1)S(1)}, bf16[512,2048]{1,0:T(8,128)(2,1)S(1)}, u32[]{:S(2)}, u32[]{:S(2)}) collective-permute-start(bf16[512,2048]{1,0:T(8,128)(2,1)S(1)} %pad_maximum_fusion.6.refs_0_), channel_id=1, source_target_pairs={{0,8},{4,12},{8,0},{12,4},{16,24},{20,28},{24,16},{28,20},{1,9},{5... | collective-permute-start | bytes 6291464 | tf_op jit(solution)/shard_map/ppermute | solution.py:43
  332.3 54.7 %collective-permute-start.35 = (bf16[512,2304]{1,0:T(8,128)(2,1)S(1)}, bf16[512,2304]{1,0:T(8,128)(2,1)S(1)}, u32[]{:S(2)}, u32[]{:S(2)}) collective-permute-start(bf16[512,2304]{1,0:T(8,128)(2,1)S(1)} %pad_maximum_fusion.2.refs_0_), channel_id=1, source_target_pairs={{0,4},{4,0},{8,12},{12,8},{16,20},{20,16},{24,28},{28,24},{1,5},{5... | collective-permute-start | bytes 7077896 | tf_op jit(solution)/shard_map/ppermute | solution.py:43
  442.5 129.9 %all-gather.20.cloned.1.call-start = ((), (), s32[]{:S(2)}) async-start(), calls=%async_computation.18 | async-start | bytes 3932160 | tf_op jit(solution)/shard_map/all_gather | solution.py:287
  447.5 231.1 %reduce-scatter.11.cloned.1.call-start = ((), (), s32[]{:S(2)}) async-start(), calls=%async_computation.19 | async-start | bytes 3932160 | tf_op jit(solution)/shard_map/reduce_scatter | solution.py:291
  474.2 46.8 %collective-permute-start.45 = (bf16[512,2048]{1,0:T(8,128)(2,1)S(1)}, bf16[512,2048]{1,0:T(8,128)(2,1)}, u32[]{:S(2)}, u32[]{:S(2)}) collective-permute-start(bf16[512,2048]{1,0:T(8,128)(2,1)S(1)} %pad_maximum_fusion.7.refs_0_), channel_id=1, source_target_pairs={{0,16},{4,20},{8,24},{12,28},{16,0},{20,4},{24,8},{28,12},{1,17},{... | collective-permute-start | bytes 6291464 | tf_op jit(solution)/shard_map/ppermute | solution.py:43
  475.7 46.4 %collective-permute-start.49 = (bf16[512,2048]{1,0:T(8,128)(2,1)S(1)}, bf16[512,2048]{1,0:T(8,128)(2,1)}, u32[]{:S(2)}, u32[]{:S(2)}) collective-permute-start(bf16[512,2048]{1,0:T(8,128)(2,1)S(1)} %pad_maximum_fusion.8.refs_0_), channel_id=1, source_target_pairs={{0,8},{4,12},{8,0},{12,4},{16,24},{20,28},{24,16},{28,20},{1,9},{5... | collective-permute-start | bytes 6291464 | tf_op jit(solution)/shard_map/ppermute | solution.py:43
  476.9 45.2 %collective-permute-start.46 = (bf16[512,2048]{1,0:T(8,128)(2,1)S(1)}, bf16[512,2048]{1,0:T(8,128)(2,1)S(1)}, u32[]{:S(2)}, u32[]{:S(2)}) collective-permute-start(bf16[512,2048]{1,0:T(8,128)(2,1)S(1)} %pad_maximum_fusion.7.refs_0_), channel_id=1, source_target_pairs={{0,4},{4,0},{8,12},{12,8},{16,20},{20,16},{24,28},{28,24},{1,5},{5... | collective-permute-start | bytes 6291464 | tf_op jit(solution)/shard_map/ppermute | solution.py:43
  476.9 46.5 %collective-permute-start.50 = (bf16[512,2048]{1,0:T(8,128)(2,1)S(1)}, bf16[512,2048]{1,0:T(8,128)(2,1)}, u32[]{:S(2)}, u32[]{:S(2)}) collective-permute-start(bf16[512,2048]{1,0:T(8,128)(2,1)S(1)} %pad_maximum_fusion.8.refs_0_), channel_id=1, source_target_pairs={{0,4},{4,0},{8,12},{12,8},{16,20},{20,16},{24,28},{28,24},{1,5},{5... | collective-permute-start | bytes 6291464 | tf_op jit(solution)/shard_map/ppermute | solution.py:43
  619.4 194.0 %all-gather.22.cloned.1.call-start = ((), (), s32[]{:S(2)}) async-start(), calls=%async_computation.21 | async-start | bytes 3932160 | tf_op jit(solution)/shard_map/all_gather | solution.py:287
  740.3 67.2 %collective-permute-start.59 = (bf16[1024,2304]{1,0:T(8,128)(2,1)}, bf16[1024,2304]{1,0:T(8,128)(2,1)}, u32[]{:S(2)}, u32[]{:S(2)}) collective-permute-start(bf16[1024,2304]{1,0:T(8,128)(2,1)} %convolution_convert_fusion), channel_id=1, source_target_pairs={{0,4},{4,0},{8,12},{12,8},{16,20},{20,16},{24,28},{28,24},{1,5},{5... | collective-permute-start | bytes 14155784 | tf_op jit(solution)/shard_map/ppermute | solution.py:43
  743.6 58.3 %collective-permute-start.60 = (bf16[1024,2048]{1,0:T(8,128)(2,1)}, bf16[1024,2048]{1,0:T(8,128)(2,1)}, u32[]{:S(2)}, u32[]{:S(2)}) collective-permute-start(bf16[1024,2048]{1,0:T(8,128)(2,1)} %convolution_convert_fusion.2), channel_id=1, source_target_pairs={{0,4},{4,0},{8,12},{12,8},{16,20},{20,16},{24,28},{28,24},{1,5},{5... | collective-permute-start | bytes 12582920 | tf_op jit(solution)/shard_map/ppermute | solution.py:43
  744.1 206.9 %reduce-scatter.15.cloned.1.call-start = ((), (), s32[]{:S(2)}) async-start(), calls=%async_computation.22 | async-start | bytes 3932160 | tf_op jit(solution)/shard_map/reduce_scatter | solution.py:291
  747.6 47.6 %collective-permute-start.57 = (bf16[512,2048]{1,0:T(8,128)(2,1)S(1)}, bf16[512,2048]{1,0:T(8,128)(2,1)S(1)}, u32[]{:S(2)}, u32[]{:S(2)}) collective-permute-start(bf16[512,2048]{1,0:T(8,128)(2,1)S(1)} %pad_maximum_fusion.9), channel_id=1, source_target_pairs={{0,8},{4,12},{8,0},{12,4},{16,24},{20,28},{24,16},{28,20},{1,9},{5... | collective-permute-start | bytes 6291464 | tf_op jit(solution)/shard_map/ppermute | solution.py:43
  749.7 47.6 %collective-permute-start.58 = (bf16[512,2048]{1,0:T(8,128)(2,1)S(1)}, bf16[512,2048]{1,0:T(8,128)(2,1)S(1)}, u32[]{:S(2)}, u32[]{:S(2)}) collective-permute-start(bf16[512,2048]{1,0:T(8,128)(2,1)S(1)} %slice.842), channel_id=1, source_target_pairs={{0,16},{4,20},{8,24},{12,28},{16,0},{20,4},{24,8},{28,12},{1,17},{... | collective-permute-start | bytes 6291464 | tf_op jit(solution)/shard_map/ppermute | solution.py:43
  839.5 133.3 %reduce-scatter.13.cloned.1.call-start = ((), (), s32[]{:S(2)}) async-start(), calls=%async_computation.20 | async-start | bytes 3932160 | tf_op jit(solution)/shard_map/reduce_scatter | solution.py:291
  850.2 36.9 %collective-permute-start.90 = (bf16[256,2048]{1,0:T(8,128)(2,1)S(1)}, bf16[256,2048]{1,0:T(8,128)(2,1)S(1)}, u32[]{:S(2)}, u32[]{:S(2)}) collective-permute-start(bf16[256,2048]{1,0:T(8,128)(2,1)S(1)} %slice.932), channel_id=1, source_target_pairs={{0,16},{4,20},{8,24},{12,28},{16,0},{20,4},{24,8},{28,12},{1,17},{... | collective-permute-start | bytes 3145736 | tf_op jit(solution)/shard_map/ppermute | solution.py:43
  853.5 66.1 %collective-permute-start.64 = (bf16[512,2048]{1,0:T(8,128)(2,1)S(1)}, bf16[512,2048]{1,0:T(8,128)(2,1)S(1)}, u32[]{:S(2)}, u32[]{:S(2)}) collective-permute-start(bf16[512,2048]{1,0:T(8,128)(2,1)S(1)} %slice.850), channel_id=1, source_target_pairs={{0,16},{4,20},{8,24},{12,28},{16,0},{20,4},{24,8},{28,12},{1,17},{... | collective-permute-start | bytes 6291464 | tf_op jit(solution)/shard_map/ppermute | solution.py:43
  861.1 72.2 %collective-permute-start.61 = (bf16[1024,2048]{1,0:T(8,128)(2,1)}, bf16[1024,2048]{1,0:T(8,128)(2,1)S(1)}, u32[]{:S(2)}, u32[]{:S(2)}) collective-permute-start(bf16[1024,2048]{1,0:T(8,128)(2,1)} %convolution_convert_fusion.4), channel_id=1, source_target_pairs={{0,4},{4,0},{8,12},{12,8},{16,20},{20,16},{24,28},{28,24},{1,5},{5... | collective-permute-start | bytes 12582920 | tf_op jit(solution)/shard_map/ppermute | solution.py:43
  876.0 54.2 %collective-permute-start.63 = (bf16[512,2304]{1,0:T(8,128)(2,1)S(1)}, bf16[512,2304]{1,0:T(8,128)(2,1)S(1)}, u32[]{:S(2)}, u32[]{:S(2)}) collective-permute-start(bf16[512,2304]{1,0:T(8,128)(2,1)S(1)} %pad_maximum_fusion.3), channel_id=1, source_target_pairs={{0,8},{4,12},{8,0},{12,4},{16,24},{20,28},{24,16},{28,20},{1,9},{5... | collective-permute-start | bytes 7077896 | tf_op jit(solution)/shard_map/ppermute | solution.py:43
  885.4 56.7 %collective-permute-start.62 = (bf16[1024,2048]{1,0:T(8,128)(2,1)}, bf16[1024,2048]{1,0:T(8,128)(2,1)}, u32[]{:S(2)}, u32[]{:S(2)}) collective-permute-start(bf16[1024,2048]{1,0:T(8,128)(2,1)} %convolution_convert_fusion.3), channel_id=1, source_target_pairs={{0,4},{4,0},{8,12},{12,8},{16,20},{20,16},{24,28},{28,24},{1,5},{5... | collective-permute-start | bytes 12582920 | tf_op jit(solution)/shard_map/ppermute | solution.py:43
  921.6 125.9 %collective-permute-start.88 = (bf16[256,2048]{1,0:T(8,128)(2,1)}, bf16[256,2048]{1,0:T(8,128)(2,1)}, u32[]{:S(2)}, u32[]{:S(2)}) collective-permute-start(bf16[256,2048]{1,0:T(8,128)(2,1)} %slice.921), channel_id=1, source_target_pairs={{0,8},{4,12},{8,0},{12,4},{16,24},{20,28},{24,16},{28,20},{1,9},{5... | collective-permute-start | bytes 3145736 | tf_op jit(solution)/shard_map/ppermute | solution.py:43
  940.6 57.1 %collective-permute-start.65 = (bf16[512,2048]{1,0:T(8,128)(2,1)}, bf16[512,2048]{1,0:T(8,128)(2,1)}, u32[]{:S(2)}, u32[]{:S(2)}) collective-permute-start(bf16[512,2048]{1,0:T(8,128)(2,1)} %pad_maximum_fusion.10), channel_id=1, source_target_pairs={{0,8},{4,12},{8,0},{12,4},{16,24},{20,28},{24,16},{28,20},{1,9},{5... | collective-permute-start | bytes 6291464 | tf_op jit(solution)/shard_map/ppermute | solution.py:43
  950.4 43.5 %collective-permute-start.66 = (bf16[512,2048]{1,0:T(8,128)(2,1)}, bf16[512,2048]{1,0:T(8,128)(2,1)}, u32[]{:S(2)}, u32[]{:S(2)}) collective-permute-start(bf16[512,2048]{1,0:T(8,128)(2,1)} %slice.857), channel_id=1, source_target_pairs={{0,16},{4,20},{8,24},{12,28},{16,0},{20,4},{24,8},{28,12},{1,17},{... | collective-permute-start | bytes 6291464 | tf_op jit(solution)/shard_map/ppermute | solution.py:43
  970.8 35.4 %collective-permute-start.67 = (bf16[1024,1024]{1,0:T(8,128)(2,1)}, bf16[1024,1024]{1,0:T(8,128)(2,1)}, u32[]{:S(2)}, u32[]{:S(2)}) collective-permute-start(bf16[1024,1024]{1,0:T(8,128)(2,1)} %convolution_convert_fusion.17), channel_id=1, source_target_pairs={{0,4},{4,0},{8,12},{12,8},{16,20},{20,16},{24,28},{28,24},{1,5},{5... | collective-permute-start | bytes 6291464 | tf_op jit(solution)/shard_map/ppermute | solution.py:43
  972.8 37.0 %collective-permute-start.68 = (bf16[1024,1024]{1,0:T(8,128)(2,1)}, bf16[1024,1024]{1,0:T(8,128)(2,1)}, u32[]{:S(2)}, u32[]{:S(2)}) collective-permute-start(bf16[1024,1024]{1,0:T(8,128)(2,1)} %convolution_convert_fusion.16), channel_id=1, source_target_pairs={{0,4},{4,0},{8,12},{12,8},{16,20},{20,16},{24,28},{28,24},{1,5},{5... | collective-permute-start | bytes 6291464 | tf_op jit(solution)/shard_map/ppermute | solution.py:43
  983.8 55.4 %all-to-all-start.2 = ((bf16[8,24,2048]{2,1,0:T(8,128)(2,1)}), bf16[8,24,2048]{2,1,0:T(8,128)(2,1)}, u32[]{:S(2)}, u32[]{:S(2)}) async-start(bf16[8,24,2048]{2,1,0:T(8,128)(2,1)} %bitcast.45), calls=%async_computation.6 | async-start | bytes 1572864 | tf_op jit(solution)/shard_map/all_to_all | solution.py:780
  988.1 245.5 %reduce-scatter.19.cloned.1.call-start = ((), (), s32[]{:S(2)}) async-start(), calls=%async_computation.24 | async-start | bytes 1474560 | tf_op jit(solution)/shard_map/reduce_scatter | solution.py:291
  993.9 32.4 %collective-permute-start.83 = (bf16[256,2304]{1,0:T(8,128)(2,1)}, bf16[256,2304]{1,0:T(8,128)(2,1)}, u32[]{:S(2)}, u32[]{:S(2)}) collective-permute-start(bf16[256,2304]{1,0:T(8,128)(2,1)} %slice.892), channel_id=1, source_target_pairs={{0,16},{4,20},{8,24},{12,28},{16,0},{20,4},{24,8},{28,12},{1,17},{... | collective-permute-start | bytes 3538952 | tf_op jit(solution)/shard_map/ppermute | solution.py:43
  1034.0 201.5 %reduce-scatter.23.cloned.1.call-start = ((), (), s32[]{:S(2)}) async-start(), calls=%async_computation.26 | async-start | bytes 1310720 | tf_op jit(solution)/shard_map/reduce_scatter | solution.py:291
  1038.7 65.2 %collective-permute-start.89 = (bf16[256,2048]{1,0:T(8,128)(2,1)}, bf16[256,2048]{1,0:T(8,128)(2,1)}, u32[]{:S(2)}, u32[]{:S(2)}) collective-permute-start(bf16[256,2048]{1,0:T(8,128)(2,1)} %slice.930), channel_id=1, source_target_pairs={{0,16},{4,20},{8,24},{12,28},{16,0},{20,4},{24,8},{28,12},{1,17},{... | collective-permute-start | bytes 3145736 | tf_op jit(solution)/shard_map/ppermute | solution.py:43
  1046.1 60.7 %collective-permute-start.84 = (bf16[512,1024]{1,0:T(8,128)(2,1)}, bf16[512,1024]{1,0:T(8,128)(2,1)}, u32[]{:S(2)}, u32[]{:S(2)}) collective-permute-start(bf16[512,1024]{1,0:T(8,128)(2,1)} %pad_maximum_fusion.21), channel_id=1, source_target_pairs={{0,8},{4,12},{8,0},{12,4},{16,24},{20,28},{24,16},{28,20},{1,9},{5... | collective-permute-start | bytes 3145736 | tf_op jit(solution)/shard_map/ppermute | solution.py:43
  1062.7 46.1 %collective-permute-start.86 = (bf16[512,1024]{1,0:T(8,128)(2,1)}, bf16[512,1024]{1,0:T(8,128)(2,1)}, u32[]{:S(2)}, u32[]{:S(2)}) collective-permute-start(bf16[512,1024]{1,0:T(8,128)(2,1)} %slice.915), channel_id=1, source_target_pairs={{0,16},{4,20},{8,24},{12,28},{16,0},{20,4},{24,8},{28,12},{1,17},{... | collective-permute-start | bytes 3145736 | tf_op jit(solution)/shard_map/ppermute | solution.py:43
  1064.1 47.9 %collective-permute-start.77 = (bf16[1024,1024]{1,0:T(8,128)(2,1)}, bf16[1024,1024]{1,0:T(8,128)(2,1)}, u32[]{:S(2)}, u32[]{:S(2)}) collective-permute-start(bf16[1024,1024]{1,0:T(8,128)(2,1)} %convolution_convert_fusion.15), channel_id=1, source_target_pairs={{0,4},{4,0},{8,12},{12,8},{16,20},{20,16},{24,28},{28,24},{1,5},{5... | collective-permute-start | bytes 6291464 | tf_op jit(solution)/shard_map/ppermute | solution.py:43
  1082.1 33.2 %collective-permute-start.80 = (bf16[1024,1280]{1,0:T(8,128)(2,1)}, bf16[1024,1280]{1,0:T(8,128)(2,1)}, u32[]{:S(2)}, u32[]{:S(2)}) collective-permute-start(bf16[1024,1280]{1,0:T(8,128)(2,1)} %convolution_convert_fusion.1), channel_id=1, source_target_pairs={{0,4},{4,0},{8,12},{12,8},{16,20},{20,16},{24,28},{28,24},{1,5},{5... | collective-permute-start | bytes 7864328 | tf_op jit(solution)/shard_map/ppermute | solution.py:43
  1093.1 127.3 %all-to-all-start.3 = ((bf16[8,24,2048]{2,1,0:T(8,128)(2,1)}), bf16[8,24,2048]{2,1,0:T(8,128)(2,1)}, u32[]{:S(2)}, u32[]{:S(2)}) async-start(bf16[8,24,2048]{2,1,0:T(8,128)(2,1)} %bitcast.47), calls=%async_computation.7 | async-start | bytes 1572864 | tf_op jit(solution)/shard_map/all_to_all | solution.py:781
  1097.3 138.2 %reduce-scatter.21.cloned.1.call-start = ((), (), s32[]{:S(2)}) async-start(), calls=%async_computation.25 | async-start | bytes 1310720 | tf_op jit(solution)/shard_map/reduce_scatter | solution.py:291
  1115.3 50.3 %collective-permute-start.78 = (bf16[512,1024]{1,0:T(8,128)(2,1)S(1)}, bf16[512,1024]{1,0:T(8,128)(2,1)S(1)}, u32[]{:S(2)}, u32[]{:S(2)}) collective-permute-start(bf16[512,1024]{1,0:T(8,128)(2,1)S(1)} %pad_maximum_fusion.19), channel_id=1, source_target_pairs={{0,8},{4,12},{8,0},{12,4},{16,24},{20,28},{24,16},{28,20},{1,9},{5... | collective-permute-start | bytes 3145736 | tf_op jit(solution)/shard_map/ppermute | solution.py:43
  1132.0 35.6 %collective-permute-start.81 = (bf16[512,1280]{1,0:T(8,128)(2,1)S(1)}, bf16[512,1280]{1,0:T(8,128)(2,1)S(1)}, u32[]{:S(2)}, u32[]{:S(2)}) collective-permute-start(bf16[512,1280]{1,0:T(8,128)(2,1)S(1)} %slice.880), channel_id=1, source_target_pairs={{0,16},{4,20},{8,24},{12,28},{16,0},{20,4},{24,8},{28,12},{1,17},{... | collective-permute-start | bytes 3932168 | tf_op jit(solution)/shard_map/ppermute | solution.py:43
  1136.4 65.1 %collective-permute-start.73 = (f32[18,2048]{1,0:T(8,128)S(1)}, f32[18,2048]{1,0:T(8,128)}, u32[]{:S(2)}, u32[]{:S(2)}) collective-permute-start(f32[18,2048]{1,0:T(8,128)S(1)} %add.493), channel_id=1, source_target_pairs={{0,8},{4,12},{8,0},{12,4},{16,24},{20,28},{24,16},{28,20},{1,9},{5... | collective-permute-start | bytes 442376 | tf_op jit(solution)/shard_map/ppermute | solution.py:43
  1170.5 67.5 %reduce-scatter.17.cloned.1.call-start = ((), (), s32[]{:S(2)}) async-start(), calls=%async_computation.23 | async-start | bytes 1474560 | tf_op jit(solution)/shard_map/reduce_scatter | solution.py:291
  (189 other events, 2555.5 us)
Sparse Core Ops, SparseCore 0:
  20.1 26.3 all-gather.23
  48.7 27.4 all-gather.9
  143.4 38.5 all-gather.13
  202.6 69.5 all-gather.11
  274.2 28.7 all-gather.15
  305.7 61.4 reduce-scatter.8
  442.7 65.9 all-gather.17
  510.2 62.1 all-gather.19
  619.6 59.0 reduce-scatter.10
  744.2 62.8 all-gather.21
  839.6 59.6 reduce-scatter.14
  901.5 60.2 reduce-scatter.12
  1034.1 34.9 reduce-scatter.18
  1071.9 27.0 reduce-scatter.22
  1170.6 24.3 reduce-scatter.20
  1199.8 31.1 reduce-scatter.16

commit v2 on v1

--- a/solution.py
+++ b/solution.py
@@ -9,6 +9,7 @@
 EPSILON = 1e-05
 BF16 = jnp.bfloat16
 F32 = jnp.float32
+LIGHT = pl.CostEstimate(flops=1, transcendentals=0, bytes_accessed=1)
 
 
 def layer_norm(values, scales, offsets):
@@ -88,14 +89,18 @@
             for array in group
         ]
         self.taken = 0
+        self.come = []
 
     def send(self, *gate):
+        gate = gate + tuple(self.come)
+        self.come = []
         for member in self.members:
             order, parts = member
             bit = order[self.taken]
             blocks = [block for _, part in parts for block in part]
             whole = join_rows([array for array, _ in parts])
             come = flip(after(whole, *gate) if gate else whole, bit)
+            self.come.append(come)
             member[1] = [(whole, blocks), (come, [block | bit for block in blocks])]
         self.taken += 1
         return self
@@ -109,10 +114,37 @@
     def finish(self, *gate):
         while self.taken < len(plane_bits()):
             self.send(*gate)
+        come = tuple(self.come)
         return [
-            parts + [(flip(array, 1), [block | 1 for block in blocks]) for array, blocks in parts]
+            parts
+            + [
+                (flip(after(array, *come), 1), [block | 1 for block in blocks])
+                for array, blocks in parts
+            ]
             for _, parts in self.members
         ]
+
+
+def add_blocks(half, count, keep, come, kind):
+    rows, columns = half.shape[0] // count, half.shape[1]
+    stride = keep[1] - keep[0] if len(keep) > 1 else 1
+
+    def kernel(half_ref, come_ref, out_ref):
+        out_ref[...] = (half_ref[...].astype(F32) + come_ref[...].astype(F32)).astype(kind)
+
+    block = (rows, columns)
+    return pl.pallas_call(
+        kernel,
+        grid=(len(keep),),
+        in_specs=[
+            pl.BlockSpec(block, lambda i: (keep[0] + i * stride, 0)),
+            pl.BlockSpec(block, lambda i: (i, 0)),
+        ],
+        out_specs=pl.BlockSpec(block, lambda i: (i, 0)),
+        out_shape=jax.ShapeDtypeStruct(come.shape, kind),
+        cost_estimate=LIGHT,
+        name="add_blocks",
+    )(half, come)
 
 
 class Scatter:
@@ -129,23 +161,29 @@
 
     def send(self, *gate):
         self.come = []
+        self.sent = []
         for order, half, blocks in self.members:
             sent = [block for block in blocks if block & order[self.taken]]
             piece = blocks_of([(half, blocks)], sent)
             piece = after(piece, *gate) if gate else piece
+            self.sent.append(piece)
             self.come.append(flip(piece, order[self.taken]))
         self.taken += 1
         return self
 
     def settle(self, *late):
         last = self.taken == len(plane_bits())
+        late = late + tuple(self.come)
         for member, come in zip(self.members, self.come):
             order, half, blocks = member
             keep = [block for block in blocks if not block & order[self.taken - 1]]
             if late:
                 come = after(come, *late)
-            total = blocks_of([(half, blocks)], keep).astype(F32) + come.astype(F32)
-            member[1:] = [total if last else total.astype(BF16), keep]
+            spots = [blocks.index(block) for block in keep]
+            member[1:] = [
+                add_blocks(half, len(blocks), spots, come, F32 if last else BF16),
+                keep,
+            ]
         self.come = None
         return self
 
@@ -161,7 +199,37 @@
         return [half.astype(F32) for _, half, _ in self.members]
 
 
-def gradient_half(features, values):
+def turned_product(features, values, side, extra=None):
+    rows, depth = features.shape
+    columns = values.shape[1]
+    tile = 256
+    steps = depth // 2 // tile
+
+    def kernel(left_ref, right_ref, *refs):
+        total = matmul(left_ref[...].T, right_ref[...])
+        if extra is not None:
+            total = total + refs[0][...].astype(F32)
+        refs[-1][...] = total.astype(BF16)
+
+    tiles = pl.BlockSpec((tile, columns), lambda i: (i, 0))
+    return pl.pallas_call(
+        kernel,
+        grid=(steps,),
+        in_specs=[
+            pl.BlockSpec((rows, tile), lambda i: (0, i + side * steps)),
+            pl.BlockSpec((rows, columns), lambda i: (0, 0)),
+        ]
+        + ([tiles] if extra is not None else []),
+        out_specs=tiles,
+        out_shape=jax.ShapeDtypeStruct((depth // 2, columns), BF16),
+        cost_estimate=LIGHT,
+        name="turned_product",
+    )(features, values, *([extra] if extra is not None else []))
+
+
+def gradient_half(features, values, kernel=False):
+    if kernel:
+        return turned_product(features, values, 0, flip(turned_product(features, values, 1), 1))
     half = features.shape[1] // 2
     far = contract_rows(features[:, half:], values).astype(BF16)
     near = contract_rows(features[:, :half], values) + flip(far, 1).astype(F32)
@@ -231,11 +299,7 @@
         + [pl.BlockSpec((extra.shape[0], tile), lambda j: (0, j)) for extra in extras],
         out_specs=[pl.BlockSpec((rows, tile), lambda j: (0, j)) for _ in types],
         out_shape=[jax.ShapeDtypeStruct((rows, columns), kind) for kind in types],
-        cost_estimate=pl.CostEstimate(
-            flops=2 * rows * depth * columns,
-            transcendentals=rows * columns if extras else 0,
-            bytes_accessed=2 * depth * (rows + columns) + 6 * rows * columns,
-        ),
+        cost_estimate=LIGHT,
         name="times",
     )(left, *[array for array, _ in parts], *extras)
 
@@ -266,11 +330,7 @@
         in_specs=[pl.BlockSpec((tile, depth), lambda i: (i, 0))] + whole,
         out_specs=pl.BlockSpec((tile, count * height), lambda i: (i, 0)),
         out_shape=jax.ShapeDtypeStruct((rows, count * height), kind),
-        cost_estimate=pl.CostEstimate(
-            flops=2 * rows * depth * count * height,
-            transcendentals=0,
-            bytes_accessed=2 * depth * (rows + count * height) + 4 * rows * count * height,
-        ),
+        cost_estimate=LIGHT,
         name="times_turned",
     )(left, *[array for array, _ in parts])
 
@@ -279,8 +339,8 @@
     return [array for parts in weights for array, _ in parts]
 
 
-def tensor_slots(values):
-    return [values] + [turn(values, k) for k in range(1, lax.axis_size("tensor"))]
+def tensor_swap(values):
+    return lax.all_to_all(values, "tensor", split_axis=0, concat_axis=0, tiled=True)
 
 
 def tensor_rows(values):
@@ -291,23 +351,25 @@
     return lax.psum_scatter(values, "tensor", scatter_dimension=0, tiled=True)
 
 
-def sum_columns(whole, count):
+def stack_columns(whole, count):
     width = whole.shape[1] // count
     whole = whole.astype(BF16)
-    pieces = [whole[:, k * width : (k + 1) * width] for k in range(count)]
-    return tensor_sum(jnp.concatenate(pieces, axis=0)).astype(F32)
-
-
-def sum_query(whole, width, query_cols, pair_cols):
-    count = lax.axis_size("tensor")
+    return jnp.concatenate([whole[:, k * width : (k + 1) * width] for k in range(count)], axis=0)
+
+
+def stack_query(whole, width, query_cols, pair_cols):
     rows = whole.shape[0]
     whole = whole.astype(BF16)
     pieces = []
-    for k in range(count):
+    for k in range(width // query_cols):
         pieces.append(whole[:, k * query_cols : (k + 1) * query_cols])
         pair = whole[:, width + k * pair_cols : width + (k + 1) * pair_cols]
         pieces.append(pair.reshape(rows * pair_cols // query_cols, query_cols))
-    total = tensor_sum(jnp.concatenate(pieces, axis=0)).astype(F32)
+    return jnp.concatenate(pieces, axis=0)
+
+
+def split_query(total, rows, pair_cols):
+    total = total.astype(F32)
     return total[:rows], total[rows:].reshape(rows, pair_cols)
 
 
@@ -330,6 +392,7 @@
             out_specs=pl.BlockSpec((rows, width), lambda j, table: (0, j)),
         ),
         out_shape=jax.ShapeDtypeStruct(values.shape, values.dtype),
+        cost_estimate=LIGHT,
         name="reorder",
     )(table, values)
 
@@ -377,11 +440,7 @@
             jax.ShapeDtypeStruct((rows, columns), BF16),
             jax.ShapeDtypeStruct((pairs, 1, 2 * rows), F32),
         ],
-        cost_estimate=pl.CostEstimate(
-            flops=4 * rows * keys * columns,
-            transcendentals=rows * keys * columns // HEAD,
-            bytes_accessed=4 * rows * columns + 8 * keys * rows,
-        ),
+        cost_estimate=LIGHT,
         name="attend",
     )(queries, key_rows, value_t, bias)
 
@@ -437,11 +496,7 @@
             jax.ShapeDtypeStruct((rows, columns), BF16),
             jax.ShapeDtypeStruct((keys, 2 * HEAD), F32),
         ],
-        cost_estimate=pl.CostEstimate(
-            flops=10 * rows * keys * columns,
-            transcendentals=rows * keys * columns // HEAD,
-            bytes_accessed=6 * rows * columns + 12 * keys * rows,
-        ),
+        cost_estimate=LIGHT,
         name="attend_back",
     )(queries, douts, key_rows, value_rows, key_t, bias, log_totals)
 
@@ -484,36 +539,6 @@
         jnp.asarray(place_of, jnp.int32), jnp.arange(dp_count, dtype=jnp.int32) ^ dp_rank
     )
 
-    last = layer_total - 1
-    split = width // 2
-    cut = tensor_count // 2
-    bias_slots = jnp.roll(
-        jnp.concatenate(tensor_slots(query_bias), axis=1), tensor_rank * query_cols, axis=1
-    )
-    kv_full = jnp.roll(
-        jnp.concatenate(tensor_slots(kv_weight), axis=2), tensor_rank * pair_cols, axis=2
-    )
-    depth = query_weight.shape[1]
-
-    def columns(rows, *more):
-        count = rows.shape[0] // depth
-        pieces = [rows[k * depth : (k + 1) * depth] for k in range(count)]
-        return jnp.concatenate(pieces + list(more), axis=1)
-
-    out_turned = [out_weight[l].T for l in range(layer_total)]
-    down_turned = [down_weight[l].T for l in range(layer_total)]
-    query_rows = tensor_rows(query_weight[0])
-    out_rows = tensor_rows(after(out_turned[0], query_rows))
-    cut_rows = cut * depth
-    ff_gather = Gather([up_weight[0]], [down_turned[0]]).send()
-    query_gather = Gather(
-        [columns(query_rows[:cut_rows])], [columns(query_rows[cut_rows:], kv_full[0])]
-    )
-    w_query = query_gather.finish()
-    out_gather = Gather([columns(out_rows[:cut_rows])], [columns(out_rows[cut_rows:])])
-    w_out = out_gather.finish()
-    ff_gather.settle()
-
     target_dev = deal // local_rows // tensor_count
     target_row = deal % local_rows
     dev_ids = jnp.arange(dp_count, dtype=jnp.int32)
@@ -534,19 +559,11 @@
     tangent = last_branch.astype(F32)
     stream = after(stream, last_branch)
 
-    vectors = jnp.concatenate(
-        [norm1_gain, norm1_shift, out_bias, norm2_gain, norm2_shift, down_bias], axis=0
-    )
-    vectors = reorder(vectors, to_slots)
-    gain_one, shift_one, bias_out, gain_two, shift_two, bias_down = [
-        vectors[i * layer_total : (i + 1) * layer_total] for i in range(6)
-    ]
-
     places = jnp.arange(group_rows, dtype=jnp.int32)
-    key_places = (places + tensor_rank * local_rows) % group_rows
-    key_labels = jnp.roll(segment, -tensor_rank * local_rows)
-    allowed = (key_places[:, None] <= key_places[None, :local_rows]) & (
-        key_labels[:, None] == key_labels[None, :local_rows]
+    own_places = tensor_rank * local_rows + row_ids
+    own_labels = lax.dynamic_slice_in_dim(segment, tensor_rank * local_rows, local_rows)
+    allowed = (places[:, None] <= own_places[None, :]) & (
+        segment[:, None] == own_labels[None, :]
     )
     score_bias = jnp.where(allowed, 0.0, -1e30).astype(F32)
     score_bias = jnp.concatenate([score_bias, score_bias], axis=1)
@@ -564,24 +581,116 @@
             start += size
         return total
 
+    last = layer_total - 1
+    split = width // 2
+    cut = tensor_count // 2
+    depth = query_weight.shape[1]
+    pair_rows = depth * pair_cols // query_cols
+    bias_rows = 16
+
+    def query_payload(l):
+        rest, terms = query_bias[l], []
+        for _ in range(3):
+            terms.append(rest.astype(BF16))
+            rest = rest - terms[-1].astype(F32)
+        terms = jnp.pad(jnp.stack(terms), ((0, bias_rows - 3), (0, 0)))
+        return jnp.concatenate(
+            [query_weight[l], kv_weight[l].reshape(pair_rows, query_cols), terms], axis=0
+        )
+
+    def query_parts(rows):
+        size = rows.shape[0] // tensor_count
+        each = [rows[k * size : (k + 1) * size] for k in range(tensor_count)]
+        pair = [part[depth : depth + pair_rows].reshape(depth, pair_cols) for part in each]
+        bias = [
+            sum(part[depth + pair_rows + i].astype(F32) for i in range(3)) for part in each
+        ]
+        return (
+            [part[:depth] for part in each],
+            jnp.concatenate(pair, axis=1),
+            jnp.concatenate(bias),
+        )
+
+    def columns(rows):
+        count = rows.shape[0] // depth
+        return jnp.concatenate([rows[k * depth : (k + 1) * depth] for k in range(count)], axis=1)
+
+    out_turned = [out_weight[l].T for l in range(layer_total)]
+    down_turned = [down_weight[l].T for l in range(layer_total)]
+    query_rows = tensor_rows(query_payload(0))
+    out_rows = tensor_rows(after(out_turned[0], tangent_come))
+    if last > 0:
+        rest = jnp.concatenate([query_payload(1), out_turned[1]], axis=0)
+        rest = tensor_rows(after(rest, tokens_come))
+        size = rest.shape[0] // tensor_count
+        rest = [rest[k * size : (k + 1) * size] for k in range(tensor_count)]
+    query_rows = after(query_rows, tokens_come, tangent_come, score_bias)
+    cut_rows = cut * depth
+    query_each, kv_full, bias_full = query_parts(query_rows)
+    query_gather = Gather(
+        [jnp.concatenate(query_each[:cut], axis=1)],
+        [jnp.concatenate(query_each[cut:] + [kv_full], axis=1)],
+    ).send()
+    out_gather = Gather([columns(out_rows[:cut_rows])], [columns(out_rows[cut_rows:])]).send(
+        *query_gather.come
+    )
+    w_query = query_gather.finish()
+    early_rows = local_rows // 2
+    if last > 0:
+        query_rows = jnp.concatenate([part[: size - depth] for part in rest], axis=0)
+        out_rows = jnp.concatenate([part[size - depth :] for part in rest], axis=0)
+        branch_early = tensor_rows(last_branch[:early_rows])
+
+    def branch_whole(early, late):
+        parts = []
+        for k in range(tensor_count):
+            parts.append(early[k * early_rows : (k + 1) * early_rows])
+            size = local_rows - early_rows
+            parts.append(late[k * size : (k + 1) * size])
+        return jnp.concatenate(parts, axis=0)
+
+    vectors = jnp.concatenate(
+        [norm1_gain, norm1_shift, out_bias, norm2_gain, norm2_shift, down_bias], axis=0
+    )
+    vectors = reorder(vectors, to_slots)
+    gain_one, shift_one, bias_out, gain_two, shift_two, bias_down = [
+        vectors[i * layer_total : (i + 1) * layer_total] for i in range(6)
+    ]
+
+    def rows_back(values):
+        slots_out = contract_rows(place_table, reorder(values, from_slots)).astype(BF16)
+        come = lax.all_to_all(slots_out, "dp", split_axis=0, concat_axis=0, tiled=True)
+        return slots_out, come
+
     saved = []
     for l in range(layer_total):
-        if l < last:
-            query_rows = tensor_rows(after(query_weight[l + 1], out_rows))
+        if 0 < l < last:
+            query_rows = tensor_rows(after(query_payload(l + 1), out_rows))
             out_rows = tensor_rows(after(out_turned[l + 1], query_rows))
         normed = layer_norm(stream, gain_one[l], shift_one[l]).astype(BF16)
         projected = product(normed, w_query)
         pair_bias = jnp.concatenate([jnp.zeros((HEAD,), F32), value_bias[l]])
         pair_own = (projected[:, width:] + pair_bias).astype(BF16)
-        queries = (projected[:, :width] + bias_slots[l]).astype(BF16)
-        pair_all = jnp.concatenate(tensor_slots(pair_own))
+        queries = (projected[:, :width] + bias_full).astype(BF16)
+        pair_all = tensor_swap(jnp.concatenate([pair_own] * tensor_count))
         pair_t = pair_all.T
+        if l == 0:
+            w_out = out_gather.settle(projected).finish(projected)
+            queries = after(queries, *arrays_of(*w_out)[:2])
+            ff_gather = Gather([up_weight[0]], [down_turned[0]]).send(pair_all)
         mixed, log_totals = attend(
             queries, pair_all[:, :HEAD], pair_t[HEAD:], score_bias, score_scale
         )
-        w_up, w_down = ff_gather.settle(mixed).finish(mixed)
+        if l > 0:
+            mixed = after(mixed, *ff_gather.come)
+            w_up, w_down = ff_gather.settle(mixed).finish(mixed)
         hidden_state = stream + product_turned(mixed, w_out) + bias_out[l]
         normed_two = layer_norm(hidden_state, gain_two[l], shift_two[l]).astype(BF16)
+        if l == 0:
+            normed_two = after(normed_two, *ff_gather.come)
+            w_up, w_down = ff_gather.settle(normed_two).finish(normed_two)
+        if l == 0 and last > 0:
+            normed_two = after(normed_two, branch_early)
         normed_two_all = tensor_rows(normed_two)
         normed_two_all = after(normed_two_all, *arrays_of(w_up, w_down))
         if l == last:
@@ -617,16 +726,21 @@
             )
         )
         if l < last:
-            attn_gather = Gather([columns(query_rows, kv_full[l + 1])], [columns(out_rows)])
+            query_each, kv_full, bias_full = query_parts(query_rows)
+            attn_gather = Gather(
+                [jnp.concatenate(query_each + [kv_full], axis=1)], [columns(out_rows)]
+            )
             attn_gather.send(normed_two_all)
             down_part = times_turned(activation, w_down, BF16)
+            down_part = after(down_part, *attn_gather.come)
             down_sum = tensor_sum(down_part)
+            ff_gather = Gather([up_weight[l + 1]], [down_turned[l + 1]]).send(down_sum)
             w_query, w_out = [[parts] for parts in attn_gather.settle(down_part).finish(down_part)]
+            if l == last - 1:
+                sent = after(last_branch[early_rows:], w_query[0][0][0], w_out[0][0][0])
+                branch_all = branch_whole(branch_early, tensor_rows(sent))
             down_sum = after(down_sum, *arrays_of(*w_query, *w_out))
-            if l == last - 1:
-                branch_all = tensor_rows(after(last_branch, down_sum))
             stream = hidden_state + down_sum.astype(F32) + bias_down[l]
-            ff_gather = Gather([up_weight[l + 1]], [down_turned[l + 1]]).send(down_sum)
 
     reduced = [None] * layer_total
     vector_grads = [None] * layer_total
@@ -653,39 +767,62 @@
             w_down,
         ) = saved[l]
         branch_grad = tangent.astype(BF16)
+        if l == last - 1:
+            branch_grad, final_sum = lax.optimization_barrier((branch_grad, final_sum))
         if l < last:
             branch_all = tensor_rows(branch_grad)
             above, both_above, normed_above, attn_above, mixed_above, ff_scatter = later
             ff_scatter.settle(branch_grad).send()
-            both_late, attn_late = after((both_above, attn_above), branch_grad)
+            both_late, attn_late = after((both_above, attn_above), branch_grad, *ff_scatter.now())
             attn_scatter = Scatter(
-                [gradient_half(normed_above, both_late)], [gradient_half(attn_late, mixed_above)]
+                [gradient_half(normed_above, both_late, True)],
+                [gradient_half(attn_late, mixed_above, True)],
             )
             attn_scatter.send()
-            branch_all = after(branch_all, *ff_scatter.now(), *attn_scatter.now())
+            beside = ff_scatter.sent + attn_scatter.sent
+            if above == last:
+                final_sum = after(final_sum, *beside)
+                layer_out = (saved[last][7] + final_sum.astype(F32) + bias_down[last]).astype(BF16)
+                out_slots, out_back = rows_back(layer_out)
+                beside.append(out_slots)
+            branch_all = after(branch_all, *beside)
             pre_grad = times(branch_all, w_down, gelu_back, (pre_gelu,), (BF16,))[0]
         normed_part = times_turned(pre_grad, w_up, BF16)
+        if l < last:
+            normed_part = after(normed_part, *ff_scatter.come, *attn_scatter.come)
         normed_two_grad = tensor_sum(normed_part)
+        beside = []
         if l < last:
+            attn_scatter.settle(normed_part).send()
             up_grad, down_grad = ff_scatter.finish(normed_part)
             reduced[above] = (up_grad, down_grad.T)
-            attn_scatter.settle(normed_part).send()
+            beside += [up_grad, down_grad] + attn_scatter.sent
         pre_late, branch_late = after((pre_grad, branch_all), normed_part)
+        ff_scatter = Scatter(
+            [gradient_half(normed_two_all, pre_late, True)],
+            [gradient_half(branch_late, activation, True)],
+        )
+        ff_scatter.send()
+        beside += ff_scatter.now() + ff_scatter.sent
         down_bias_part = jnp.sum(after(branch_grad, normed_part).astype(F32), axis=0)
         up_bias_grads[l] = jnp.sum(pre_late.astype(F32), axis=0)
-        ff_scatter = Scatter(
-            [gradient_half(normed_two_all, pre_late)], [gradient_half(branch_late, activation)]
-        )
-        ff_scatter.send()
-        beside = ff_scatter.now()
+        beside += [down_bias_part, up_bias_grads[l]]
         if l == last:
-            final_part = times_turned(after(activation, *beside), w_down, BF16)
-            beside = beside + [final_part]
+            final_part = times_turned(after(activation, *ff_scatter.sent), w_down, BF16)
+            beside.append(final_part)
         else:
-            beside = beside + attn_scatter.now()
+            both_whole, out_whole = attn_scatter.finish(*ff_scatter.now())
+            out_stack = stack_columns(out_whole, tensor_count)
+            query_stack = stack_query(both_whole, width, query_cols, pair_cols)
+            beside += [out_stack, query_stack]
         normed_two_grad = after(normed_two_grad, *beside)
         if l == last:
             final_sum = tensor_sum(after(final_part, normed_two_grad))
+        else:
+            out_grad = tensor_sum(after(out_stack, normed_two_grad)).astype(F32).T
+            query_sum = tensor_sum(after(query_stack, normed_two_grad))
+            query_w_grad, kv_grad = split_query(query_sum, depth, pair_cols)
+            reduced[above] = (query_w_grad, kv_grad, out_grad) + reduced[above]
         hidden_part, gain_two_part, shift_two_part = jax.vjp(
             layer_norm, hidden_state, gain_two[l], shift_two[l]
         )[1](normed_two_grad.astype(F32))
@@ -694,13 +831,14 @@
         out_bias_part = jnp.sum(attn_grad.astype(F32), axis=0)
         mixed_grad = product(attn_grad, w_out).astype(BF16)
         if l == 0:
-            ff_scatter.settle(attn_grad).send()
             attn_late = after(attn_grad, mixed_grad)
             out_scatter = Scatter(
                 [gradient_half(attn_late, mixed[:, :split])],
                 [gradient_half(attn_late, mixed[:, split:])],
             ).send()
-            mixed_grad = after(mixed_grad, *ff_scatter.now(), *out_scatter.now())
+            mixed_grad = after(mixed_grad, *out_scatter.sent)
+        elif l == last:
+            mixed_grad = after(mixed_grad, *ff_scatter.come)
         query_grad, pair_part = attend_back(
             queries,
             mixed_grad,
@@ -711,19 +849,23 @@
             log_totals,
             score_scale,
         )
-        pair_grad = pair_part[:local_rows]
-        for k in range(1, tensor_count):
-            piece = pair_part[k * local_rows : (k + 1) * local_rows].astype(BF16)
-            pair_grad = pair_grad + turn(piece, tensor_count - k).astype(F32)
-        pair_grad = pair_grad.astype(BF16)
+        pair_come = tensor_swap(pair_part.astype(BF16))
+        pair_grad = sum(
+            pair_come[k * local_rows : (k + 1) * local_rows].astype(F32)
+            for k in range(tensor_count)
+        ).astype(BF16)
         query_bias_grads[l] = jnp.sum(query_grad.astype(F32), axis=0)
         value_bias_grads[l] = jnp.sum(pair_grad[:, HEAD:].astype(F32), axis=0)
         both_grad = jnp.concatenate([query_grad, pair_grad], axis=1)
-        if l == 0 and last > 0:
-            both_whole, out_whole = attn_scatter.finish(query_grad)
-            out_grad = sum_columns(out_whole, tensor_count).T
-            query_w_grad, kv_grad = sum_query(both_whole, width, query_cols, pair_cols)
-            reduced[above] = (query_w_grad, kv_grad, out_grad) + reduced[above]
+        if l == 0:
+            both_grad = after(both_grad, *ff_scatter.come)
+            both_scatter = Scatter(
+                [gradient_half(normed, both_grad[:, :split])],
+                [gradient_half(normed, both_grad[:, split:])],
+            ).send()
+            out_scatter.settle(*both_scatter.sent).send()
+            ff_scatter.settle(*out_scatter.sent).send()
+            both_grad = after(both_grad, *both_scatter.sent, *out_scatter.sent, *ff_scatter.sent)
         normed_grad = product_turned(both_grad, w_query)
         stream_part, gain_one_part, shift_one_part = jax.vjp(
             layer_norm, stream_in, gain_one[l], shift_one[l]
@@ -738,18 +880,6 @@
             shift_two_part,
             down_bias_part,
         ]
-    out_scatter.settle(both_grad).send()
-    both_scatter = Scatter(
-        [gradient_half(normed, both_grad[:, :split])], [gradient_half(normed, both_grad[:, split:])]
-    ).send()
-    up_grad, down_grad = ff_scatter.finish(both_grad)
-    out_grad = sum_columns(jnp.concatenate(out_scatter.finish(), axis=1), tensor_count).T
-    both_whole = jnp.concatenate(both_scatter.finish(), axis=1)
-    query_w_grad, kv_grad = sum_query(both_whole, width, query_cols, pair_cols)
-    reduced[0] = (query_w_grad, kv_grad, out_grad, up_grad, down_grad.T)
-    final_sum = after(final_sum, normed_two_grad)
-    layer_out = (saved[last][7] + final_sum.astype(F32) + bias_down[last]).astype(BF16)
-
     stacked = jnp.stack([vector_grads[l][m] for m in range(6) for l in range(layer_total)])
     stacked = reorder(stacked, from_slots)
     query_rows = jnp.stack(query_bias_grads)
@@ -757,11 +887,8 @@
     smalls = jnp.concatenate([stacked, query_rows, value_rows], axis=0)
     small_count = smalls.shape[0]
     smalls = jnp.concatenate([smalls, jnp.stack(up_bias_grads)], axis=0)
-    for k in range(dp_count.bit_length() - 1):
-        smalls = smalls + flip(smalls, 1 << k)
-    up_bias_grad = smalls[small_count:]
-    smalls = smalls[:small_count]
-    total = smalls
+    smalls = smalls + flip(smalls, 1)
+    total = smalls[:small_count]
     if tensor_count & (tensor_count - 1) == 0:
         for k in range(tensor_count.bit_length() - 1):
             total = total + lax.ppermute(
@@ -769,16 +896,29 @@
             )
     else:
         total = lax.psum(total, "tensor")
+    total = jnp.concatenate([total, smalls[small_count:]], axis=0)
+    for bit in plane_bits():
+        total = total + flip(total, bit)
+    up_bias_grad = total[small_count:]
     vector_sums = [total[m * layer_total : (m + 1) * layer_total] for m in range(8)]
     query_bias_grad = lax.dynamic_slice_in_dim(
         vector_sums[6], tensor_rank * query_cols, query_cols, 1
     )
     value_bias_grad = vector_sums[7][:, :HEAD]
 
-    out_slots = contract_rows(place_table, reorder(layer_out, from_slots)).astype(BF16)
-    grad_slots = contract_rows(place_table, reorder(tangent.astype(BF16), from_slots)).astype(BF16)
-    out_back = lax.all_to_all(out_slots, "dp", split_axis=0, concat_axis=0, tiled=True)
-    grad_back = lax.all_to_all(grad_slots, "dp", split_axis=0, concat_axis=0, tiled=True)
+    grad_back = rows_back(tangent.astype(BF16))[1]
+    out_back = after(out_back, tangent)
+    both_scatter.settle(normed_grad).send()
+    out_whole = jnp.concatenate(out_scatter.finish(), axis=1)
+    out_grad = tensor_sum(stack_columns(out_whole, tensor_count)).astype(F32).T
+    both_whole = jnp.concatenate(both_scatter.finish(), axis=1)
+    query_stack = stack_query(both_whole, width, query_cols, pair_cols)
+    query_w_grad, kv_grad = split_query(tensor_sum(query_stack), depth, pair_cols)
+    up_grad, down_grad = ff_scatter.finish()
+    reduced[0] = (query_w_grad, kv_grad, out_grad, up_grad, down_grad.T)
+    if last == 0:
+        layer_out = (saved[last][7] + final_sum.astype(F32) + bias_down[last]).astype(BF16)
+        out_back = rows_back(layer_out)[1]
     layer_rows = contract_rows(send_table, out_back).astype(BF16)
     token_rows = contract_rows(send_table, grad_back).astype(BF16)
     summed = [jnp.stack([reduced[l][m] for l in range(layer_total)]) for m in range(5)]

time: 1260 us -> 1150 us (0.913)
  waiting for transfers between devices: 532 us -> 359 us
  Pallas kernels: 248 us -> 393 us
  matrix products: 114 us -> 27.7 us
  starting transfers between devices: 105 us -> 86.8 us
  local copies, waits for them, and re-layouts: 105 us -> 122 us
  blocking collectives: 0 us -> 14.2 us
    pallas_call x0 -> x32, Pallas kernels: none -> 145 us  [the longest x12 85.6 us: turned_product(): pl.pallas_call(kernel, grid=(steps,), in_specs=[pl.BlockSpec((rows, tile)...]
    ppermute x73, waiting for transfers between devices: 397 us -> 274 us  [flip(): return lax.ppermute(values, 'dp', [(i, i ^ bit) for i in range(count)])]
    dot_general x24 -> x12, matrix products: 107 us -> 20.3 us  [contract_rows(): lax.dot_general(left, right, (((0,), (0,)), ((), ())), preferred_element_...]
    ppermute x18 -> x0, starting transfers between devices: 32.9 us -> none  [turn(): lax.ppermute(values, 'tensor', [((i + step) % count, i) for i in range(co...]
    ppermute x18 -> x0, waiting for transfers between devices: 30.4 us -> none  [turn(): lax.ppermute(values, 'tensor', [((i + step) % count, i) for i in range(co...]
    all_gather x8, waiting for transfers between devices: 46.4 us -> 22.8 us  [tensor_rows(): return lax.all_gather(values, 'tensor', axis=0, tiled=True)]
    all_to_all x2 -> x5, waiting for transfers between devices: 0.01 us -> 22.5 us  [the longest x3 22.5 us: tensor_swap(): lax.all_to_all(values, 'tensor', split_axis=0, concat_axis=0, tiled=True)]
    convert_element_type x19 -> x9, other arithmetic: 30.5 us -> 9.85 us  [the longest x2 3.46 us: local(): queries = (projected[:, :width] + bias_full).astype(BF16)]
  transfers between devices with their start and end apart: 113 -> 98, of which waited for: 44 -> 42; matrix products, arithmetic and copies ran while one was open for 23% -> 21% of each run, Pallas kernels for 10% -> 30%
where the time goes in v2:
time: 1150 us; the launch traced here: 1140 us
  Pallas kernels  393 us (34%)
  waiting for transfers between devices  359 us (31%)
  local copies, waits for them, and re-layouts  122 us (11%)
  other arithmetic  122 us (11%)
  starting transfers between devices  86.8 us (8%)
  matrix products  27.7 us (2%)
  between operations  16 us (1%)
  blocking collectives  14.2 us (1%)
    ppermute x73, waiting for transfers between devices, flip(): return lax.ppermute(values, 'dp', [(i, i ^ bit) for i in range(count)])  274 us
    pallas_call x10, Pallas kernels, times(): pl.pallas_call(kernel, grid=(columns // tile,), in_specs=[pl.BlockSpec((r...  85.9 us
    pallas_call x12, Pallas kernels, turned_product(): pl.pallas_call(kernel, grid=(steps,), in_specs=[pl.BlockSpec((rows, tile)...  85.6 us
    pallas_call x10, Pallas kernels, times_turned(): pl.pallas_call(kernel, grid=(rows // tile,), in_specs=[pl.BlockSpec((tile...  84.6 us
    pallas_call x20, Pallas kernels, add_blocks(): pl.pallas_call(kernel, grid=(len(keep),), in_specs=[pl.BlockSpec(block, l...  59.4 us
    ppermute x73, starting transfers between devices, flip(): return lax.ppermute(values, 'dp', [(i, i ^ bit) for i in range(count)])  52.6 us
    unnamed x284, local copies, waits for them, and re-layouts  45.9 us
    pallas_call x6, Pallas kernels, reorder(): pl.pallas_call(copy_block, grid_spec=pltpu.PrefetchScalarGridSpec(num_sca...  32.6 us
  transfers between devices with their start and end apart: 98, of which 42 were waited for; matrix products, arithmetic and copies ran while one was open for 21% of the time, Pallas kernels for 30%

profile of v2, /device:TPU:0, one launch (start us, length us, event | category | flops | bytes accessed | tf_op | source)
XLA Modules:
  0.0 1140.6 jit_solution(13099353770428177114)
XLA Ops:
  14.7 5.2 all-to-all-start.1
  21.4 11.1 all-to-all-done.1
  39.5 9.6 all-to-all-done
  59.1 10.9 collective-permute-done.1
  72.3 4.8 reorder.8
  84.5 5.8 reorder.7
  92.7 11.8 %collective-permute-done.2.refs_1_ = bf16[512,1024]{1,0:T(8,128)(2,1)} collective-permute-done((bf16[512,1024]{1,0:T(8,128)(2,1)}, bf16[512,1024]{1,0:T(8,128)(2,1)}, u32[]{:S(2)}, u32[]{:S(2)}) %collective-permute-start.2) | collective-permute-done | bytes 1048608 | tf_op jit(solution)/shard_map/ppermute | solution.py:44
  105.9 5.7 reorder.6
  120.2 4.2 times.10
  124.5 4.8 times.11
  145.1 4.9 all-to-all-start.2
  151.0 8.9 collective-permute-done.11.refs_1_
  167.2 9.9 attend.2
  180.5 4.9 times_turned.11
  185.5 5.0 times_turned.10
  194.3 9.8 collective-permute-done.17
  213.0 43.8 %collective-permute-done.19.refs_1_ = bf16[512,2048]{1,0:T(8,128)(2,1)} collective-permute-done((bf16[512,2048]{1,0:T(8,128)(2,1)}, bf16[512,2048]{1,0:T(8,128)(2,1)}, u32[]{:S(2)}, u32[]{:S(2)}) %collective-permute-start.19) | collective-permute-done | bytes 2097184 | tf_op jit(solution)/shard_map/ppermute | solution.py:44
  276.3 13.4 %times.12 = (f32[768,2048]{1,0:T(8,128)}, bf16[768,2048]{1,0:T(8,128)(2,1)}) custom-call(bf16[768,2048]{1,0:T(8,128)(2,1)} %all-gather.15.cloned.1.call-done.left_ref, bf16[512,2048]{1,0:T(8,128)(2,1)} %pad_maximum_fusion.5.refs_0_, bf16[512,2048]{1,0:T(8,128)(2,1)} %collective-permute-done.18.refs_1_, bf16[512,2048]{1,0:T(8,128)(2,1)} %collective-permute-done.20.refs_2_, ...), custom_call_target="tpu_custom_call" | custom-call | flops 1 | bytes 1 | tf_op jit(solution)/shard_map/times/pallas_call | solution.py:294
  289.7 11.9 %times_turned.12 = bf16[768,2048]{1,0:T(8,128)(2,1)} custom-call(bf16[768,2048]{1,0:T(8,128)(2,1)} %get-tuple-element.167.left_ref.right_ref, bf16[512,2048]{1,0:T(8,128)(2,1)} %pad_maximum_fusion.6.refs_0_, bf16[512,2048]{1,0:T(8,128)(2,1)} %collective-permute-done.19.refs_1_, bf16[512,2048]{1,0:T(8,128)(2,1)} %collective-permute-done.22.refs_2_, ...), custom_call_target="tpu_custom_call" | custom-call | flops 1 | bytes 1 | tf_op jit(solution)/shard_map/times_turned/pallas_call | solution.py:327
  309.3 45.8 %collective-permute-done.27.refs_1_ = bf16[512,2048]{1,0:T(8,128)(2,1)} collective-permute-done((bf16[512,2048]{1,0:T(8,128)(2,1)}, bf16[512,2048]{1,0:T(8,128)(2,1)}, u32[]{:S(2)}, u32[]{:S(2)}) %collective-permute-start.27) | collective-permute-done | bytes 2097184 | tf_op jit(solution)/shard_map/ppermute | solution.py:44
  363.8 5.1 collective-permute-done.30.refs_2_
  375.8 7.0 times.13
  384.7 4.9 all-to-all-start.3
  391.9 9.5 all-to-all-done.3
  403.1 9.9 attend.3
  413.0 7.9 times_turned.13
  439.1 38.3 %collective-permute-done.35.refs_1_ = bf16[512,2048]{1,0:T(8,128)(2,1)} collective-permute-done((bf16[512,2048]{1,0:T(8,128)(2,1)}, bf16[512,2048]{1,0:T(8,128)(2,1)}, u32[]{:S(2)}, u32[]{:S(2)}) %collective-permute-start.35) | collective-permute-done | bytes 2097184 | tf_op jit(solution)/shard_map/ppermute | solution.py:44
  492.1 11.7 %times.14.refs_5_ = f32[768,2048]{1,0:T(8,128)} custom-call(bf16[768,2048]{1,0:T(8,128)(2,1)} %slice_dynamic-update-slice_fusion.left_ref, bf16[512,2048]{1,0:T(8,128)(2,1)} %pad_maximum_fusion.9.refs_0_, bf16[512,2048]{1,0:T(8,128)(2,1)} %collective-permute-done.35.refs_1_, bf16[512,2048]{1,0:T(8,128)(2,1)} %collective-permute-done.38.refs_2_, ...), custom_call_target="tpu_custom_call" | custom-call | flops 1 | bytes 1 | tf_op jit(solution)/shard_map/times/pallas_call | solution.py:294
  503.8 15.6 %times.15 = (bf16[768,2048]{1,0:T(8,128)(2,1)}, bf16[768,2048]{1,0:T(8,128)(2,1)}) custom-call(bf16[768,2048]{1,0:T(8,128)(2,1)} %all-gather.19.cloned.1.call-done.left_ref, bf16[512,2048]{1,0:T(8,128)(2,1)} %pad_maximum_fusion.8.refs_0_, bf16[512,2048]{1,0:T(8,128)(2,1)} %collective-permute-done.34.refs_1_, ...), custom_call_target="tpu_custom_call" | custom-call | flops 1 | bytes 1 | tf_op jit(solution)/shard_map/times/pallas_call | solution.py:294
  519.4 11.9 %times_turned.14 = bf16[768,2048]{1,0:T(8,128)(2,1)} custom-call(bf16[768,2048]{1,0:T(8,128)(2,1)} %get-tuple-element.197.left_ref.right_ref, bf16[512,2048]{1,0:T(8,128)(2,1)} %pad_maximum_fusion.8.refs_0_, bf16[512,2048]{1,0:T(8,128)(2,1)} %collective-permute-done.34.refs_1_, bf16[512,2048]{1,0:T(8,128)(2,1)} %collective-permute-done.36.refs_2_, ...), custom_call_target="tpu_custom_call" | custom-call | flops 1 | bytes 1 | tf_op jit(solution)/shard_map/times_turned/pallas_call | solution.py:327
  531.6 7.5 turned_product.12
  539.2 7.4 turned_product.14
  551.8 8.3 turned_product.13.half_ref
  560.1 8.3 turned_product.15.half_ref
  573.4 11.9 %times_turned.15 = bf16[768,2048]{1,0:T(8,128)(2,1)} custom-call(bf16[768,2048]{1,0:T(8,128)(2,1)} %get-tuple-element.201.right_ref.left_ref, bf16[512,2048]{1,0:T(8,128)(2,1)} %pad_maximum_fusion.9.refs_0_, bf16[512,2048]{1,0:T(8,128)(2,1)} %collective-permute-done.35.refs_1_, bf16[512,2048]{1,0:T(8,128)(2,1)} %collective-permute-done.38.refs_2_, ...), custom_call_target="tpu_custom_call" | custom-call | flops 1 | bytes 1 | tf_op jit(solution)/shard_map/times_turned/pallas_call | solution.py:327
  585.3 4.6 reduce-scatter.11.cloned.1.call-done
  597.8 6.9 times.16
  607.1 30.5 %collective-permute-done.42.come_ref = bf16[512,2048]{1,0:T(8,128)(2,1)} collective-permute-done((bf16[512,2048]{1,0:T(8,128)(2,1)}, bf16[512,2048]{1,0:T(8,128)(2,1)}, u32[]{:S(2)}, u32[]{:S(2)}) %collective-permute-start.42) | collective-permute-done | bytes 2097184 | tf_op jit(solution)/shard_map/ppermute | solution.py:44
  638.8 12.7 %attend_back.2 = (bf16[192,2048]{1,0:T(8,128)(2,1)}, f32[768,256]{1,0:T(8,128)}) custom-call(bf16[192,2048]{1,0:T(8,128)(2,1)} %fusion.11.refs_0_, bf16[192,2048]{1,0:T(8,128)(2,1)} %convert_element_type.433.refs_1_, bf16[768,128]{1,0:T(8,128)(2,1)} %get-tuple-element.408.refs_1_.refs_2_, bf16[768,128]{1,0:T(8,128)(2,1)} %get-tuple-element.407.refs_3_, ...), custom_call_target="tpu_custom_call" | custom-call | flops 1 | bytes 1 | tf_op jit(solution)/shard_map/attend_back/pallas_call | solution.py:479
  652.7 14.2 %all_to_all.90 = bf16[4,192,256]{2,1,0:T(8,128)(2,1)S(1)} all-to-all(bf16[4,192,256]{2,1,0:T(8,128)(2,1)S(1)} %bitcast.132), channel_id=1, replica_groups=mesh['dp'=8,'tensor'=4] {'tensor'}, dimensions={0} | all-to-all | bytes 786432 | tf_op jit(solution)/shard_map/all_to_all | solution.py:343
  668.6 8.4 times_turned.16
  690.0 5.2 turned_product.16
  695.3 5.0 turned_product.18
  703.5 6.5 turned_product.17.half_ref
  714.0 5.9 turned_product.19.half_ref
  731.5 5.9 reorder.9
  739.8 22.8 %all-gather.23.cloned.1.call-done.left_ref = bf16[768,2048]{1,0:T(8,128)(2,1)} async-done(((bf16[192,2048]{1,0:T(8,128)(2,1)}), bf16[768,2048]{1,0:T(8,128)(2,1)}) %all-gather.23.cloned.1.call-update) | async-done | bytes 3145744 | tf_op jit(solution)/shard_map/all_gather | solution.py:347
  762.7 14.2 %times.17.left_ref.right_ref = bf16[768,2048]{1,0:T(8,128)(2,1)} custom-call(bf16[768,2048]{1,0:T(8,128)(2,1)} %all-gather.23.cloned.1.call-done.left_ref, bf16[512,2048]{1,0:T(8,128)(2,1)} %pad_maximum_fusion.6.refs_0_, bf16[512,2048]{1,0:T(8,128)(2,1)} %collective-permute-done.19.refs_1_, bf16[512,2048]{1,0:T(8,128)(2,1)} %collective-permute-done.22.refs_2_, ...), custom_call_target="tpu_custom_call" | custom-call | flops 1 | bytes 1 | tf_op jit(solution)/shard_map/times/pallas_call | solution.py:294
  776.8 11.9 %times_turned.17 = bf16[768,2048]{1,0:T(8,128)(2,1)} custom-call(bf16[768,2048]{1,0:T(8,128)(2,1)} %times.17.left_ref.right_ref, bf16[512,2048]{1,0:T(8,128)(2,1)} %pad_maximum_fusion.5.refs_0_, bf16[512,2048]{1,0:T(8,128)(2,1)} %collective-permute-done.18.refs_1_, bf16[512,2048]{1,0:T(8,128)(2,1)} %collective-permute-done.20.refs_2_, ...), custom_call_target="tpu_custom_call" | custom-call | flops 1 | bytes 1 | tf_op jit(solution)/shard_map/times_turned/pallas_call | solution.py:327
  793.5 7.4 turned_product.20
  800.9 7.4 turned_product.22
  832.3 8.3 turned_product.21.half_ref
  840.6 8.4 turned_product.23.half_ref
  898.8 12.6 %attend_back.3 = (bf16[192,2048]{1,0:T(8,128)(2,1)}, f32[768,256]{1,0:T(8,128)}) custom-call(bf16[192,2048]{1,0:T(8,128)(2,1)} %fusion.8.refs_0_, bf16[192,2048]{1,0:T(8,128)(2,1)} %pad_maximum_fusion.25.refs_1_, bf16[768,128]{1,0:T(8,128)(2,1)} %get-tuple-element.404.refs_1_.refs_2_, bf16[768,128]{1,0:T(8,128)(2,1)} %get-tuple-element.403.refs_3_, ...), custom_call_target="tpu_custom_call" | custom-call | flops 1 | bytes 1 | tf_op jit(solution)/shard_map/attend_back/pallas_call | solution.py:479
  917.6 13.0 %all-to-all-done.6 = bf16[4,192,256]{2,1,0:T(8,128)(2,1)S(1)} async-done(((bf16[4,192,256]{2,1,0:T(8,128)(2,1)}), bf16[4,192,256]{2,1,0:T(8,128)(2,1)S(1)}, u32[]{:S(2)}, u32[]{:S(2)}) %all-to-all-start.6) | async-done | bytes 393248 | tf_op jit(solution)/shard_map/all_to_all | solution.py:343
  930.8 7.7 collective-permute-done.56.come_ref
  944.1 4.4 all-to-all-start.5
  965.6 17.5 %collective-permute-done.60.come_ref = bf16[512,1024]{1,0:T(8,128)(2,1)} collective-permute-done((bf16[512,1024]{1,0:T(8,128)(2,1)}, bf16[512,1024]{1,0:T(8,128)(2,1)}, u32[]{:S(2)}, u32[]{:S(2)}) %collective-permute-start.60) | collective-permute-done | bytes 1048608 | tf_op jit(solution)/shard_map/ppermute | solution.py:44
  1006.2 5.0 times_turned.18
  1011.2 5.8 times_turned.19
  1025.3 4.8 reorder.11
  1035.0 5.7 reorder.10
  1066.6 10.8 collective-permute-done.64
  1118.0 5.5 copy.76
  (737 shorter events, 448.4 us)
Async XLA Ops:
  7.2 41.9 %all-gather.9.cloned.1.call-start = ((), (), s32[]{:S(2)}) async-start(), calls=%async_computation.16 | async-start | bytes 1556480 | tf_op jit(solution)/shard_map/all_gather | solution.py:347
  14.7 17.8 %all-to-all-start.1 = ((bf16[8,24,2048]{2,1,0:T(8,128)(2,1)}), bf16[8,24,2048]{2,1,0:T(8,128)(2,1)S(1)}, u32[]{:S(2)}, u32[]{:S(2)}) async-start(bf16[8,24,2048]{2,1,0:T(8,128)(2,1)} %bitcast.6), calls=%async_computation.1 | async-start | bytes 1572864 | tf_op jit(solution)/shard_map/all_to_all | solution.py:554
  36.0 78.2 %all-gather.11.cloned.1.call-start = ((), (), s32[]{:S(2)}) async-start(), calls=%async_computation.17 | async-start | bytes 1310720 | tf_op jit(solution)/shard_map/all_gather | solution.py:347
  70.1 34.4 %collective-permute-start.3 = (bf16[512,1280]{1,0:T(8,128)(2,1)S(1)}, bf16[512,1280]{1,0:T(8,128)(2,1)S(1)}, u32[]{:S(2)}, u32[]{:S(2)}) collective-permute-start(bf16[512,1280]{1,0:T(8,128)(2,1)S(1)} %pad_maximum_fusion.12.refs_0_), channel_id=1, source_target_pairs={{0,8},{4,12},{8,0},{12,4},{16,24},{20,28},{24,16},{28,20},{1,9},{5... | collective-permute-start | bytes 3932168 | tf_op jit(solution)/shard_map/ppermute | solution.py:44
  78.0 126.2 %all-gather.13.cloned.1.call-start = ((), (), s32[]{:S(2)}) async-start(), calls=%async_computation.18 | async-start | bytes 1966080 | tf_op jit(solution)/shard_map/all_gather | solution.py:347
  80.2 24.3 %collective-permute-start.2 = (bf16[512,1024]{1,0:T(8,128)(2,1)}, bf16[512,1024]{1,0:T(8,128)(2,1)}, u32[]{:S(2)}, u32[]{:S(2)}) collective-permute-start(bf16[512,1024]{1,0:T(8,128)(2,1)} %pad_maximum_fusion.14.refs_0_), channel_id=1, source_target_pairs={{0,16},{4,20},{8,24},{12,28},{16,0},{20,4},{24,8},{28,12},{1,17},{... | collective-permute-start | bytes 3145736 | tf_op jit(solution)/shard_map/ppermute | solution.py:44
  113.0 145.9 %all-gather.17.cloned.1.call-start = ((), (), s32[]{:S(2)}) async-start(), calls=%async_computation.20 | async-start | bytes 2867200 | tf_op jit(solution)/shard_map/all_gather | solution.py:347
  135.2 24.7 %collective-permute-start.11 = (bf16[512,1024]{1,0:T(8,128)(2,1)S(1)}, bf16[512,1024]{1,0:T(8,128)(2,1)}, u32[]{:S(2)}, u32[]{:S(2)}) collective-permute-start(bf16[512,1024]{1,0:T(8,128)(2,1)S(1)} %pad_maximum_fusion.16.refs_0_), channel_id=1, source_target_pairs={{0,8},{4,12},{8,0},{12,4},{16,24},{20,28},{24,16},{28,20},{1,9},{5... | collective-permute-start | bytes 3145736 | tf_op jit(solution)/shard_map/ppermute | solution.py:44
  136.6 24.6 %collective-permute-start.10 = (bf16[512,1024]{1,0:T(8,128)(2,1)}, bf16[512,1024]{1,0:T(8,128)(2,1)}, u32[]{:S(2)}, u32[]{:S(2)}) collective-permute-start(bf16[512,1024]{1,0:T(8,128)(2,1)} %pad_maximum_fusion.15.refs_0_), channel_id=1, source_target_pairs={{0,16},{4,20},{8,24},{12,28},{16,0},{20,4},{24,8},{28,12},{1,17},{... | collective-permute-start | bytes 3145736 | tf_op jit(solution)/shard_map/ppermute | solution.py:44
  145.1 19.6 %all-to-all-start.2 = ((bf16[4,192,256]{2,1,0:T(8,128)(2,1)}), bf16[4,192,256]{2,1,0:T(8,128)(2,1)S(1)}, u32[]{:S(2)}, u32[]{:S(2)}) async-start(bf16[4,192,256]{2,1,0:T(8,128)(2,1)} %bitcast.18), calls=%async_computation.2 | async-start | bytes 786432 | tf_op jit(solution)/shard_map/all_to_all | solution.py:343
  149.9 121.4 %all-gather.15.cloned.1.call-start = ((), (), s32[]{:S(2)}) async-start(), calls=%async_computation.19 | async-start | bytes 3932160 | tf_op jit(solution)/shard_map/all_gather | solution.py:347
  161.2 24.2 %collective-permute-start.12 = (bf16[512,1024]{1,0:T(8,128)(2,1)}, bf16[512,1024]{1,0:T(8,128)(2,1)}, u32[]{:S(2)}, u32[]{:S(2)}) collective-permute-start(bf16[512,1024]{1,0:T(8,128)(2,1)} %pad_maximum_fusion.15.refs_0_), channel_id=1, source_target_pairs={{0,4},{4,0},{8,12},{12,8},{16,20},{20,16},{24,28},{28,24},{1,5},{5... | collective-permute-start | bytes 3145736 | tf_op jit(solution)/shard_map/ppermute | solution.py:44
  161.2 24.2 %collective-permute-start.13 = (bf16[512,1024]{1,0:T(8,128)(2,1)}, bf16[512,1024]{1,0:T(8,128)(2,1)}, u32[]{:S(2)}, u32[]{:S(2)}) collective-permute-start(bf16[512,1024]{1,0:T(8,128)(2,1)} %collective-permute-done.10.refs_1_), channel_id=1, source_target_pairs={{0,4},{4,0},{8,12},{12,8},{16,20},{20,16},{24,28},{28,24},{1,5},{5... | collective-permute-start | bytes 3145736 | tf_op jit(solution)/shard_map/ppermute | solution.py:44
  161.8 18.8 %collective-permute-start.15 = (bf16[512,1024]{1,0:T(8,128)(2,1)}, bf16[512,1024]{1,0:T(8,128)(2,1)}, u32[]{:S(2)}, u32[]{:S(2)}) collective-permute-start(bf16[512,1024]{1,0:T(8,128)(2,1)} %collective-permute-done.11.refs_1_), channel_id=1, source_target_pairs={{0,4},{4,0},{8,12},{12,8},{16,20},{20,16},{24,28},{28,24},{1,5},{5... | collective-permute-start | bytes 3145736 | tf_op jit(solution)/shard_map/ppermute | solution.py:44
  164.9 29.5 %collective-permute-start.16 = (bf16[256,2048]{1,0:T(8,128)(2,1)}, bf16[256,2048]{1,0:T(8,128)(2,1)}, u32[]{:S(2)}, u32[]{:S(2)}) collective-permute-start(bf16[256,2048]{1,0:T(8,128)(2,1)} %get-tuple-element.154), channel_id=1, source_target_pairs={{0,8},{4,12},{8,0},{12,4},{16,24},{20,28},{24,16},{28,20},{1,9},{5... | collective-permute-start | bytes 3145736 | tf_op jit(solution)/shard_map/ppermute | solution.py:44
  179.1 25.1 %collective-permute-start.17 = (bf16[256,2048]{1,0:T(8,128)(2,1)}, bf16[256,2048]{1,0:T(8,128)(2,1)}, u32[]{:S(2)}, u32[]{:S(2)}) collective-permute-start(bf16[256,2048]{1,0:T(8,128)(2,1)} %bitcast.26), channel_id=1, source_target_pairs={{0,16},{4,20},{8,24},{12,28},{16,0},{20,4},{24,8},{28,12},{1,17},{... | collective-permute-start | bytes 3145736 | tf_op jit(solution)/shard_map/ppermute | solution.py:44
  204.2 158.1 %reduce-scatter.9.cloned.1.call-start = ((), (), s32[]{:S(2)}) async-start(), calls=%async_computation.21 | async-start | bytes 3932160 | tf_op jit(solution)/shard_map/reduce_scatter | solution.py:351
  210.2 46.6 %collective-permute-start.19 = (bf16[512,2048]{1,0:T(8,128)(2,1)}, bf16[512,2048]{1,0:T(8,128)(2,1)}, u32[]{:S(2)}, u32[]{:S(2)}) collective-permute-start(bf16[512,2048]{1,0:T(8,128)(2,1)} %pad_maximum_fusion.6.refs_0_), channel_id=1, source_target_pairs={{0,8},{4,12},{8,0},{12,4},{16,24},{20,28},{24,16},{28,20},{1,9},{5... | collective-permute-start | bytes 6291464 | tf_op jit(solution)/shard_map/ppermute | solution.py:44
  211.5 46.4 %collective-permute-start.18 = (bf16[512,2048]{1,0:T(8,128)(2,1)}, bf16[512,2048]{1,0:T(8,128)(2,1)}, u32[]{:S(2)}, u32[]{:S(2)}) collective-permute-start(bf16[512,2048]{1,0:T(8,128)(2,1)} %pad_maximum_fusion.5.refs_0_), channel_id=1, source_target_pairs={{0,16},{4,20},{8,24},{12,28},{16,0},{20,4},{24,8},{28,12},{1,17},{... | collective-permute-start | bytes 6291464 | tf_op jit(solution)/shard_map/ppermute | solution.py:44
  271.4 30.2 %collective-permute-start.24 = (bf16[256,2304]{1,0:T(8,128)(2,1)S(1)}, bf16[256,2304]{1,0:T(8,128)(2,1)}, u32[]{:S(2)}, u32[]{:S(2)}) collective-permute-start(bf16[256,2304]{1,0:T(8,128)(2,1)S(1)} %concatenate.153), channel_id=1, source_target_pairs={{0,8},{4,12},{8,0},{12,4},{16,24},{20,28},{24,16},{28,20},{1,9},{5... | collective-permute-start | bytes 3538952 | tf_op jit(solution)/shard_map/ppermute | solution.py:44
  274.2 27.4 %collective-permute-start.25 = (bf16[256,2048]{1,0:T(8,128)(2,1)}, bf16[256,2048]{1,0:T(8,128)(2,1)}, u32[]{:S(2)}, u32[]{:S(2)}) collective-permute-start(bf16[256,2048]{1,0:T(8,128)(2,1)} %pad_maximum_fusion.17), channel_id=1, source_target_pairs={{0,16},{4,20},{8,24},{12,28},{16,0},{20,4},{24,8},{28,12},{1,17},{... | collective-permute-start | bytes 3145736 | tf_op jit(solution)/shard_map/ppermute | solution.py:44
  304.6 53.0 %collective-permute-start.26 = (bf16[512,2304]{1,0:T(8,128)(2,1)}, bf16[512,2304]{1,0:T(8,128)(2,1)}, u32[]{:S(2)}, u32[]{:S(2)}) collective-permute-start(bf16[512,2304]{1,0:T(8,128)(2,1)} %pad_maximum_fusion.2.refs_0_), channel_id=1, source_target_pairs={{0,16},{4,20},{8,24},{12,28},{16,0},{20,4},{24,8},{28,12},{1,17},{... | collective-permute-start | bytes 7077896 | tf_op jit(solution)/shard_map/ppermute | solution.py:44
  308.0 47.2 %collective-permute-start.27 = (bf16[512,2048]{1,0:T(8,128)(2,1)}, bf16[512,2048]{1,0:T(8,128)(2,1)}, u32[]{:S(2)}, u32[]{:S(2)}) collective-permute-start(bf16[512,2048]{1,0:T(8,128)(2,1)} %pad_maximum_fusion.7.refs_0_), channel_id=1, source_target_pairs={{0,8},{4,12},{8,0},{12,4},{16,24},{20,28},{24,16},{28,20},{1,9},{5... | collective-permute-start | bytes 6291464 | tf_op jit(solution)/shard_map/ppermute | solution.py:44
  362.3 50.7 %collective-permute-start.32 = (bf16[256,2048]{1,0:T(8,128)(2,1)}, bf16[256,2048]{1,0:T(8,128)(2,1)}, u32[]{:S(2)}, u32[]{:S(2)}) collective-permute-start(bf16[256,2048]{1,0:T(8,128)(2,1)} %get-tuple-element.182), channel_id=1, source_target_pairs={{0,8},{4,12},{8,0},{12,4},{16,24},{20,28},{24,16},{28,20},{1,9},{5... | collective-permute-start | bytes 3145736 | tf_op jit(solution)/shard_map/ppermute | solution.py:44
  375.3 37.7 %collective-permute-start.33 = (bf16[256,2048]{1,0:T(8,128)(2,1)S(1)}, bf16[256,2048]{1,0:T(8,128)(2,1)}, u32[]{:S(2)}, u32[]{:S(2)}) collective-permute-start(bf16[256,2048]{1,0:T(8,128)(2,1)S(1)} %bitcast.118), channel_id=1, source_target_pairs={{0,16},{4,20},{8,24},{12,28},{16,0},{20,4},{24,8},{28,12},{1,17},{... | collective-permute-start | bytes 3145736 | tf_op jit(solution)/shard_map/ppermute | solution.py:44
  389.7 45.7 %all-gather.21.cloned.1.call-start = ((), (), s32[]{:S(2)}) async-start(), calls=%async_computation.23 | async-start | bytes 1966080 | tf_op jit(solution)/shard_map/all_gather | solution.py:347
  390.4 113.4 %all-gather.19.cloned.1.call-start = ((), (), s32[]{:S(2)}) async-start(), calls=%async_computation.22 | async-start | bytes 3932160 | tf_op jit(solution)/shard_map/all_gather | solution.py:347
  424.6 165.3 %reduce-scatter.11.cloned.1.call-start = ((), (), s32[]{:S(2)}) async-start(), calls=%async_computation.24 | async-start | bytes 3932160 | tf_op jit(solution)/shard_map/reduce_scatter | solution.py:351
  430.7 46.6 %collective-permute-start.35 = (bf16[512,2048]{1,0:T(8,128)(2,1)}, bf16[512,2048]{1,0:T(8,128)(2,1)}, u32[]{:S(2)}, u32[]{:S(2)}) collective-permute-start(bf16[512,2048]{1,0:T(8,128)(2,1)} %pad_maximum_fusion.9.refs_0_), channel_id=1, source_target_pairs={{0,8},{4,12},{8,0},{12,4},{16,24},{20,28},{24,16},{28,20},{1,9},{5... | collective-permute-start | bytes 6291464 | tf_op jit(solution)/shard_map/ppermute | solution.py:44
  432.2 46.4 %collective-permute-start.34 = (bf16[512,2048]{1,0:T(8,128)(2,1)}, bf16[512,2048]{1,0:T(8,128)(2,1)}, u32[]{:S(2)}, u32[]{:S(2)}) collective-permute-start(bf16[512,2048]{1,0:T(8,128)(2,1)} %pad_maximum_fusion.8.refs_0_), channel_id=1, source_target_pairs={{0,16},{4,20},{8,24},{12,28},{16,0},{20,4},{24,8},{28,12},{1,17},{... | collective-permute-start | bytes 6291464 | tf_op jit(solution)/shard_map/ppermute | solution.py:44
  478.6 25.2 %collective-permute-start.36 = (bf16[512,2048]{1,0:T(8,128)(2,1)}, bf16[512,2048]{1,0:T(8,128)(2,1)}, u32[]{:S(2)}, u32[]{:S(2)}) collective-permute-start(bf16[512,2048]{1,0:T(8,128)(2,1)} %pad_maximum_fusion.8.refs_0_), channel_id=1, source_target_pairs={{0,4},{4,0},{8,12},{12,8},{16,20},{20,16},{24,28},{28,24},{1,5},{5... | collective-permute-start | bytes 6291464 | tf_op jit(solution)/shard_map/ppermute | solution.py:44
  478.6 25.2 %collective-permute-start.37 = (bf16[512,2048]{1,0:T(8,128)(2,1)}, bf16[512,2048]{1,0:T(8,128)(2,1)}, u32[]{:S(2)}, u32[]{:S(2)}) collective-permute-start(bf16[512,2048]{1,0:T(8,128)(2,1)} %collective-permute-done.34.refs_1_), channel_id=1, source_target_pairs={{0,4},{4,0},{8,12},{12,8},{16,20},{20,16},{24,28},{28,24},{1,5},{5... | collective-permute-start | bytes 6291464 | tf_op jit(solution)/shard_map/ppermute | solution.py:44
  531.3 151.9 %reduce-scatter.13.cloned.1.call-start = ((), (), s32[]{:S(2)}) async-start(), calls=%async_computation.25 | async-start | bytes 3932160 | tf_op jit(solution)/shard_map/reduce_scatter | solution.py:351
  589.9 172.7 %all-gather.23.cloned.1.call-start = ((), (), s32[]{:S(2)}) async-start(), calls=%async_computation.26 | async-start | bytes 3932160 | tf_op jit(solution)/shard_map/all_gather | solution.py:347
  590.0 47.6 %collective-permute-start.42 = (bf16[512,2048]{1,0:T(8,128)(2,1)}, bf16[512,2048]{1,0:T(8,128)(2,1)}, u32[]{:S(2)}, u32[]{:S(2)}) collective-permute-start(bf16[512,2048]{1,0:T(8,128)(2,1)} %pad_maximum_fusion.10), channel_id=1, source_target_pairs={{0,8},{4,12},{8,0},{12,4},{16,24},{20,28},{24,16},{28,20},{1,9},{5... | collective-permute-start | bytes 6291464 | tf_op jit(solution)/shard_map/ppermute | solution.py:44
  591.6 47.2 %collective-permute-start.43 = (bf16[512,2048]{1,0:T(8,128)(2,1)}, bf16[512,2048]{1,0:T(8,128)(2,1)}, u32[]{:S(2)}, u32[]{:S(2)}) collective-permute-start(bf16[512,2048]{1,0:T(8,128)(2,1)} %slice.932), channel_id=1, source_target_pairs={{0,16},{4,20},{8,24},{12,28},{16,0},{20,4},{24,8},{28,12},{1,17},{... | collective-permute-start | bytes 6291464 | tf_op jit(solution)/shard_map/ppermute | solution.py:44
  700.7 170.1 %reduce-scatter.15.cloned.1.call-start = ((), (), s32[]{:S(2)}) async-start(), calls=%async_computation.27 | async-start | bytes 3932160 | tf_op jit(solution)/shard_map/reduce_scatter | solution.py:351
  713.4 80.1 %collective-permute-start.48 = (bf16[512,2304]{1,0:T(8,128)(2,1)}, bf16[512,2304]{1,0:T(8,128)(2,1)}, u32[]{:S(2)}, u32[]{:S(2)}) collective-permute-start(bf16[512,2304]{1,0:T(8,128)(2,1)} %pad_maximum_fusion.3), channel_id=1, source_target_pairs={{0,8},{4,12},{8,0},{12,4},{16,24},{20,28},{24,16},{28,20},{1,9},{5... | collective-permute-start | bytes 7077896 | tf_op jit(solution)/shard_map/ppermute | solution.py:44
  723.3 70.2 %collective-permute-start.49 = (bf16[512,2048]{1,0:T(8,128)(2,1)}, bf16[512,2048]{1,0:T(8,128)(2,1)}, u32[]{:S(2)}, u32[]{:S(2)}) collective-permute-start(bf16[512,2048]{1,0:T(8,128)(2,1)} %slice.943), channel_id=1, source_target_pairs={{0,16},{4,20},{8,24},{12,28},{16,0},{20,4},{24,8},{28,12},{1,17},{... | collective-permute-start | bytes 6291464 | tf_op jit(solution)/shard_map/ppermute | solution.py:44
  727.0 62.4 %collective-permute-start.47 = (bf16[256,2048]{1,0:T(8,128)(2,1)}, bf16[256,2048]{1,0:T(8,128)(2,1)S(1)}, u32[]{:S(2)}, u32[]{:S(2)}) collective-permute-start(bf16[256,2048]{1,0:T(8,128)(2,1)} %slice.940), channel_id=1, source_target_pairs={{0,8},{4,12},{8,0},{12,4},{16,24},{20,28},{24,16},{28,20},{1,9},{5... | collective-permute-start | bytes 3145736 | tf_op jit(solution)/shard_map/ppermute | solution.py:44
  728.4 65.1 %collective-permute-start.46 = (bf16[256,2048]{1,0:T(8,128)(2,1)}, bf16[256,2048]{1,0:T(8,128)(2,1)}, u32[]{:S(2)}, u32[]{:S(2)}) collective-permute-start(bf16[256,2048]{1,0:T(8,128)(2,1)} %slice.939), channel_id=1, source_target_pairs={{0,16},{4,20},{8,24},{12,28},{16,0},{20,4},{24,8},{28,12},{1,17},{... | collective-permute-start | bytes 3145736 | tf_op jit(solution)/shard_map/ppermute | solution.py:44
  800.9 31.4 %collective-permute-start.50 = (bf16[1024,2048]{1,0:T(8,128)(2,1)}, bf16[1024,2048]{1,0:T(8,128)(2,1)}, u32[]{:S(2)}, u32[]{:S(2)}) collective-permute-start(bf16[1024,2048]{1,0:T(8,128)(2,1)} %turned_product.20), channel_id=1, source_target_pairs={{0,4},{4,0},{8,12},{12,8},{16,20},{20,16},{24,28},{28,24},{1,5},{5... | collective-permute-start | bytes 12582920 | tf_op jit(solution)/shard_map/ppermute | solution.py:44
  808.3 32.2 %collective-permute-start.51 = (bf16[1024,2048]{1,0:T(8,128)(2,1)}, bf16[1024,2048]{1,0:T(8,128)(2,1)}, u32[]{:S(2)}, u32[]{:S(2)}) collective-permute-start(bf16[1024,2048]{1,0:T(8,128)(2,1)} %turned_product.22), channel_id=1, source_target_pairs={{0,4},{4,0},{8,12},{12,8},{16,20},{20,16},{24,28},{28,24},{1,5},{5... | collective-permute-start | bytes 12582920 | tf_op jit(solution)/shard_map/ppermute | solution.py:44
  814.9 34.1 %collective-permute-start.53 = (bf16[256,2304]{1,0:T(8,128)(2,1)}, bf16[256,2304]{1,0:T(8,128)(2,1)}, u32[]{:S(2)}, u32[]{:S(2)}) collective-permute-start(bf16[256,2304]{1,0:T(8,128)(2,1)} %slice.945), channel_id=1, source_target_pairs={{0,16},{4,20},{8,24},{12,28},{16,0},{20,4},{24,8},{28,12},{1,17},{... | collective-permute-start | bytes 3538952 | tf_op jit(solution)/shard_map/ppermute | solution.py:44
  822.1 26.9 %collective-permute-start.52 = (bf16[256,2048]{1,0:T(8,128)(2,1)}, bf16[256,2048]{1,0:T(8,128)(2,1)}, u32[]{:S(2)}, u32[]{:S(2)}) collective-permute-start(bf16[256,2048]{1,0:T(8,128)(2,1)} %slice.946), channel_id=1, source_target_pairs={{0,8},{4,12},{8,0},{12,4},{16,24},{20,28},{24,16},{28,20},{1,9},{5... | collective-permute-start | bytes 3145736 | tf_op jit(solution)/shard_map/ppermute | solution.py:44
  890.5 47.9 %collective-permute-start.56 = (bf16[512,2048]{1,0:T(8,128)(2,1)}, bf16[512,2048]{1,0:T(8,128)(2,1)}, u32[]{:S(2)}, u32[]{:S(2)}) collective-permute-start(bf16[512,2048]{1,0:T(8,128)(2,1)} %pad_maximum_fusion.11), channel_id=1, source_target_pairs={{0,8},{4,12},{8,0},{12,4},{16,24},{20,28},{24,16},{28,20},{1,9},{5... | collective-permute-start | bytes 6291464 | tf_op jit(solution)/shard_map/ppermute | solution.py:44
  891.2 47.6 %collective-permute-start.57 = (bf16[512,2048]{1,0:T(8,128)(2,1)}, bf16[512,2048]{1,0:T(8,128)(2,1)}, u32[]{:S(2)}, u32[]{:S(2)}) collective-permute-start(bf16[512,2048]{1,0:T(8,128)(2,1)} %slice.949), channel_id=1, source_target_pairs={{0,16},{4,20},{8,24},{12,28},{16,0},{20,4},{24,8},{28,12},{1,17},{... | collective-permute-start | bytes 6291464 | tf_op jit(solution)/shard_map/ppermute | solution.py:44
  916.8 36.1 %reduce-scatter.19.cloned.1.call-start = ((), (), s32[]{:S(2)}) async-start(), calls=%async_computation.29 | async-start | bytes 1474560 | tf_op jit(solution)/shard_map/reduce_scatter | solution.py:351
  944.1 118.7 %all-to-all-start.5 = ((bf16[8,24,2048]{2,1,0:T(8,128)(2,1)}), bf16[8,24,2048]{2,1,0:T(8,128)(2,1)}, u32[]{:S(2)}, u32[]{:S(2)}) async-start(bf16[8,24,2048]{2,1,0:T(8,128)(2,1)} %bitcast.126), calls=%async_computation.8 | async-start | bytes 1572864 | tf_op jit(solution)/shard_map/all_to_all | solution.py:662
  948.5 179.0 %reduce-scatter.23.cloned.1.call-start = ((), (), s32[]{:S(2)}) async-start(), calls=%async_computation.31 | async-start | bytes 1310720 | tf_op jit(solution)/shard_map/reduce_scatter | solution.py:351
  949.1 178.4 %reduce-scatter.21.cloned.1.call-start = ((), (), s32[]{:S(2)}) async-start(), calls=%async_computation.30 | async-start | bytes 1310720 | tf_op jit(solution)/shard_map/reduce_scatter | solution.py:351
  949.3 33.8 %collective-permute-start.60 = (bf16[512,1024]{1,0:T(8,128)(2,1)}, bf16[512,1024]{1,0:T(8,128)(2,1)}, u32[]{:S(2)}, u32[]{:S(2)}) collective-permute-start(bf16[512,1024]{1,0:T(8,128)(2,1)} %pad_maximum_fusion.19), channel_id=1, source_target_pairs={{0,8},{4,12},{8,0},{12,4},{16,24},{20,28},{24,16},{28,20},{1,9},{5... | collective-permute-start | bytes 3145736 | tf_op jit(solution)/shard_map/ppermute | solution.py:44
  951.3 31.9 %collective-permute-start.61 = (bf16[512,1024]{1,0:T(8,128)(2,1)}, bf16[512,1024]{1,0:T(8,128)(2,1)}, u32[]{:S(2)}, u32[]{:S(2)}) collective-permute-start(bf16[512,1024]{1,0:T(8,128)(2,1)} %slice.964), channel_id=1, source_target_pairs={{0,16},{4,20},{8,24},{12,28},{16,0},{20,4},{24,8},{28,12},{1,17},{... | collective-permute-start | bytes 3145736 | tf_op jit(solution)/shard_map/ppermute | solution.py:44
  959.9 90.9 %collective-permute-start.67 = (bf16[512,1024]{1,0:T(8,128)(2,1)}, bf16[512,1024]{1,0:T(8,128)(2,1)}, u32[]{:S(2)}, u32[]{:S(2)}) collective-permute-start(bf16[512,1024]{1,0:T(8,128)(2,1)} %pad_maximum_fusion.20), channel_id=1, source_target_pairs={{0,8},{4,12},{8,0},{12,4},{16,24},{20,28},{24,16},{28,20},{1,9},{5... | collective-permute-start | bytes 3145736 | tf_op jit(solution)/shard_map/ppermute | solution.py:44
  990.9 51.0 %collective-permute-start.72 = (bf16[256,1024]{1,0:T(8,128)(2,1)}, bf16[256,1024]{1,0:T(8,128)(2,1)}, u32[]{:S(2)}, u32[]{:S(2)}) collective-permute-start(bf16[256,1024]{1,0:T(8,128)(2,1)} %slice.977), channel_id=1, source_target_pairs={{0,8},{4,12},{8,0},{12,4},{16,24},{20,28},{24,16},{28,20},{1,9},{5... | collective-permute-start | bytes 1572872 | tf_op jit(solution)/shard_map/ppermute | solution.py:44
  991.8 51.6 %collective-permute-start.71 = (bf16[256,1024]{1,0:T(8,128)(2,1)}, bf16[256,1024]{1,0:T(8,128)(2,1)}, u32[]{:S(2)}, u32[]{:S(2)}) collective-permute-start(bf16[256,1024]{1,0:T(8,128)(2,1)} %slice.976), channel_id=1, source_target_pairs={{0,16},{4,20},{8,24},{12,28},{16,0},{20,4},{24,8},{28,12},{1,17},{... | collective-permute-start | bytes 1572872 | tf_op jit(solution)/shard_map/ppermute | solution.py:44
  1005.3 45.5 %collective-permute-start.68 = (bf16[512,1280]{1,0:T(8,128)(2,1)}, bf16[512,1280]{1,0:T(8,128)(2,1)}, u32[]{:S(2)}, u32[]{:S(2)}) collective-permute-start(bf16[512,1280]{1,0:T(8,128)(2,1)} %slice.975), channel_id=1, source_target_pairs={{0,16},{4,20},{8,24},{12,28},{16,0},{20,4},{24,8},{28,12},{1,17},{... | collective-permute-start | bytes 3932168 | tf_op jit(solution)/shard_map/ppermute | solution.py:44
  1040.7 67.0 %collective-permute-start.74 = (bf16[256,2048]{1,0:T(8,128)(2,1)}, bf16[256,2048]{1,0:T(8,128)(2,1)}, u32[]{:S(2)}, u32[]{:S(2)}) collective-permute-start(bf16[256,2048]{1,0:T(8,128)(2,1)} %slice.979), channel_id=1, source_target_pairs={{0,8},{4,12},{8,0},{12,4},{16,24},{20,28},{24,16},{28,20},{1,9},{5... | collective-permute-start | bytes 3145736 | tf_op jit(solution)/shard_map/ppermute | solution.py:44
  1041.9 65.8 %collective-permute-start.73 = (bf16[256,2048]{1,0:T(8,128)(2,1)}, bf16[256,2048]{1,0:T(8,128)(2,1)}, u32[]{:S(2)}, u32[]{:S(2)}) collective-permute-start(bf16[256,2048]{1,0:T(8,128)(2,1)} %slice.978), channel_id=1, source_target_pairs={{0,16},{4,20},{8,24},{12,28},{16,0},{20,4},{24,8},{28,12},{1,17},{... | collective-permute-start | bytes 3145736 | tf_op jit(solution)/shard_map/ppermute | solution.py:44
  1058.2 21.3 %collective-permute-start.69 = (bf16[256,1024]{1,0:T(8,128)(2,1)}, bf16[256,1024]{1,0:T(8,128)(2,1)}, u32[]{:S(2)}, u32[]{:S(2)}) collective-permute-start(bf16[256,1024]{1,0:T(8,128)(2,1)} %slice.986), channel_id=1, source_target_pairs={{0,16},{4,20},{8,24},{12,28},{16,0},{20,4},{24,8},{28,12},{1,17},{... | collective-permute-start | bytes 1572872 | tf_op jit(solution)/shard_map/ppermute | solution.py:44
  1058.6 22.3 %collective-permute-start.70 = (bf16[256,1280]{1,0:T(8,128)(2,1)S(1)}, bf16[256,1280]{1,0:T(8,128)(2,1)S(1)}, u32[]{:S(2)}, u32[]{:S(2)}) collective-permute-start(bf16[256,1280]{1,0:T(8,128)(2,1)S(1)} %slice.987), channel_id=1, source_target_pairs={{0,8},{4,12},{8,0},{12,4},{16,24},{20,28},{24,16},{28,20},{1,9},{5... | collective-permute-start | bytes 1966088 | tf_op jit(solution)/shard_map/ppermute | solution.py:44
  1059.6 17.8 %collective-permute-start.64 = (f32[16,2048]{1,0:T(8,128)S(1)}, f32[16,2048]{1,0:T(8,128)S(1)}, u32[]{:S(2)}, u32[]{:S(2)}) collective-permute-start(f32[16,2048]{1,0:T(8,128)S(1)} %slice_add_fusion.3), channel_id=1, source_target_pairs={{0,2},{1,3},{2,0},{3,1},{4,6},{5,7},{6,4},{7,5},{8,10},{9,11},{10,... | collective-permute-start | bytes 393224 | tf_op jit(solution)/shard_map/ppermute | solution.py:894
  1062.8 38.6 %all-to-all-start.7 = ((bf16[8,24,2048]{2,1,0:T(8,128)(2,1)}), bf16[8,24,2048]{2,1,0:T(8,128)(2,1)S(1)}, u32[]{:S(2)}, u32[]{:S(2)}) async-start(bf16[8,24,2048]{2,1,0:T(8,128)(2,1)} %bitcast.56), calls=%async_computation.11 | async-start | bytes 1572864 | tf_op jit(solution)/shard_map/all_to_all | solution.py:662
  1066.3 63.6 %reduce-scatter.17.cloned.1.call-start = ((), (), s32[]{:S(2)}) async-start(), calls=%async_computation.28 | async-start | bytes 1474560 | tf_op jit(solution)/shard_map/reduce_scatter | solution.py:351
  (162 other events, 1656.8 us)
Sparse Core Ops, SparseCore 0:
  12.5 34.2 all-gather.8
  78.1 28.3 all-gather.10
  113.2 37.2 all-gather.12
  151.9 48.2 all-gather.16
  204.3 64.5 all-gather.14
  301.7 60.4 reduce-scatter.8
  392.0 38.3 all-gather.20
  432.6 62.3 all-gather.18
  531.5 58.3 reduce-scatter.10
  592.0 60.2 reduce-scatter.12
  700.9 61.7 all-gather.22
  809.0 59.4 reduce-scatter.14
  920.0 28.8 reduce-scatter.18
  951.3 26.6 reduce-scatter.22
  1050.9 29.7 reduce-scatter.20
  1094.0 27.9 reduce-scatter.16

commit v3 on v2

--- a/solution.py
+++ b/solution.py
@@ -10,13 +10,6 @@
 BF16 = jnp.bfloat16
 F32 = jnp.float32
 LIGHT = pl.CostEstimate(flops=1, transcendentals=0, bytes_accessed=1)
-
-
-def layer_norm(values, scales, offsets):
-    row_mean = jnp.mean(values, axis=-1, keepdims=True)
-    centred = values - row_mean
-    row_var = jnp.mean(centred * centred, axis=-1, keepdims=True)
-    return centred * lax.rsqrt(row_var + EPSILON) * scales + offsets
 
 
 def gelu_tanh(values):
@@ -114,13 +107,8 @@
     def finish(self, *gate):
         while self.taken < len(plane_bits()):
             self.send(*gate)
-        come = tuple(self.come)
         return [
-            parts
-            + [
-                (flip(after(array, *come), 1), [block | 1 for block in blocks])
-                for array, blocks in parts
-            ]
+            parts + [(flip(array, 1), [block | 1 for block in blocks]) for array, blocks in parts]
             for _, parts in self.members
         ]
 
@@ -145,6 +133,43 @@
         cost_estimate=LIGHT,
         name="add_blocks",
     )(half, come)
+
+
+def take_blocks(half, count, keep):
+    rows, columns = half.shape[0] // count, half.shape[1]
+    stride = keep[1] - keep[0] if len(keep) > 1 else 1
+    block = (rows, columns)
+    return pl.pallas_call(
+        lambda half_ref, out_ref: out_ref.__setitem__(..., half_ref[...]),
+        grid=(len(keep),),
+        in_specs=[pl.BlockSpec(block, lambda i: (keep[0] + i * stride, 0))],
+        out_specs=pl.BlockSpec(block, lambda i: (i, 0)),
+        out_shape=jax.ShapeDtypeStruct((len(keep) * rows, columns), half.dtype),
+        cost_estimate=LIGHT,
+        name="take_blocks",
+    )(half)
+
+
+def column_sum(values):
+    rows, columns = values.shape
+    tile = 256 if rows % 256 == 0 else rows
+
+    def kernel(values_ref, out_ref):
+        @pl.when(pl.program_id(0) == 0)
+        def _():
+            out_ref[...] = jnp.zeros_like(out_ref)
+
+        out_ref[...] += jnp.sum(values_ref[...].astype(F32), axis=0, keepdims=True)
+
+    return pl.pallas_call(
+        kernel,
+        grid=(rows // tile,),
+        in_specs=[pl.BlockSpec((tile, columns), lambda i: (i, 0))],
+        out_specs=pl.BlockSpec((1, columns), lambda i: (0, 0)),
+        out_shape=jax.ShapeDtypeStruct((1, columns), F32),
+        cost_estimate=LIGHT,
+        name="column_sum",
+    )(values)[0]
 
 
 class Scatter:
@@ -163,8 +188,8 @@
         self.come = []
         self.sent = []
         for order, half, blocks in self.members:
-            sent = [block for block in blocks if block & order[self.taken]]
-            piece = blocks_of([(half, blocks)], sent)
+            spots = [i for i, block in enumerate(blocks) if block & order[self.taken]]
+            piece = take_blocks(half, len(blocks), spots)
             piece = after(piece, *gate) if gate else piece
             self.sent.append(piece)
             self.come.append(flip(piece, order[self.taken]))
@@ -190,6 +215,14 @@
     def now(self):
         return [half for _, half, _ in self.members]
 
+    def open_sum(self, member):
+        while self.taken < len(plane_bits()):
+            self.settle()
+            self.send()
+        order, half, blocks = self.members[member]
+        spot = next(i for i, block in enumerate(blocks) if not block & order[-1])
+        return half, len(blocks), spot, self.come[member]
+
     def finish(self, *late):
         if self.come:
             self.settle(*late)
@@ -197,6 +230,34 @@
             self.send()
             self.settle(*late)
         return [half.astype(F32) for _, half, _ in self.members]
+
+
+def stack_sums(items, turned):
+    rows, columns = items[0][3].shape
+    shape = (1, columns, rows) if turned else (1, rows, columns)
+
+    def kernel(*refs):
+        for l in range(len(items)):
+
+            @pl.when(pl.program_id(0) == l)
+            def _():
+                total = refs[2 * l][...].astype(F32) + refs[2 * l + 1][...].astype(F32)
+                refs[-1][0] = total.T if turned else total
+
+    specs, arrays = [], []
+    for half, _, spot, come in items:
+        specs.append(pl.BlockSpec((rows, columns), lambda l, spot=spot: (spot, 0)))
+        specs.append(pl.BlockSpec((rows, columns), lambda l: (0, 0)))
+        arrays += [half, come]
+    return pl.pallas_call(
+        kernel,
+        grid=(len(items),),
+        in_specs=specs,
+        out_specs=pl.BlockSpec(shape, lambda l: (l, 0, 0)),
+        out_shape=jax.ShapeDtypeStruct((len(items),) + shape[1:], F32),
+        cost_estimate=LIGHT,
+        name="stack_sums",
+    )(*arrays)
 
 
 def turned_product(features, values, side, extra=None):
@@ -236,12 +297,93 @@
     return near.astype(BF16)
 
 
+def norm_parts(values):
+    centred = values - jnp.mean(values, axis=-1, keepdims=True)
+    return centred, lax.rsqrt(jnp.mean(centred * centred, axis=-1, keepdims=True) + EPSILON)
+
+
+def row_tile(rows):
+    return 64 if rows % 64 == 0 else rows
+
+
+def add_and_norm(base, part, bias, gain, shift):
+    rows, width = base.shape
+    tile = row_tile(rows)
+    wide = pl.BlockSpec((tile, width), lambda i: (i, 0))
+    line = pl.BlockSpec((1, width), lambda i: (0, 0))
+    added = [] if part is None else [part, bias]
+
+    def kernel(gain_ref, shift_ref, base_ref, *refs):
+        total = base_ref[...].astype(F32)
+        if part is not None:
+            total = total + refs[0][...].astype(F32) + refs[1][...]
+        centred, slope = norm_parts(total)
+        refs[-2][...] = total
+        refs[-1][...] = (centred * slope * gain_ref[...] + shift_ref[...]).astype(BF16)
+
+    return pl.pallas_call(
+        kernel,
+        grid=(rows // tile,),
+        in_specs=[line, line, wide] + [wide, line][: len(added)],
+        out_specs=[wide, wide],
+        out_shape=[
+            jax.ShapeDtypeStruct((rows, width), F32),
+            jax.ShapeDtypeStruct((rows, width), BF16),
+        ],
+        cost_estimate=LIGHT,
+        name="add_and_norm",
+    )(gain, shift, base, *added)
+
+
+def norm_back(values, grad, gain, tangent):
+    rows, width = values.shape
+    tile = row_tile(rows)
+    wide = pl.BlockSpec((tile, width), lambda i: (i, 0))
+
+    def kernel(gain_ref, values_ref, grad_ref, tangent_ref, out_ref, low_ref, sums_ref):
+        centred, slope = norm_parts(values_ref[...])
+        scaled = centred * slope
+        grads = grad_ref[...].astype(F32)
+        inner = grads * gain_ref[...]
+        mean_inner = jnp.mean(inner, axis=-1, keepdims=True)
+        mean_scaled = jnp.mean(inner * scaled, axis=-1, keepdims=True)
+        total = tangent_ref[...] + slope * (inner - mean_inner - scaled * mean_scaled)
+        low = total.astype(BF16)
+        out_ref[...] = total
+        low_ref[...] = low
+
+        @pl.when(pl.program_id(0) == 0)
+        def _():
+            sums_ref[...] = jnp.zeros_like(sums_ref)
+
+        for i, term in enumerate((grads * scaled, grads, low.astype(F32))):
+            sums_ref[i : i + 1, :] += jnp.sum(term, axis=0, keepdims=True)
+
+    return pl.pallas_call(
+        kernel,
+        grid=(rows // tile,),
+        in_specs=[pl.BlockSpec((1, width), lambda i: (0, 0)), wide, wide, wide],
+        out_specs=[wide, wide, pl.BlockSpec((8, width), lambda i: (0, 0))],
+        out_shape=[
+            jax.ShapeDtypeStruct((rows, width), F32),
+            jax.ShapeDtypeStruct((rows, width), BF16),
+            jax.ShapeDtypeStruct((8, width), F32),
+        ],
+        cost_estimate=LIGHT,
+        name="norm_back",
+    )(gain, values, grad, tangent)
+
+
 def plain_product(total):
     return (total,)
 
 
 def round_product(total):
     return (total.astype(BF16),)
+
+
+def bias_round(total, bias):
+    return ((total + bias).astype(BF16),)
 
 
 def gelu_both(total, bias):
@@ -397,6 +539,53 @@
     )(table, values)
 
 
+def place_rows(left, values, table):
+    rows, count = values.shape[0], table.shape[0]
+    width = values.shape[1] // (128 * count) * 128
+    if width * count != values.shape[1] // 256 * 256:
+        columns = values.shape[1] // (count * 64) * (count * 64)
+        return matmul(left, reorder(values[:, :columns], table)).astype(BF16)
+
+    def kernel(table_ref, left_ref, source, target):
+        target[...] = matmul(left_ref[...], source[...]).astype(BF16)
+
+    return pl.pallas_call(
+        kernel,
+        grid_spec=pltpu.PrefetchScalarGridSpec(
+            num_scalar_prefetch=1,
+            grid=(count,),
+            in_specs=[
+                pl.BlockSpec((rows, rows), lambda j, table: (0, 0)),
+                pl.BlockSpec((rows, width), lambda j, table: (0, table[j])),
+            ],
+            out_specs=pl.BlockSpec((rows, width), lambda j, table: (0, j)),
+        ),
+        out_shape=jax.ShapeDtypeStruct((rows, width * count), BF16),
+        cost_estimate=LIGHT,
+        name="place_rows",
+    )(table, left, values)
+
+
+def add_rounded(base, part, bias):
+    rows, width = base.shape
+    tile = 64 if rows % 64 == 0 else rows
+    wide = pl.BlockSpec((tile, width), lambda i: (i, 0))
+
+    def kernel(base_ref, part_ref, bias_ref, out_ref):
+        total = base_ref[...] + part_ref[...].astype(F32) + bias_ref[...]
+        out_ref[...] = total.astype(BF16)
+
+    return pl.pallas_call(
+        kernel,
+        grid=(rows // tile,),
+        in_specs=[wide, wide, pl.BlockSpec((1, width), lambda i: (0, 0))],
+        out_specs=wide,
+        out_shape=jax.ShapeDtypeStruct((rows, width), BF16),
+        cost_estimate=LIGHT,
+        name="add_rounded",
+    )(base, part, bias)
+
+
 def stack_heads(block):
     return jnp.concatenate([block[:, :HEAD], block[:, HEAD:]], axis=0)
 
@@ -415,10 +604,9 @@
     log_ref[0] = top + jnp.log(total)
 
 
-def attend(queries, key_rows, value_t, bias, scale):
-    rows, columns = queries.shape
+def attend(queries, columns, key_rows, value_t, bias, scale):
+    rows, keys = queries.shape[0], key_rows.shape[0]
     pairs = columns // (2 * HEAD)
-    keys = key_rows.shape[0]
 
     def kernel(*refs):
         attend_kernel(scale, *refs)
@@ -468,10 +656,9 @@
     grad_ref[:, HEAD:] = query_grad[rows:]
 
 
-def attend_back(queries, douts, key_rows, value_rows, key_t, bias, log_totals, scale):
-    rows, columns = queries.shape
+def attend_back(queries, columns, douts, key_rows, value_rows, key_t, bias, log_totals, scale):
+    rows, keys = queries.shape[0], key_rows.shape[0]
     pairs = columns // (2 * HEAD)
-    keys = key_rows.shape[0]
 
     def kernel(*refs):
         attend_back_kernel(scale, *refs)
@@ -554,8 +741,8 @@
     tangent_come = lax.all_to_all(tangent_sent, "dp", split_axis=0, concat_axis=0, tiled=True)
     arrived_place = tokens_come[:, width].astype(jnp.int32)
     place_table = (row_ids[:, None] == arrived_place[None, :]).astype(BF16)
-    stream = reorder(matmul(place_table, tokens_come[:, :width]).astype(BF16), to_slots).astype(F32)
-    last_branch = reorder(matmul(place_table, tangent_come).astype(BF16), to_slots)
+    stream = place_rows(place_table, tokens_come, to_slots)
+    last_branch = place_rows(place_table, tangent_come, to_slots)
     tangent = last_branch.astype(F32)
     stream = after(stream, last_branch)
 
@@ -568,8 +755,16 @@
     score_bias = jnp.where(allowed, 0.0, -1e30).astype(F32)
     score_bias = jnp.concatenate([score_bias, score_bias], axis=1)
 
-    def product(left, weights):
-        pieces = [times(left, parts, plain_product, (), (F32,))[0] for parts in weights]
+    def product(left, weights, bias=None):
+        pieces, start = [], 0
+        for parts in weights:
+            size = parts[0][0].shape[1]
+            if bias is None:
+                pieces.append(times(left, parts, round_product, (), (BF16,))[0])
+            else:
+                extra = (bias[:, start : start + size],)
+                pieces.append(times(left, parts, bias_round, extra, (BF16,))[0])
+            start += size
         return pieces[0] if len(pieces) == 1 else jnp.concatenate(pieces, axis=1)
 
     def product_turned(left, weights):
@@ -658,7 +853,7 @@
     ]
 
     def rows_back(values):
-        slots_out = contract_rows(place_table, reorder(values, from_slots)).astype(BF16)
+        slots_out = place_rows(place_table.T, values, from_slots)
         come = lax.all_to_all(slots_out, "dp", split_axis=0, concat_axis=0, tiled=True)
         return slots_out, come
 
@@ -667,25 +862,32 @@
         if 0 < l < last:
             query_rows = tensor_rows(after(query_payload(l + 1), out_rows))
             out_rows = tensor_rows(after(out_turned[l + 1], query_rows))
-        normed = layer_norm(stream, gain_one[l], shift_one[l]).astype(BF16)
-        projected = product(normed, w_query)
-        pair_bias = jnp.concatenate([jnp.zeros((HEAD,), F32), value_bias[l]])
-        pair_own = (projected[:, width:] + pair_bias).astype(BF16)
-        queries = (projected[:, :width] + bias_full).astype(BF16)
+        if l == 0:
+            stream, normed = add_and_norm(stream, None, None, gain_one[:1], shift_one[:1])
+        bias = jnp.concatenate([bias_full, jnp.zeros((HEAD,), F32), value_bias[l]])[None]
+        queries = product(normed, w_query, bias)
+        projected = queries
+        pair_own = queries[:, width:]
         pair_all = tensor_swap(jnp.concatenate([pair_own] * tensor_count))
         pair_t = pair_all.T
         if l == 0:
-            w_out = out_gather.settle(projected).finish(projected)
-            queries = after(queries, *arrays_of(*w_out)[:2])
+            out_gather.settle(projected).send(projected)
             ff_gather = Gather([up_weight[0]], [down_turned[0]]).send(pair_all)
         mixed, log_totals = attend(
-            queries, pair_all[:, :HEAD], pair_t[HEAD:], score_bias, score_scale
+            queries, width, pair_all[:, :HEAD], pair_t[HEAD:], score_bias, score_scale
         )
+        if l == 0:
+            w_out = out_gather.settle(mixed).finish(mixed)
         if l > 0:
             mixed = after(mixed, *ff_gather.come)
             w_up, w_down = ff_gather.settle(mixed).finish(mixed)
-        hidden_state = stream + product_turned(mixed, w_out) + bias_out[l]
-        normed_two = layer_norm(hidden_state, gain_two[l], shift_two[l]).astype(BF16)
+        hidden_state, normed_two = add_and_norm(
+            stream,
+            product_turned(mixed, w_out),
+            bias_out[l : l + 1],
+            gain_two[l : l + 1],
+            shift_two[l : l + 1],
+        )
         if l == 0:
             normed_two = after(normed_two, *ff_gather.come)
             w_up, w_down = ff_gather.settle(normed_two).finish(normed_two)
@@ -740,9 +942,16 @@
                 sent = after(last_branch[early_rows:], w_query[0][0][0], w_out[0][0][0])
                 branch_all = branch_whole(branch_early, tensor_rows(sent))
             down_sum = after(down_sum, *arrays_of(*w_query, *w_out))
-            stream = hidden_state + down_sum.astype(F32) + bias_down[l]
+            stream, normed = add_and_norm(
+                hidden_state,
+                down_sum,
+                bias_down[l : l + 1],
+                gain_one[l + 1 : l + 2],
+                shift_one[l + 1 : l + 2],
+            )
 
     reduced = [None] * layer_total
+    ff_open = [None] * layer_total
     vector_grads = [None] * layer_total
     query_bias_grads = [None] * layer_total
     value_bias_grads = [None] * layer_total
@@ -766,9 +975,8 @@
             w_up,
             w_down,
         ) = saved[l]
-        branch_grad = tangent.astype(BF16)
-        if l == last - 1:
-            branch_grad, final_sum = lax.optimization_barrier((branch_grad, final_sum))
+        if l == last:
+            branch_grad = last_branch
         if l < last:
             branch_all = tensor_rows(branch_grad)
             above, both_above, normed_above, attn_above, mixed_above, ff_scatter = later
@@ -782,7 +990,7 @@
             beside = ff_scatter.sent + attn_scatter.sent
             if above == last:
                 final_sum = after(final_sum, *beside)
-                layer_out = (saved[last][7] + final_sum.astype(F32) + bias_down[last]).astype(BF16)
+                layer_out = add_rounded(saved[last][7], final_sum, bias_down[last][None])
                 out_slots, out_back = rows_back(layer_out)
                 beside.append(out_slots)
             branch_all = after(branch_all, *beside)
@@ -794,9 +1002,8 @@
         beside = []
         if l < last:
             attn_scatter.settle(normed_part).send()
-            up_grad, down_grad = ff_scatter.finish(normed_part)
-            reduced[above] = (up_grad, down_grad.T)
-            beside += [up_grad, down_grad] + attn_scatter.sent
+            beside += attn_scatter.sent
+            ff_open[above] = ff_scatter
         pre_late, branch_late = after((pre_grad, branch_all), normed_part)
         ff_scatter = Scatter(
             [gradient_half(normed_two_all, pre_late, True)],
@@ -804,8 +1011,9 @@
         )
         ff_scatter.send()
         beside += ff_scatter.now() + ff_scatter.sent
-        down_bias_part = jnp.sum(after(branch_grad, normed_part).astype(F32), axis=0)
-        up_bias_grads[l] = jnp.sum(pre_late.astype(F32), axis=0)
+        if l == last:
+            down_bias_part = column_sum(after(branch_grad, normed_part))
+        up_bias_grads[l] = column_sum(pre_late)
         beside += [down_bias_part, up_bias_grads[l]]
         if l == last:
             final_part = times_turned(after(activation, *ff_scatter.sent), w_down, BF16)
@@ -822,14 +1030,10 @@
             out_grad = tensor_sum(after(out_stack, normed_two_grad)).astype(F32).T
             query_sum = tensor_sum(after(query_stack, normed_two_grad))
             query_w_grad, kv_grad = split_query(query_sum, depth, pair_cols)
-            reduced[above] = (query_w_grad, kv_grad, out_grad) + reduced[above]
-        hidden_part, gain_two_part, shift_two_part = jax.vjp(
-            layer_norm, hidden_state, gain_two[l], shift_two[l]
-        )[1](normed_two_grad.astype(F32))
-        hidden_grad = tangent + hidden_part
-        attn_grad = hidden_grad.astype(BF16)
-        out_bias_part = jnp.sum(attn_grad.astype(F32), axis=0)
-        mixed_grad = product(attn_grad, w_out).astype(BF16)
+        hidden_grad, attn_grad, two_sums = norm_back(
+            hidden_state, normed_two_grad, gain_two[l : l + 1], tangent
+        )
+        mixed_grad = product(attn_grad, w_out)
         if l == 0:
             attn_late = after(attn_grad, mixed_grad)
             out_scatter = Scatter(
@@ -837,10 +1041,9 @@
                 [gradient_half(attn_late, mixed[:, split:])],
             ).send()
             mixed_grad = after(mixed_grad, *out_scatter.sent)
-        elif l == last:
-            mixed_grad = after(mixed_grad, *ff_scatter.come)
         query_grad, pair_part = attend_back(
             queries,
+            width,
             mixed_grad,
             pair_all[:, :HEAD],
             pair_all[:, HEAD:],
@@ -857,31 +1060,39 @@
         query_bias_grads[l] = jnp.sum(query_grad.astype(F32), axis=0)
         value_bias_grads[l] = jnp.sum(pair_grad[:, HEAD:].astype(F32), axis=0)
         both_grad = jnp.concatenate([query_grad, pair_grad], axis=1)
+        if l == last > 0:
+            both_grad = after(both_grad, *ff_scatter.come)
         if l == 0:
             both_grad = after(both_grad, *ff_scatter.come)
             both_scatter = Scatter(
                 [gradient_half(normed, both_grad[:, :split])],
                 [gradient_half(normed, both_grad[:, split:])],
             ).send()
-            out_scatter.settle(*both_scatter.sent).send()
-            ff_scatter.settle(*out_scatter.sent).send()
+            ff_scatter.settle(*both_scatter.sent).send()
+            out_scatter.settle(*ff_scatter.sent).send()
             both_grad = after(both_grad, *both_scatter.sent, *out_scatter.sent, *ff_scatter.sent)
+            ff_open[0] = ff_scatter
         normed_grad = product_turned(both_grad, w_query)
-        stream_part, gain_one_part, shift_one_part = jax.vjp(
-            layer_norm, stream_in, gain_one[l], shift_one[l]
-        )[1](normed_grad)
-        tangent = hidden_grad + stream_part
+        if l == last > 0:
+            normed_grad, final_sum = lax.optimization_barrier((normed_grad, final_sum))
+        tangent, branch_grad, one_sums = norm_back(
+            stream_in, normed_grad, gain_one[l : l + 1], hidden_grad
+        )
+        if l < last:
+            reduced[above] = (query_w_grad, kv_grad, out_grad)
         later = (l, both_grad, normed, attn_grad, mixed, ff_scatter)
         vector_grads[l] = [
-            gain_one_part,
-            shift_one_part,
-            out_bias_part,
-            gain_two_part,
-            shift_two_part,
+            one_sums[0],
+            one_sums[1],
+            two_sums[2],
+            two_sums[0],
+            two_sums[1],
             down_bias_part,
         ]
+        down_bias_part = one_sums[2]
+
     stacked = jnp.stack([vector_grads[l][m] for m in range(6) for l in range(layer_total)])
-    stacked = reorder(stacked, from_slots)
+    stacked = reorder(after(stacked, *ff_open[0].come), from_slots)
     query_rows = jnp.stack(query_bias_grads)
     value_rows = jnp.pad(jnp.stack(value_bias_grads), ((0, 0), (0, width - HEAD)))
     smalls = jnp.concatenate([stacked, query_rows, value_rows], axis=0)
@@ -906,7 +1117,7 @@
     )
     value_bias_grad = vector_sums[7][:, :HEAD]
 
-    grad_back = rows_back(tangent.astype(BF16))[1]
+    grad_back = rows_back(branch_grad)[1]
     out_back = after(out_back, tangent)
     both_scatter.settle(normed_grad).send()
     out_whole = jnp.concatenate(out_scatter.finish(), axis=1)
@@ -914,14 +1125,16 @@
     both_whole = jnp.concatenate(both_scatter.finish(), axis=1)
     query_stack = stack_query(both_whole, width, query_cols, pair_cols)
     query_w_grad, kv_grad = split_query(tensor_sum(query_stack), depth, pair_cols)
-    up_grad, down_grad = ff_scatter.finish()
-    reduced[0] = (query_w_grad, kv_grad, out_grad, up_grad, down_grad.T)
+    reduced[0] = (query_w_grad, kv_grad, out_grad)
+    up_stack, down_stack = [
+        stack_sums([ff.open_sum(m) for ff in ff_open], m == 1) for m in range(2)
+    ]
     if last == 0:
-        layer_out = (saved[last][7] + final_sum.astype(F32) + bias_down[last]).astype(BF16)
+        layer_out = add_rounded(saved[last][7], final_sum, bias_down[last][None])
         out_back = rows_back(layer_out)[1]
     layer_rows = contract_rows(send_table, out_back).astype(BF16)
     token_rows = contract_rows(send_table, grad_back).astype(BF16)
-    summed = [jnp.stack([reduced[l][m] for l in range(layer_total)]) for m in range(5)]
+    summed = [jnp.stack([reduced[l][m] for l in range(layer_total)]) for m in range(3)]
     return (
         layer_rows,
         token_rows,
@@ -935,9 +1148,9 @@
         vector_sums[2],
         vector_sums[3],
         vector_sums[4],
-        summed[3],
+        up_stack,
         up_bias_grad,
-        summed[4],
+        down_stack,
         vector_sums[5],
     )
 

time: 1150 us -> 1120 us (0.974)
  Pallas kernels: 393 us -> 487 us
  other arithmetic: 122 us -> 57.3 us
  waiting for transfers between devices: 359 us -> 312 us
  local copies, waits for them, and re-layouts: 122 us -> 79.7 us
  blocking collectives: 14.2 us -> 43.1 us
    pallas_call x0 -> x38, Pallas kernels: none -> 129 us  [the longest x20 46 us: take_blocks(): pl.pallas_call(lambda half_ref, out_ref: out_ref.__setitem__(..., half_re...]
    ppermute x73, waiting for transfers between devices: 274 us -> 224 us  [flip(): return lax.ppermute(values, 'dp', [(i, i ^ bit) for i in range(count)])]
    reduce_sum x22 -> x0, other arithmetic: 32.9 us -> none  [the longest x4 11.3 us: layer_norm(): return centred * lax.rsqrt(row_var + EPSILON) * scales + offsets]
    all_to_all x1 -> x2, blocking collectives: 14.2 us -> 43.1 us  [tensor_swap(): lax.all_to_all(values, 'tensor', split_axis=0, concat_axis=0, tiled=True)]
    slice x22 -> x10, local copies, waits for them, and re-layouts: 32.2 us -> 7.92 us  [the longest x2 2.01 us: local(): pair_own = queries[:, width:]]
    pallas_call x6 -> x2, Pallas kernels: 32.6 us -> 9.57 us  [reorder(): pl.pallas_call(copy_block, grid_spec=pltpu.PrefetchScalarGridSpec(num_sca...]
    unnamed x284 -> x190, local copies, waits for them, and re-layouts: 45.9 us -> 25.1 us
    convert_element_type x12 -> x2, other arithmetic: 17.2 us -> 2.05 us  [the longest x1 1.34 us: local(): tangent = last_branch.astype(F32)]
  transfers between devices with their start and end apart: 98 -> 97, of which waited for: 42 -> 33; matrix products, arithmetic and copies ran while one was open for 21% -> 13% of each run, Pallas kernels for 30% -> 39%
where the time goes in v3:
time: 1120 us; the launch traced here: 1110 us
  Pallas kernels  487 us (43%)
  waiting for transfers between devices  312 us (28%)
  starting transfers between devices  85.7 us (8%)
  local copies, waits for them, and re-layouts  79.7 us (7%)
  other arithmetic  57.3 us (5%)
  blocking collectives  43.1 us (4%)
  matrix products  24.6 us (2%)
  between operations  15.7 us (1%)
    ppermute x73, waiting for transfers between devices, flip(): return lax.ppermute(values, 'dp', [(i, i ^ bit) for i in range(count)])  224 us
    pallas_call x12, Pallas kernels, turned_product(): pl.pallas_call(kernel, grid=(steps,), in_specs=[pl.BlockSpec((rows, tile)...  86.4 us
    pallas_call x10, Pallas kernels, times(): pl.pallas_call(kernel, grid=(columns // tile,), in_specs=[pl.BlockSpec((r...  85.4 us
    pallas_call x10, Pallas kernels, times_turned(): pl.pallas_call(kernel, grid=(rows // tile,), in_specs=[pl.BlockSpec((tile...  84.7 us
    ppermute x73, starting transfers between devices, flip(): return lax.ppermute(values, 'dp', [(i, i ^ bit) for i in range(count)])  53.3 us
    pallas_call x16, Pallas kernels, add_blocks(): pl.pallas_call(kernel, grid=(len(keep),), in_specs=[pl.BlockSpec(block, l...  47.3 us
    pallas_call x20, Pallas kernels, take_blocks(): pl.pallas_call(lambda half_ref, out_ref: out_ref.__setitem__(..., half_re...  46 us
    all_to_all x2, blocking collectives, tensor_swap(): lax.all_to_all(values, 'tensor', split_axis=0, concat_axis=0, tiled=True)  43.1 us
  transfers between devices with their start and end apart: 97, of which 33 were waited for; matrix products, arithmetic and copies ran while one was open for 13% of the time, Pallas kernels for 39%

profile of v3, /device:TPU:0, one launch (start us, length us, event | category | flops | bytes accessed | tf_op | source)
XLA Modules:
  0.0 1105.5 jit_solution(17946329915062874135)
XLA Ops:
  14.0 5.2 all-to-all-start.1
  20.1 11.7 %all-to-all-done.1 = bf16[8,24,2048]{2,1,0:T(8,128)(2,1)S(1)} async-done(((bf16[8,24,2048]{2,1,0:T(8,128)(2,1)}), bf16[8,24,2048]{2,1,0:T(8,128)(2,1)S(1)}, u32[]{:S(2)}, u32[]{:S(2)}) %all-to-all-start.1) | async-done | bytes 786464 | tf_op jit(solution)/shard_map/all_to_all | solution.py:741
  39.6 11.7 %all-to-all-done = bf16[8,24,2176]{2,1,0:T(8,128)(2,1)S(1)} async-done(((bf16[8,24,2176]{2,1,0:T(8,128)(2,1)}), bf16[8,24,2176]{2,1,0:T(8,128)(2,1)S(1)}, u32[]{:S(2)}, u32[]{:S(2)}) %all-to-all-start) | async-done | bytes 835616 | tf_op jit(solution)/shard_map/all_to_all | solution.py:739
  53.4 4.8 reorder.2
  65.5 10.9 collective-permute-done.1
  82.0 6.5 place_rows.4.base_ref
  88.4 6.5 place_rows.5.values_ref
  103.1 6.4 collective-permute-done.5.refs_1_
  112.4 13.3 %collective-permute-done.2.refs_1_ = bf16[512,1024]{1,0:T(8,128)(2,1)S(1)} collective-permute-done((bf16[512,1024]{1,0:T(8,128)(2,1)S(1)}, bf16[512,1024]{1,0:T(8,128)(2,1)S(1)}, u32[]{:S(2)}, u32[]{:S(2)}) %collective-permute-start.2) | collective-permute-done | bytes 1048608 | tf_op jit(solution)/shard_map/ppermute | solution.py:37
  134.1 4.8 times.11
  140.7 4.6 all-to-all-start.2
  159.6 8.4 all-to-all-done.2
  171.5 9.9 attend.2
  187.2 5.0 times_turned.10
  192.2 5.1 times_turned.11
  215.7 41.2 %collective-permute-done.18.refs_1_ = bf16[512,2048]{1,0:T(8,128)(2,1)} collective-permute-done((bf16[512,2048]{1,0:T(8,128)(2,1)S(1)}, bf16[512,2048]{1,0:T(8,128)(2,1)}, u32[]{:S(2)}, u32[]{:S(2)}) %collective-permute-start.18) | collective-permute-done | bytes 2097184 | tf_op jit(solution)/shard_map/ppermute | solution.py:37
  276.9 13.5 %times.12 = (f32[768,2048]{1,0:T(8,128)}, bf16[768,2048]{1,0:T(8,128)(2,1)}) custom-call(bf16[768,2048]{1,0:T(8,128)(2,1)} %all-gather.15.cloned.1.call-done.left_ref, bf16[512,2048]{1,0:T(8,128)(2,1)} %copy-done.5, bf16[512,2048]{1,0:T(8,128)(2,1)} %collective-permute-done.18.refs_1_, bf16[512,2048]{1,0:T(8,128)(2,1)} %collective-permute-done.19.refs_2_, ...), custom_call_target="tpu_custom_call" | custom-call | flops 1 | bytes 1 | tf_op jit(solution)/shard_map/times/pallas_call | solution.py:436
  290.4 11.9 %times_turned.12 = bf16[768,2048]{1,0:T(8,128)(2,1)} custom-call(bf16[768,2048]{1,0:T(8,128)(2,1)} %get-tuple-element.155.left_ref.right_ref, bf16[512,2048]{1,0:T(8,128)(2,1)} %pad_maximum_fusion.2.refs_0_, bf16[512,2048]{1,0:T(8,128)(2,1)} %collective-permute-done.21.refs_1_, bf16[512,2048]{1,0:T(8,128)(2,1)} %collective-permute-done.22.refs_2_, ...), custom_call_target="tpu_custom_call" | custom-call | flops 1 | bytes 1 | tf_op jit(solution)/shard_map/times_turned/pallas_call | solution.py:469
  309.8 48.1 %collective-permute-done.26.refs_1_ = bf16[512,2304]{1,0:T(8,128)(2,1)} collective-permute-done((bf16[512,2304]{1,0:T(8,128)(2,1)S(1)}, bf16[512,2304]{1,0:T(8,128)(2,1)}, u32[]{:S(2)}, u32[]{:S(2)}) %collective-permute-start.26) | collective-permute-done | bytes 2359328 | tf_op jit(solution)/shard_map/ppermute | solution.py:37
  359.1 6.7 collective-permute-done.30.refs_2_
  372.7 7.3 times.13.refs_0_
  387.2 19.3 %all-to-all-done.3 = bf16[4,192,256]{2,1,0:T(8,128)(2,1)S(1)} async-done(((bf16[4,192,256]{2,1,0:T(8,128)(2,1)}), bf16[4,192,256]{2,1,0:T(8,128)(2,1)S(1)}, u32[]{:S(2)}, u32[]{:S(2)}) %all-to-all-start.3) | async-done | bytes 393248 | tf_op jit(solution)/shard_map/all_to_all | solution.py:485
  408.2 9.9 attend.3
  418.1 7.7 times_turned.13.refs_0_
  441.6 38.9 %collective-permute-done.34.refs_1_ = bf16[512,2048]{1,0:T(8,128)(2,1)} collective-permute-done((bf16[512,2048]{1,0:T(8,128)(2,1)}, bf16[512,2048]{1,0:T(8,128)(2,1)}, u32[]{:S(2)}, u32[]{:S(2)}) %collective-permute-start.34) | collective-permute-done | bytes 2097184 | tf_op jit(solution)/shard_map/ppermute | solution.py:37
  489.2 11.6 %times.14.refs_5_ = f32[768,2048]{1,0:T(8,128)} custom-call(bf16[768,2048]{1,0:T(8,128)(2,1)} %copy-done.3, bf16[512,2048]{1,0:T(8,128)(2,1)} %pad_maximum_fusion.5.refs_0_, bf16[512,2048]{1,0:T(8,128)(2,1)} %collective-permute-done.37.refs_1_, bf16[512,2048]{1,0:T(8,128)(2,1)} %collective-permute-done.38.refs_2_, ...), custom_call_target="tpu_custom_call" | custom-call | flops 1 | bytes 1 | tf_op jit(solution)/shard_map/times/pallas_call | solution.py:436
  500.8 15.5 %times.15 = (bf16[768,2048]{1,0:T(8,128)(2,1)}, bf16[768,2048]{1,0:T(8,128)(2,1)}) custom-call(bf16[768,2048]{1,0:T(8,128)(2,1)} %all-gather.19.cloned.1.call-done.left_ref, bf16[512,2048]{1,0:T(8,128)(2,1)} %pad_maximum_fusion.4.refs_0_, bf16[512,2048]{1,0:T(8,128)(2,1)} %collective-permute-done.34.refs_1_, ...), custom_call_target="tpu_custom_call" | custom-call | flops 1 | bytes 1 | tf_op jit(solution)/shard_map/times/pallas_call | solution.py:436
  516.3 11.9 %times_turned.14 = bf16[768,2048]{1,0:T(8,128)(2,1)} custom-call(bf16[768,2048]{1,0:T(8,128)(2,1)} %get-tuple-element.181.left_ref.right_ref.values_ref, bf16[512,2048]{1,0:T(8,128)(2,1)} %pad_maximum_fusion.4.refs_0_, bf16[512,2048]{1,0:T(8,128)(2,1)} %collective-permute-done.34.refs_1_, bf16[512,2048]{1,0:T(8,128)(2,1)} %collective-permute-done.35.refs_2_, ...), custom_call_target="tpu_custom_call" | custom-call | flops 1 | bytes 1 | tf_op jit(solution)/shard_map/times_turned/pallas_call | solution.py:469
  528.5 7.4 turned_product.12
  536.5 7.4 turned_product.14
  543.9 8.2 turned_product.13.half_ref
  552.2 8.3 turned_product.15.half_ref
  565.7 12.0 %times_turned.15 = bf16[768,2048]{1,0:T(8,128)(2,1)} custom-call(bf16[768,2048]{1,0:T(8,128)(2,1)} %get-tuple-element.184.right_ref.left_ref, bf16[512,2048]{1,0:T(8,128)(2,1)} %pad_maximum_fusion.5.refs_0_, bf16[512,2048]{1,0:T(8,128)(2,1)} %collective-permute-done.37.refs_1_, bf16[512,2048]{1,0:T(8,128)(2,1)} %collective-permute-done.38.refs_2_, ...), custom_call_target="tpu_custom_call" | custom-call | flops 1 | bytes 1 | tf_op jit(solution)/shard_map/times_turned/pallas_call | solution.py:469
  577.7 8.4 reduce-scatter.11.cloned.1.call-done.grad_ref
  590.5 4.7 norm_back.4
  595.3 6.4 times.16.refs_1_
  601.7 12.7 %attend_back.2 = (bf16[192,2048]{1,0:T(8,128)(2,1)}, f32[768,256]{1,0:T(8,128)}) custom-call(bf16[192,2304]{1,0:T(8,128)(2,1)} %times.13.refs_0_, bf16[192,2048]{1,0:T(8,128)(2,1)} %times.16.refs_1_, bf16[768,128]{1,0:T(8,128)(2,1)} %get-tuple-element.339.refs_1_.refs_2_, bf16[768,128]{1,0:T(8,128)(2,1)} %get-tuple-element.338.refs_3_, ...), custom_call_target="tpu_custom_call" | custom-call | flops 1 | bytes 1 | tf_op jit(solution)/shard_map/attend_back/pallas_call | solution.py:666
  615.6 26.7 %all_to_all.88 = bf16[4,192,256]{2,1,0:T(8,128)(2,1)S(1)} all-to-all(bf16[4,192,256]{2,1,0:T(8,128)(2,1)S(1)} %bitcast.93), channel_id=1, replica_groups=mesh['dp'=8,'tensor'=4] {'tensor'}, dimensions={0} | all-to-all | bytes 786432 | tf_op jit(solution)/shard_map/all_to_all | solution.py:485
  643.4 8.5 times_turned.16.grad_ref
  654.8 5.2 norm_back.5
  666.8 5.2 turned_product.16
  672.0 5.0 turned_product.18
  680.3 6.4 turned_product.17.half_ref
  691.0 5.9 turned_product.19.half_ref
  711.2 6.5 place_rows.6
  717.7 24.2 %all-gather.23.cloned.1.call-done.left_ref = bf16[768,2048]{1,0:T(8,128)(2,1)} async-done(((bf16[192,2048]{1,0:T(8,128)(2,1)}), bf16[768,2048]{1,0:T(8,128)(2,1)}) %all-gather.23.cloned.1.call-update) | async-done | bytes 3145744 | tf_op jit(solution)/shard_map/all_gather | solution.py:489
  741.9 14.2 %times.17.left_ref.right_ref.values_ref = bf16[768,2048]{1,0:T(8,128)(2,1)} custom-call(bf16[768,2048]{1,0:T(8,128)(2,1)} %all-gather.23.cloned.1.call-done.left_ref, bf16[512,2048]{1,0:T(8,128)(2,1)} %pad_maximum_fusion.2.refs_0_, bf16[512,2048]{1,0:T(8,128)(2,1)} %collective-permute-done.21.refs_1_, bf16[512,2048]{1,0:T(8,128)(2,1)} %collective-permute-done.22.refs_2_, ...), custom_call_target="tpu_custom_call" | custom-call | flops 1 | bytes 1 | tf_op jit(solution)/shard_map/times/pallas_call | solution.py:436
  756.1 11.9 %times_turned.17 = bf16[768,2048]{1,0:T(8,128)(2,1)} custom-call(bf16[768,2048]{1,0:T(8,128)(2,1)} %times.17.left_ref.right_ref.values_ref, bf16[512,2048]{1,0:T(8,128)(2,1)} %copy-done.5, bf16[512,2048]{1,0:T(8,128)(2,1)} %collective-permute-done.18.refs_1_, bf16[512,2048]{1,0:T(8,128)(2,1)} %collective-permute-done.19.refs_2_, ...), custom_call_target="tpu_custom_call" | custom-call | flops 1 | bytes 1 | tf_op jit(solution)/shard_map/times_turned/pallas_call | solution.py:469
  769.8 8.6 turned_product.20
  778.3 7.5 turned_product.22
  800.1 8.3 turned_product.21.half_ref
  808.3 8.3 turned_product.23.half_ref
  841.4 4.7 norm_back.6
  870.5 12.6 %attend_back.3 = (bf16[192,2048]{1,0:T(8,128)(2,1)}, f32[768,256]{1,0:T(8,128)}) custom-call(bf16[192,2304]{1,0:T(8,128)(2,1)} %pad_maximum_fusion.15.refs_0_, bf16[192,2048]{1,0:T(8,128)(2,1)} %pad_maximum_fusion.18.refs_1_, bf16[768,128]{1,0:T(8,128)(2,1)} %get-tuple-element.335.refs_1_.refs_2_, bf16[768,128]{1,0:T(8,128)(2,1)} %get-tuple-element.334.refs_3_, ...), custom_call_target="tpu_custom_call" | custom-call | flops 1 | bytes 1 | tf_op jit(solution)/shard_map/attend_back/pallas_call | solution.py:666
  884.4 16.4 %all_to_all.89 = bf16[4,192,256]{2,1,0:T(8,128)(2,1)S(1)} all-to-all(bf16[4,192,256]{2,1,0:T(8,128)(2,1)S(1)} %bitcast.94), channel_id=1, replica_groups=mesh['dp'=8,'tensor'=4] {'tensor'}, dimensions={0} | all-to-all | bytes 786432 | tf_op jit(solution)/shard_map/all_to_all | solution.py:485
  900.9 5.4 collective-permute-done.56.come_ref
  969.1 4.9 times_turned.18
  974.1 5.8 times_turned.19
  982.5 5.2 norm_back.7
  987.7 7.7 collective-permute-done.74.come_ref
  1021.9 4.8 reorder.3
  1052.6 6.4 place_rows.7
  1065.7 12.9 %collective-permute-done.67 = f32[18,2048]{1,0:T(8,128)S(1)} collective-permute-done((f32[18,2048]{1,0:T(8,128)S(1)}, f32[18,2048]{1,0:T(8,128)S(1)}, u32[]{:S(2)}, u32[]{:S(2)}) %collective-permute-start.67) | collective-permute-done | bytes 147488 | tf_op jit(solution)/shard_map/ppermute | solution.py:37
  1085.8 4.8 stack_sums.3
  (602 shorter events, 412.1 us)
Async XLA Ops:
  7.2 52.5 %all-gather.9.cloned.1.call-start = ((), (), s32[]{:S(2)}) async-start(), calls=%async_computation.16 | async-start | bytes 1556480 | tf_op jit(solution)/shard_map/all_gather | solution.py:489
  19.2 90.4 %all-gather.11.cloned.1.call-start = ((), (), s32[]{:S(2)}) async-start(), calls=%async_computation.17 | async-start | bytes 1310720 | tf_op jit(solution)/shard_map/all_gather | solution.py:489
  38.2 89.0 %all-gather.17.cloned.1.call-start = ((), (), s32[]{:S(2)}) async-start(), calls=%async_computation.20 | async-start | bytes 2867200 | tf_op jit(solution)/shard_map/all_gather | solution.py:489
  51.3 157.2 %all-gather.13.cloned.1.call-start = ((), (), s32[]{:S(2)}) async-start(), calls=%async_computation.18 | async-start | bytes 1966080 | tf_op jit(solution)/shard_map/all_gather | solution.py:489
  77.6 32.0 %collective-permute-start.5 = (bf16[512,1280]{1,0:T(8,128)(2,1)S(1)}, bf16[512,1280]{1,0:T(8,128)(2,1)}, u32[]{:S(2)}, u32[]{:S(2)}) collective-permute-start(bf16[512,1280]{1,0:T(8,128)(2,1)S(1)} %pad_maximum_fusion.6.refs_0_), channel_id=1, source_target_pairs={{0,8},{4,12},{8,0},{12,4},{16,24},{20,28},{24,16},{28,20},{1,9},{5... | collective-permute-start | bytes 3932168 | tf_op jit(solution)/shard_map/ppermute | solution.py:37
  101.6 24.1 %collective-permute-start.2 = (bf16[512,1024]{1,0:T(8,128)(2,1)S(1)}, bf16[512,1024]{1,0:T(8,128)(2,1)S(1)}, u32[]{:S(2)}, u32[]{:S(2)}) collective-permute-start(bf16[512,1024]{1,0:T(8,128)(2,1)S(1)} %pad_maximum_fusion.8.refs_0_), channel_id=1, source_target_pairs={{0,16},{4,20},{8,24},{12,28},{16,0},{20,4},{24,8},{28,12},{1,17},{... | collective-permute-start | bytes 3145736 | tf_op jit(solution)/shard_map/ppermute | solution.py:37
  103.0 31.1 %collective-permute-start.6 = (bf16[512,1280]{1,0:T(8,128)(2,1)S(1)}, bf16[512,1280]{1,0:T(8,128)(2,1)}, u32[]{:S(2)}, u32[]{:S(2)}) collective-permute-start(bf16[512,1280]{1,0:T(8,128)(2,1)S(1)} %pad_maximum_fusion.6.refs_0_), channel_id=1, source_target_pairs={{0,4},{4,0},{8,12},{12,8},{16,20},{20,16},{24,28},{28,24},{1,5},{5... | collective-permute-start | bytes 3932168 | tf_op jit(solution)/shard_map/ppermute | solution.py:37
  109.5 24.5 %collective-permute-start.7 = (bf16[512,1280]{1,0:T(8,128)(2,1)}, bf16[512,1280]{1,0:T(8,128)(2,1)}, u32[]{:S(2)}, u32[]{:S(2)}) collective-permute-start(bf16[512,1280]{1,0:T(8,128)(2,1)} %collective-permute-done.5.refs_1_), channel_id=1, source_target_pairs={{0,4},{4,0},{8,12},{12,8},{16,20},{20,16},{24,28},{28,24},{1,5},{5... | collective-permute-start | bytes 3932168 | tf_op jit(solution)/shard_map/ppermute | solution.py:37
  140.7 27.3 %all-to-all-start.2 = ((bf16[4,192,256]{2,1,0:T(8,128)(2,1)}), bf16[4,192,256]{2,1,0:T(8,128)(2,1)S(1)}, u32[]{:S(2)}, u32[]{:S(2)}) async-start(bf16[4,192,256]{2,1,0:T(8,128)(2,1)} %bitcast.14), calls=%async_computation.2 | async-start | bytes 786432 | tf_op jit(solution)/shard_map/all_to_all | solution.py:485
  145.3 125.9 %all-gather.15.cloned.1.call-start = ((), (), s32[]{:S(2)}) async-start(), calls=%async_computation.19 | async-start | bytes 3932160 | tf_op jit(solution)/shard_map/all_gather | solution.py:489
  148.9 34.6 %collective-permute-start.11 = (bf16[512,1024]{1,0:T(8,128)(2,1)S(1)}, bf16[512,1024]{1,0:T(8,128)(2,1)}, u32[]{:S(2)}, u32[]{:S(2)}) collective-permute-start(bf16[512,1024]{1,0:T(8,128)(2,1)S(1)} %pad_maximum_fusion.9.refs_0_), channel_id=1, source_target_pairs={{0,4},{4,0},{8,12},{12,8},{16,20},{20,16},{24,28},{28,24},{1,5},{5... | collective-permute-start | bytes 3145736 | tf_op jit(solution)/shard_map/ppermute | solution.py:37
  149.0 32.5 %collective-permute-start.10 = (bf16[512,1024]{1,0:T(8,128)(2,1)S(1)}, bf16[512,1024]{1,0:T(8,128)(2,1)}, u32[]{:S(2)}, u32[]{:S(2)}) collective-permute-start(bf16[512,1024]{1,0:T(8,128)(2,1)S(1)} %pad_maximum_fusion.9.refs_0_), channel_id=1, source_target_pairs={{0,16},{4,20},{8,24},{12,28},{16,0},{20,4},{24,8},{28,12},{1,17},{... | collective-permute-start | bytes 3145736 | tf_op jit(solution)/shard_map/ppermute | solution.py:37
  151.9 29.6 %collective-permute-start.13 = (bf16[512,1024]{1,0:T(8,128)(2,1)S(1)}, bf16[512,1024]{1,0:T(8,128)(2,1)}, u32[]{:S(2)}, u32[]{:S(2)}) collective-permute-start(bf16[512,1024]{1,0:T(8,128)(2,1)S(1)} %pad_maximum_fusion.10.refs_0_), channel_id=1, source_target_pairs={{0,8},{4,12},{8,0},{12,4},{16,24},{20,28},{24,16},{28,20},{1,9},{5... | collective-permute-start | bytes 3145736 | tf_op jit(solution)/shard_map/ppermute | solution.py:37
  159.6 32.5 %collective-permute-start.14 = (bf16[512,1024]{1,0:T(8,128)(2,1)S(1)}, bf16[512,1024]{1,0:T(8,128)(2,1)}, u32[]{:S(2)}, u32[]{:S(2)}) collective-permute-start(bf16[512,1024]{1,0:T(8,128)(2,1)S(1)} %pad_maximum_fusion.10.refs_0_), channel_id=1, source_target_pairs={{0,4},{4,0},{8,12},{12,8},{16,20},{20,16},{24,28},{28,24},{1,5},{5... | collective-permute-start | bytes 3145736 | tf_op jit(solution)/shard_map/ppermute | solution.py:37
  182.0 25.5 %collective-permute-start.16 = (bf16[256,2048]{1,0:T(8,128)(2,1)}, bf16[256,2048]{1,0:T(8,128)(2,1)}, u32[]{:S(2)}, u32[]{:S(2)}) collective-permute-start(bf16[256,2048]{1,0:T(8,128)(2,1)} %get-tuple-element.146), channel_id=1, source_target_pairs={{0,8},{4,12},{8,0},{12,4},{16,24},{20,28},{24,16},{28,20},{1,9},{5... | collective-permute-start | bytes 3145736 | tf_op jit(solution)/shard_map/ppermute | solution.py:37
  183.5 25.0 %collective-permute-start.17 = (bf16[256,2048]{1,0:T(8,128)(2,1)S(1)}, bf16[256,2048]{1,0:T(8,128)(2,1)}, u32[]{:S(2)}, u32[]{:S(2)}) collective-permute-start(bf16[256,2048]{1,0:T(8,128)(2,1)S(1)} %bitcast.77), channel_id=1, source_target_pairs={{0,16},{4,20},{8,24},{12,28},{16,0},{20,4},{24,8},{28,12},{1,17},{... | collective-permute-start | bytes 3145736 | tf_op jit(solution)/shard_map/ppermute | solution.py:37
  208.5 160.3 %reduce-scatter.9.cloned.1.call-start = ((), (), s32[]{:S(2)}) async-start(), calls=%async_computation.21 | async-start | bytes 3932160 | tf_op jit(solution)/shard_map/reduce_scatter | solution.py:493
  210.3 46.6 %collective-permute-start.18 = (bf16[512,2048]{1,0:T(8,128)(2,1)S(1)}, bf16[512,2048]{1,0:T(8,128)(2,1)}, u32[]{:S(2)}, u32[]{:S(2)}) collective-permute-start(bf16[512,2048]{1,0:T(8,128)(2,1)S(1)} %pad_maximum_fusion.1.refs_0_), channel_id=1, source_target_pairs={{0,16},{4,20},{8,24},{12,28},{16,0},{20,4},{24,8},{28,12},{1,17},{... | collective-permute-start | bytes 6291464 | tf_op jit(solution)/shard_map/ppermute | solution.py:37
  214.7 46.5 %collective-permute-start.21 = (bf16[512,2048]{1,0:T(8,128)(2,1)}, bf16[512,2048]{1,0:T(8,128)(2,1)}, u32[]{:S(2)}, u32[]{:S(2)}) collective-permute-start(bf16[512,2048]{1,0:T(8,128)(2,1)} %pad_maximum_fusion.2.refs_0_), channel_id=1, source_target_pairs={{0,8},{4,12},{8,0},{12,4},{16,24},{20,28},{24,16},{28,20},{1,9},{5... | collective-permute-start | bytes 6291464 | tf_op jit(solution)/shard_map/ppermute | solution.py:37
  215.2 55.0 %collective-permute-start.19 = (bf16[512,2048]{1,0:T(8,128)(2,1)S(1)}, bf16[512,2048]{1,0:T(8,128)(2,1)}, u32[]{:S(2)}, u32[]{:S(2)}) collective-permute-start(bf16[512,2048]{1,0:T(8,128)(2,1)S(1)} %pad_maximum_fusion.1.refs_0_), channel_id=1, source_target_pairs={{0,4},{4,0},{8,12},{12,8},{16,20},{20,16},{24,28},{28,24},{1,5},{5... | collective-permute-start | bytes 6291464 | tf_op jit(solution)/shard_map/ppermute | solution.py:37
  215.2 55.0 %collective-permute-start.22 = (bf16[512,2048]{1,0:T(8,128)(2,1)}, bf16[512,2048]{1,0:T(8,128)(2,1)}, u32[]{:S(2)}, u32[]{:S(2)}) collective-permute-start(bf16[512,2048]{1,0:T(8,128)(2,1)} %pad_maximum_fusion.2.refs_0_), channel_id=1, source_target_pairs={{0,4},{4,0},{8,12},{12,8},{16,20},{20,16},{24,28},{28,24},{1,5},{5... | collective-permute-start | bytes 6291464 | tf_op jit(solution)/shard_map/ppermute | solution.py:37
  271.2 31.1 %collective-permute-start.24 = (bf16[256,2304]{1,0:T(8,128)(2,1)S(1)}, bf16[256,2304]{1,0:T(8,128)(2,1)S(1)}, u32[]{:S(2)}, u32[]{:S(2)}) collective-permute-start(bf16[256,2304]{1,0:T(8,128)(2,1)S(1)} %concatenate.130), channel_id=1, source_target_pairs={{0,8},{4,12},{8,0},{12,4},{16,24},{20,28},{24,16},{28,20},{1,9},{5... | collective-permute-start | bytes 3538952 | tf_op jit(solution)/shard_map/ppermute | solution.py:37
  274.8 27.5 %collective-permute-start.25 = (bf16[256,2048]{1,0:T(8,128)(2,1)}, bf16[256,2048]{1,0:T(8,128)(2,1)}, u32[]{:S(2)}, u32[]{:S(2)}) collective-permute-start(bf16[256,2048]{1,0:T(8,128)(2,1)} %pad_maximum_fusion.11), channel_id=1, source_target_pairs={{0,16},{4,20},{8,24},{12,28},{16,0},{20,4},{24,8},{28,12},{1,17},{... | collective-permute-start | bytes 3145736 | tf_op jit(solution)/shard_map/ppermute | solution.py:37
  303.3 135.5 %all-gather.21.cloned.1.call-start = ((), (), s32[]{:S(2)}) async-start(), calls=%async_computation.23 | async-start | bytes 1966080 | tf_op jit(solution)/shard_map/all_gather | solution.py:489
  305.3 52.6 %collective-permute-start.26 = (bf16[512,2304]{1,0:T(8,128)(2,1)S(1)}, bf16[512,2304]{1,0:T(8,128)(2,1)}, u32[]{:S(2)}, u32[]{:S(2)}) collective-permute-start(bf16[512,2304]{1,0:T(8,128)(2,1)S(1)} %pad_maximum_fusion.refs_0_), channel_id=1, source_target_pairs={{0,16},{4,20},{8,24},{12,28},{16,0},{20,4},{24,8},{28,12},{1,17},{... | collective-permute-start | bytes 7077896 | tf_op jit(solution)/shard_map/ppermute | solution.py:37
  309.1 49.3 %collective-permute-start.29 = (bf16[512,2048]{1,0:T(8,128)(2,1)}, bf16[512,2048]{1,0:T(8,128)(2,1)}, u32[]{:S(2)}, u32[]{:S(2)}) collective-permute-start(bf16[512,2048]{1,0:T(8,128)(2,1)} %pad_maximum_fusion.3.refs_0_), channel_id=1, source_target_pairs={{0,8},{4,12},{8,0},{12,4},{16,24},{20,28},{24,16},{28,20},{1,9},{5... | collective-permute-start | bytes 6291464 | tf_op jit(solution)/shard_map/ppermute | solution.py:37
  309.8 56.0 %collective-permute-start.27 = (bf16[512,2304]{1,0:T(8,128)(2,1)S(1)}, bf16[512,2304]{1,0:T(8,128)(2,1)}, u32[]{:S(2)}, u32[]{:S(2)}) collective-permute-start(bf16[512,2304]{1,0:T(8,128)(2,1)S(1)} %pad_maximum_fusion.refs_0_), channel_id=1, source_target_pairs={{0,4},{4,0},{8,12},{12,8},{16,20},{20,16},{24,28},{28,24},{1,5},{5... | collective-permute-start | bytes 7077896 | tf_op jit(solution)/shard_map/ppermute | solution.py:37
  381.9 24.6 %all-to-all-start.3 = ((bf16[4,192,256]{2,1,0:T(8,128)(2,1)}), bf16[4,192,256]{2,1,0:T(8,128)(2,1)S(1)}, u32[]{:S(2)}, u32[]{:S(2)}) async-start(bf16[4,192,256]{2,1,0:T(8,128)(2,1)} %bitcast.31), calls=%async_computation.4 | async-start | bytes 786432 | tf_op jit(solution)/shard_map/all_to_all | solution.py:485
  385.3 115.5 %all-gather.19.cloned.1.call-start = ((), (), s32[]{:S(2)}) async-start(), calls=%async_computation.22 | async-start | bytes 3932160 | tf_op jit(solution)/shard_map/all_gather | solution.py:489
  386.1 32.0 %collective-permute-start.32 = (bf16[256,2048]{1,0:T(8,128)(2,1)S(1)}, bf16[256,2048]{1,0:T(8,128)(2,1)}, u32[]{:S(2)}, u32[]{:S(2)}) collective-permute-start(bf16[256,2048]{1,0:T(8,128)(2,1)S(1)} %copy-done.24), channel_id=1, source_target_pairs={{0,8},{4,12},{8,0},{12,4},{16,24},{20,28},{24,16},{28,20},{1,9},{5... | collective-permute-start | bytes 3145736 | tf_op jit(solution)/shard_map/ppermute | solution.py:37
  386.7 31.4 %collective-permute-start.33 = (bf16[256,2048]{1,0:T(8,128)(2,1)S(1)}, bf16[256,2048]{1,0:T(8,128)(2,1)}, u32[]{:S(2)}, u32[]{:S(2)}) collective-permute-start(bf16[256,2048]{1,0:T(8,128)(2,1)S(1)} %bitcast.79), channel_id=1, source_target_pairs={{0,16},{4,20},{8,24},{12,28},{16,0},{20,4},{24,8},{28,12},{1,17},{... | collective-permute-start | bytes 3145736 | tf_op jit(solution)/shard_map/ppermute | solution.py:37
  430.0 156.1 %reduce-scatter.11.cloned.1.call-start = ((), (), s32[]{:S(2)}) async-start(), calls=%async_computation.24 | async-start | bytes 3932160 | tf_op jit(solution)/shard_map/reduce_scatter | solution.py:493
  432.8 47.7 %collective-permute-start.34 = (bf16[512,2048]{1,0:T(8,128)(2,1)}, bf16[512,2048]{1,0:T(8,128)(2,1)}, u32[]{:S(2)}, u32[]{:S(2)}) collective-permute-start(bf16[512,2048]{1,0:T(8,128)(2,1)} %pad_maximum_fusion.4.refs_0_), channel_id=1, source_target_pairs={{0,16},{4,20},{8,24},{12,28},{16,0},{20,4},{24,8},{28,12},{1,17},{... | collective-permute-start | bytes 6291464 | tf_op jit(solution)/shard_map/ppermute | solution.py:37
  436.9 47.5 %collective-permute-start.37 = (bf16[512,2048]{1,0:T(8,128)(2,1)}, bf16[512,2048]{1,0:T(8,128)(2,1)}, u32[]{:S(2)}, u32[]{:S(2)}) collective-permute-start(bf16[512,2048]{1,0:T(8,128)(2,1)} %pad_maximum_fusion.5.refs_0_), channel_id=1, source_target_pairs={{0,8},{4,12},{8,0},{12,4},{16,24},{20,28},{24,16},{28,20},{1,9},{5... | collective-permute-start | bytes 6291464 | tf_op jit(solution)/shard_map/ppermute | solution.py:37
  441.0 59.8 %collective-permute-start.35 = (bf16[512,2048]{1,0:T(8,128)(2,1)}, bf16[512,2048]{1,0:T(8,128)(2,1)}, u32[]{:S(2)}, u32[]{:S(2)}) collective-permute-start(bf16[512,2048]{1,0:T(8,128)(2,1)} %pad_maximum_fusion.4.refs_0_), channel_id=1, source_target_pairs={{0,4},{4,0},{8,12},{12,8},{16,20},{20,16},{24,28},{28,24},{1,5},{5... | collective-permute-start | bytes 6291464 | tf_op jit(solution)/shard_map/ppermute | solution.py:37
  441.1 46.4 %collective-permute-start.38 = (bf16[512,2048]{1,0:T(8,128)(2,1)}, bf16[512,2048]{1,0:T(8,128)(2,1)}, u32[]{:S(2)}, u32[]{:S(2)}) collective-permute-start(bf16[512,2048]{1,0:T(8,128)(2,1)} %pad_maximum_fusion.5.refs_0_), channel_id=1, source_target_pairs={{0,4},{4,0},{8,12},{12,8},{16,20},{20,16},{24,28},{28,24},{1,5},{5... | collective-permute-start | bytes 6291464 | tf_op jit(solution)/shard_map/ppermute | solution.py:37
  528.3 126.5 %reduce-scatter.13.cloned.1.call-start = ((), (), s32[]{:S(2)}) async-start(), calls=%async_computation.25 | async-start | bytes 3932160 | tf_op jit(solution)/shard_map/reduce_scatter | solution.py:493
  586.1 155.8 %all-gather.23.cloned.1.call-start = ((), (), s32[]{:S(2)}) async-start(), calls=%async_computation.26 | async-start | bytes 3932160 | tf_op jit(solution)/shard_map/all_gather | solution.py:489
  586.2 57.2 %collective-permute-start.42 = (bf16[512,2048]{1,0:T(8,128)(2,1)}, bf16[512,2048]{1,0:T(8,128)(2,1)}, u32[]{:S(2)}, u32[]{:S(2)}) collective-permute-start(bf16[512,2048]{1,0:T(8,128)(2,1)} %take_blocks.20), channel_id=1, source_target_pairs={{0,8},{4,12},{8,0},{12,4},{16,24},{20,28},{24,16},{28,20},{1,9},{5... | collective-permute-start | bytes 6291464 | tf_op jit(solution)/shard_map/ppermute | solution.py:37
  587.7 55.7 %collective-permute-start.43 = (bf16[512,2048]{1,0:T(8,128)(2,1)}, bf16[512,2048]{1,0:T(8,128)(2,1)}, u32[]{:S(2)}, u32[]{:S(2)}) collective-permute-start(bf16[512,2048]{1,0:T(8,128)(2,1)} %take_blocks.21), channel_id=1, source_target_pairs={{0,16},{4,20},{8,24},{12,28},{16,0},{20,4},{24,8},{28,12},{1,17},{... | collective-permute-start | bytes 6291464 | tf_op jit(solution)/shard_map/ppermute | solution.py:37
  677.5 163.9 %reduce-scatter.15.cloned.1.call-start = ((), (), s32[]{:S(2)}) async-start(), calls=%async_computation.27 | async-start | bytes 3932160 | tf_op jit(solution)/shard_map/reduce_scatter | solution.py:493
  689.6 80.1 %collective-permute-start.48 = (bf16[512,2304]{1,0:T(8,128)(2,1)}, bf16[512,2304]{1,0:T(8,128)(2,1)S(1)}, u32[]{:S(2)}, u32[]{:S(2)}) collective-permute-start(bf16[512,2304]{1,0:T(8,128)(2,1)} %take_blocks.24), channel_id=1, source_target_pairs={{0,8},{4,12},{8,0},{12,4},{16,24},{20,28},{24,16},{28,20},{1,9},{5... | collective-permute-start | bytes 7077896 | tf_op jit(solution)/shard_map/ppermute | solution.py:37
  699.6 70.1 %collective-permute-start.49 = (bf16[512,2048]{1,0:T(8,128)(2,1)}, bf16[512,2048]{1,0:T(8,128)(2,1)}, u32[]{:S(2)}, u32[]{:S(2)}) collective-permute-start(bf16[512,2048]{1,0:T(8,128)(2,1)} %take_blocks.25), channel_id=1, source_target_pairs={{0,16},{4,20},{8,24},{12,28},{16,0},{20,4},{24,8},{28,12},{1,17},{... | collective-permute-start | bytes 6291464 | tf_op jit(solution)/shard_map/ppermute | solution.py:37
  703.3 66.3 %collective-permute-start.46 = (bf16[256,2048]{1,0:T(8,128)(2,1)}, bf16[256,2048]{1,0:T(8,128)(2,1)S(1)}, u32[]{:S(2)}, u32[]{:S(2)}) collective-permute-start(bf16[256,2048]{1,0:T(8,128)(2,1)} %take_blocks.22), channel_id=1, source_target_pairs={{0,16},{4,20},{8,24},{12,28},{16,0},{20,4},{24,8},{28,12},{1,17},{... | collective-permute-start | bytes 3145736 | tf_op jit(solution)/shard_map/ppermute | solution.py:37
  706.1 63.5 %collective-permute-start.47 = (bf16[256,2048]{1,0:T(8,128)(2,1)}, bf16[256,2048]{1,0:T(8,128)(2,1)}, u32[]{:S(2)}, u32[]{:S(2)}) collective-permute-start(bf16[256,2048]{1,0:T(8,128)(2,1)} %take_blocks.23), channel_id=1, source_target_pairs={{0,8},{4,12},{8,0},{12,4},{16,24},{20,28},{24,16},{28,20},{1,9},{5... | collective-permute-start | bytes 3145736 | tf_op jit(solution)/shard_map/ppermute | solution.py:37
  769.7 281.0 %reduce-scatter.19.cloned.1.call-start = ((), (), s32[]{:S(2)}) async-start(), calls=%async_computation.29 | async-start | bytes 1474560 | tf_op jit(solution)/shard_map/reduce_scatter | solution.py:493
  785.8 22.5 %collective-permute-start.51 = (bf16[1024,2048]{1,0:T(8,128)(2,1)}, bf16[1024,2048]{1,0:T(8,128)(2,1)}, u32[]{:S(2)}, u32[]{:S(2)}) collective-permute-start(bf16[1024,2048]{1,0:T(8,128)(2,1)} %turned_product.22), channel_id=1, source_target_pairs={{0,4},{4,0},{8,12},{12,8},{16,20},{20,16},{24,28},{28,24},{1,5},{5... | collective-permute-start | bytes 12582920 | tf_op jit(solution)/shard_map/ppermute | solution.py:37
  792.4 32.3 %collective-permute-start.53 = (bf16[256,2304]{1,0:T(8,128)(2,1)}, bf16[256,2304]{1,0:T(8,128)(2,1)S(1)}, u32[]{:S(2)}, u32[]{:S(2)}) collective-permute-start(bf16[256,2304]{1,0:T(8,128)(2,1)} %take_blocks.26), channel_id=1, source_target_pairs={{0,16},{4,20},{8,24},{12,28},{16,0},{20,4},{24,8},{28,12},{1,17},{... | collective-permute-start | bytes 3538952 | tf_op jit(solution)/shard_map/ppermute | solution.py:37
  799.6 25.0 %collective-permute-start.52 = (bf16[256,2048]{1,0:T(8,128)(2,1)}, bf16[256,2048]{1,0:T(8,128)(2,1)S(1)}, u32[]{:S(2)}, u32[]{:S(2)}) collective-permute-start(bf16[256,2048]{1,0:T(8,128)(2,1)} %take_blocks.27), channel_id=1, source_target_pairs={{0,8},{4,12},{8,0},{12,4},{16,24},{20,28},{24,16},{28,20},{1,9},{5... | collective-permute-start | bytes 3145736 | tf_op jit(solution)/shard_map/ppermute | solution.py:37
  858.4 47.9 %collective-permute-start.56 = (bf16[512,2048]{1,0:T(8,128)(2,1)}, bf16[512,2048]{1,0:T(8,128)(2,1)}, u32[]{:S(2)}, u32[]{:S(2)}) collective-permute-start(bf16[512,2048]{1,0:T(8,128)(2,1)} %take_blocks.28), channel_id=1, source_target_pairs={{0,8},{4,12},{8,0},{12,4},{16,24},{20,28},{24,16},{28,20},{1,9},{5... | collective-permute-start | bytes 6291464 | tf_op jit(solution)/shard_map/ppermute | solution.py:37
  858.8 47.6 %collective-permute-start.57 = (bf16[512,2048]{1,0:T(8,128)(2,1)}, bf16[512,2048]{1,0:T(8,128)(2,1)}, u32[]{:S(2)}, u32[]{:S(2)}) collective-permute-start(bf16[512,2048]{1,0:T(8,128)(2,1)} %take_blocks.29), channel_id=1, source_target_pairs={{0,16},{4,20},{8,24},{12,28},{16,0},{20,4},{24,8},{28,12},{1,17},{... | collective-permute-start | bytes 6291464 | tf_op jit(solution)/shard_map/ppermute | solution.py:37
  908.9 183.5 %reduce-scatter.23.cloned.1.call-start = ((), (), s32[]{:S(2)}) async-start(), calls=%async_computation.31 | async-start | bytes 1310720 | tf_op jit(solution)/shard_map/reduce_scatter | solution.py:493
  918.2 35.4 %collective-permute-start.60 = (bf16[512,1024]{1,0:T(8,128)(2,1)}, bf16[512,1024]{1,0:T(8,128)(2,1)}, u32[]{:S(2)}, u32[]{:S(2)}) collective-permute-start(bf16[512,1024]{1,0:T(8,128)(2,1)} %take_blocks.30), channel_id=1, source_target_pairs={{0,8},{4,12},{8,0},{12,4},{16,24},{20,28},{24,16},{28,20},{1,9},{5... | collective-permute-start | bytes 3145736 | tf_op jit(solution)/shard_map/ppermute | solution.py:37
  919.8 33.7 %collective-permute-start.61 = (bf16[512,1024]{1,0:T(8,128)(2,1)}, bf16[512,1024]{1,0:T(8,128)(2,1)}, u32[]{:S(2)}, u32[]{:S(2)}) collective-permute-start(bf16[512,1024]{1,0:T(8,128)(2,1)} %take_blocks.31), channel_id=1, source_target_pairs={{0,16},{4,20},{8,24},{12,28},{16,0},{20,4},{24,8},{28,12},{1,17},{... | collective-permute-start | bytes 3145736 | tf_op jit(solution)/shard_map/ppermute | solution.py:37
  930.4 72.7 %collective-permute-start.70 = (bf16[512,1280]{1,0:T(8,128)(2,1)}, bf16[512,1280]{1,0:T(8,128)(2,1)}, u32[]{:S(2)}, u32[]{:S(2)}) collective-permute-start(bf16[512,1280]{1,0:T(8,128)(2,1)} %take_blocks.33), channel_id=1, source_target_pairs={{0,16},{4,20},{8,24},{12,28},{16,0},{20,4},{24,8},{28,12},{1,17},{... | collective-permute-start | bytes 3932168 | tf_op jit(solution)/shard_map/ppermute | solution.py:37
  941.9 85.9 %all-to-all-start.5 = ((bf16[8,24,2048]{2,1,0:T(8,128)(2,1)}), bf16[8,24,2048]{2,1,0:T(8,128)(2,1)S(1)}, u32[]{:S(2)}, u32[]{:S(2)}) async-start(bf16[8,24,2048]{2,1,0:T(8,128)(2,1)} %bitcast.40), calls=%async_computation.8 | async-start | bytes 1572864 | tf_op jit(solution)/shard_map/all_to_all | solution.py:857
  945.4 147.0 %reduce-scatter.21.cloned.1.call-start = ((), (), s32[]{:S(2)}) async-start(), calls=%async_computation.30 | async-start | bytes 1310720 | tf_op jit(solution)/shard_map/reduce_scatter | solution.py:493
  958.5 44.6 %collective-permute-start.69 = (bf16[512,1024]{1,0:T(8,128)(2,1)}, bf16[512,1024]{1,0:T(8,128)(2,1)}, u32[]{:S(2)}, u32[]{:S(2)}) collective-permute-start(bf16[512,1024]{1,0:T(8,128)(2,1)} %take_blocks.32), channel_id=1, source_target_pairs={{0,8},{4,12},{8,0},{12,4},{16,24},{20,28},{24,16},{28,20},{1,9},{5... | collective-permute-start | bytes 3145736 | tf_op jit(solution)/shard_map/ppermute | solution.py:37
  964.2 31.3 %collective-permute-start.74 = (bf16[256,1024]{1,0:T(8,128)(2,1)}, bf16[256,1024]{1,0:T(8,128)(2,1)}, u32[]{:S(2)}, u32[]{:S(2)}) collective-permute-start(bf16[256,1024]{1,0:T(8,128)(2,1)} %take_blocks.37), channel_id=1, source_target_pairs={{0,8},{4,12},{8,0},{12,4},{16,24},{20,28},{24,16},{28,20},{1,9},{5... | collective-permute-start | bytes 1572872 | tf_op jit(solution)/shard_map/ppermute | solution.py:37
  964.3 32.8 %collective-permute-start.73 = (bf16[256,1024]{1,0:T(8,128)(2,1)}, bf16[256,1024]{1,0:T(8,128)(2,1)}, u32[]{:S(2)}, u32[]{:S(2)}) collective-permute-start(bf16[256,1024]{1,0:T(8,128)(2,1)} %take_blocks.36), channel_id=1, source_target_pairs={{0,16},{4,20},{8,24},{12,28},{16,0},{20,4},{24,8},{28,12},{1,17},{... | collective-permute-start | bytes 1572872 | tf_op jit(solution)/shard_map/ppermute | solution.py:37
  969.0 48.9 %collective-permute-start.62 = (bf16[256,2048]{1,0:T(8,128)(2,1)}, bf16[256,2048]{1,0:T(8,128)(2,1)S(1)}, u32[]{:S(2)}, u32[]{:S(2)}) collective-permute-start(bf16[256,2048]{1,0:T(8,128)(2,1)} %take_blocks.34), channel_id=1, source_target_pairs={{0,16},{4,20},{8,24},{12,28},{16,0},{20,4},{24,8},{28,12},{1,17},{... | collective-permute-start | bytes 3145736 | tf_op jit(solution)/shard_map/ppermute | solution.py:37
  995.5 26.4 %collective-permute-start.63 = (bf16[256,2048]{1,0:T(8,128)(2,1)}, bf16[256,2048]{1,0:T(8,128)(2,1)}, u32[]{:S(2)}, u32[]{:S(2)}) collective-permute-start(bf16[256,2048]{1,0:T(8,128)(2,1)} %take_blocks.35), channel_id=1, source_target_pairs={{0,8},{4,12},{8,0},{12,4},{16,24},{20,28},{24,16},{28,20},{1,9},{5... | collective-permute-start | bytes 3145736 | tf_op jit(solution)/shard_map/ppermute | solution.py:37
  1007.9 26.6 %collective-permute-start.72 = (bf16[256,1280]{1,0:T(8,128)(2,1)}, bf16[256,1280]{1,0:T(8,128)(2,1)}, u32[]{:S(2)}, u32[]{:S(2)}) collective-permute-start(bf16[256,1280]{1,0:T(8,128)(2,1)} %take_blocks.39), channel_id=1, source_target_pairs={{0,8},{4,12},{8,0},{12,4},{16,24},{20,28},{24,16},{28,20},{1,9},{5... | collective-permute-start | bytes 1966088 | tf_op jit(solution)/shard_map/ppermute | solution.py:37
  1011.7 83.2 %reduce-scatter.17.cloned.1.call-start = ((), (), s32[]{:S(2)}) async-start(), calls=%async_computation.28 | async-start | bytes 1474560 | tf_op jit(solution)/shard_map/reduce_scatter | solution.py:493
  (110 other events, 1203.2 us)
Sparse Core Ops, SparseCore 0:
  11.8 34.2 all-gather.8
  48.3 27.0 all-gather.10
  77.5 48.8 all-gather.16
  127.8 44.2 all-gather.12
  208.6 62.4 all-gather.14
  302.5 57.2 reduce-scatter.8
  361.3 45.5 all-gather.20
  430.1 61.5 all-gather.18
  528.4 57.6 reduce-scatter.10
  588.3 66.4 reduce-scatter.12
  677.6 64.2 all-gather.22
  769.8 60.2 reduce-scatter.14
  909.1 29.3 reduce-scatter.18
  940.6 25.8 reduce-scatter.22
  1011.8 30.6 reduce-scatter.20
  1045.4 29.8 reduce-scatter.16

commit v4 on v3

--- a/solution.py
+++ b/solution.py
@@ -741,10 +741,6 @@
     tangent_come = lax.all_to_all(tangent_sent, "dp", split_axis=0, concat_axis=0, tiled=True)
     arrived_place = tokens_come[:, width].astype(jnp.int32)
     place_table = (row_ids[:, None] == arrived_place[None, :]).astype(BF16)
-    stream = place_rows(place_table, tokens_come, to_slots)
-    last_branch = place_rows(place_table, tangent_come, to_slots)
-    tangent = last_branch.astype(F32)
-    stream = after(stream, last_branch)
 
     places = jnp.arange(group_rows, dtype=jnp.int32)
     own_places = tensor_rank * local_rows + row_ids
@@ -830,11 +826,16 @@
         *query_gather.come
     )
     w_query = query_gather.finish()
+    sent = [parts[0][0] for parts in w_query]
+    tokens_come, tangent_come = after((tokens_come, tangent_come), *sent)
+    stream = place_rows(place_table, tokens_come, to_slots)
+    last_branch = place_rows(place_table, tangent_come, to_slots)
+    tangent = last_branch.astype(F32)
+    stream = after(stream, last_branch)
     early_rows = local_rows // 2
     if last > 0:
         query_rows = jnp.concatenate([part[: size - depth] for part in rest], axis=0)
         out_rows = jnp.concatenate([part[size - depth :] for part in rest], axis=0)
-        branch_early = tensor_rows(last_branch[:early_rows])
 
     def branch_whole(early, late):
         parts = []
@@ -872,6 +873,8 @@
         pair_t = pair_all.T
         if l == 0:
             out_gather.settle(projected).send(projected)
+            if last > 0:
+                branch_early = tensor_rows(after(last_branch[:early_rows], projected))
             ff_gather = Gather([up_weight[0]], [down_turned[0]]).send(pair_all)
         mixed, log_totals = attend(
             queries, width, pair_all[:, :HEAD], pair_t[HEAD:], score_bias, score_scale
@@ -1020,16 +1023,10 @@
             beside.append(final_part)
         else:
             both_whole, out_whole = attn_scatter.finish(*ff_scatter.now())
-            out_stack = stack_columns(out_whole, tensor_count)
-            query_stack = stack_query(both_whole, width, query_cols, pair_cols)
-            beside += [out_stack, query_stack]
+            beside += [both_whole, out_whole]
         normed_two_grad = after(normed_two_grad, *beside)
         if l == last:
             final_sum = tensor_sum(after(final_part, normed_two_grad))
-        else:
-            out_grad = tensor_sum(after(out_stack, normed_two_grad)).astype(F32).T
-            query_sum = tensor_sum(after(query_stack, normed_two_grad))
-            query_w_grad, kv_grad = split_query(query_sum, depth, pair_cols)
         hidden_grad, attn_grad, two_sums = norm_back(
             hidden_state, normed_two_grad, gain_two[l : l + 1], tangent
         )
@@ -1052,6 +1049,11 @@
             log_totals,
             score_scale,
         )
+        if l < last:
+            both_whole, out_whole = after((both_whole, out_whole), query_grad)
+            out_grad = tensor_sum(stack_columns(out_whole, tensor_count)).astype(F32).T
+            query_sum = tensor_sum(stack_query(both_whole, width, query_cols, pair_cols))
+            query_w_grad, kv_grad = split_query(query_sum, depth, pair_cols)
         pair_come = tensor_swap(pair_part.astype(BF16))
         pair_grad = sum(
             pair_come[k * local_rows : (k + 1) * local_rows].astype(F32)

time: 1120 us -> 1110 us (level)
  blocking collectives: 43.1 us -> 26.7 us
    all_to_all x2 -> x1, blocking collectives: 43.1 us -> 26.7 us  [tensor_swap(): lax.all_to_all(values, 'tensor', split_axis=0, concat_axis=0, tiled=True)]
    all_gather x8, waiting for transfers between devices: 25.3 us -> 38.4 us  [tensor_rows(): return lax.all_gather(values, 'tensor', axis=0, tiled=True)]
    unnamed x190 -> x204, local copies, waits for them, and re-layouts: 25.1 us -> 28 us
    all_to_all x2 -> x3, waiting for transfers between devices: 27.7 us -> 27.2 us  [tensor_swap(): lax.all_to_all(values, 'tensor', split_axis=0, concat_axis=0, tiled=True)]
  transfers between devices with their start and end apart: 97 -> 98, of which waited for: 33 -> 36; matrix products, arithmetic and copies ran while one was open for 13% -> 14% of each run, Pallas kernels for 39% -> 39%
where the time goes in v4:
time: 1110 us; the launch traced here: 1100 us
  Pallas kernels  488 us (44%)
  waiting for transfers between devices  312 us (28%)
  starting transfers between devices  88.2 us (8%)
  local copies, waits for them, and re-layouts  85.7 us (8%)
  other arithmetic  59 us (5%)
  blocking collectives  26.7 us (2%)
  matrix products  23 us (2%)
  between operations  16 us (1%)
    ppermute x73, waiting for transfers between devices, flip(): return lax.ppermute(values, 'dp', [(i, i ^ bit) for i in range(count)])  217 us
    pallas_call x12, Pallas kernels, turned_product(): pl.pallas_call(kernel, grid=(steps,), in_specs=[pl.BlockSpec((rows, tile)...  86.5 us
    pallas_call x10, Pallas kernels, times(): pl.pallas_call(kernel, grid=(columns // tile,), in_specs=[pl.BlockSpec((r...  85.7 us
    pallas_call x10, Pallas kernels, times_turned(): pl.pallas_call(kernel, grid=(rows // tile,), in_specs=[pl.BlockSpec((tile...  84.8 us
    ppermute x73, starting transfers between devices, flip(): return lax.ppermute(values, 'dp', [(i, i ^ bit) for i in range(count)])  52.3 us
    pallas_call x16, Pallas kernels, add_blocks(): pl.pallas_call(kernel, grid=(len(keep),), in_specs=[pl.BlockSpec(block, l...  46.8 us
    pallas_call x20, Pallas kernels, take_blocks(): pl.pallas_call(lambda half_ref, out_ref: out_ref.__setitem__(..., half_re...  46.1 us
    all_gather x8, waiting for transfers between devices, tensor_rows(): return lax.all_gather(values, 'tensor', axis=0, tiled=True)  38.4 us
  transfers between devices with their start and end apart: 98, of which 36 were waited for; matrix products, arithmetic and copies ran while one was open for 14% of the time, Pallas kernels for 39%

profile of v4, /device:TPU:0, one launch (start us, length us, event | category | flops | bytes accessed | tf_op | source)
XLA Modules:
  0.0 1098.4 jit_solution(10153590101917792965)
XLA Ops:
  14.1 5.3 all-to-all-start.1
  20.3 11.7 %all-to-all-done.1 = bf16[8,24,2048]{2,1,0:T(8,128)(2,1)S(1)} async-done(((bf16[8,24,2048]{2,1,0:T(8,128)(2,1)}), bf16[8,24,2048]{2,1,0:T(8,128)(2,1)S(1)}, u32[]{:S(2)}, u32[]{:S(2)}) %all-to-all-start.1) | async-done | bytes 786464 | tf_op jit(solution)/shard_map/all_to_all | solution.py:741
  39.1 4.8 reorder.2
  46.7 5.4 all-to-all-done
  58.2 10.8 collective-permute-done.1
  83.1 6.5 place_rows.5.values_ref
  89.6 7.5 collective-permute-done.2.refs_1_
  103.2 6.4 place_rows.4.base_ref
  114.8 11.6 %all-gather.17.cloned.1.call-done = bf16[2240,512]{1,0:T(8,128)(2,1)} async-done(((bf16[560,512]{1,0:T(8,128)(2,1)}), bf16[2240,512]{1,0:T(8,128)(2,1)}) %all-gather.17.cloned.1.call-update) | async-done | bytes 2293776 | tf_op jit(solution)/shard_map/all_gather | solution.py:489
  137.4 4.7 times.11
  165.4 9.9 attend.2
  182.4 5.0 times_turned.10
  187.4 5.1 times_turned.11
  199.3 4.4 collective-permute-done.16
  211.8 41.8 %collective-permute-done.18.refs_1_ = bf16[512,2048]{1,0:T(8,128)(2,1)} collective-permute-done((bf16[512,2048]{1,0:T(8,128)(2,1)S(1)}, bf16[512,2048]{1,0:T(8,128)(2,1)}, u32[]{:S(2)}, u32[]{:S(2)}) %collective-permute-start.18) | collective-permute-done | bytes 2097184 | tf_op jit(solution)/shard_map/ppermute | solution.py:37
  274.6 13.5 %times.12 = (f32[768,2048]{1,0:T(8,128)}, bf16[768,2048]{1,0:T(8,128)(2,1)}) custom-call(bf16[768,2048]{1,0:T(8,128)(2,1)} %all-gather.15.cloned.1.call-done.left_ref, bf16[512,2048]{1,0:T(8,128)(2,1)} %copy-done.5, bf16[512,2048]{1,0:T(8,128)(2,1)} %collective-permute-done.18.refs_1_, bf16[512,2048]{1,0:T(8,128)(2,1)} %collective-permute-done.19.refs_2_, ...), custom_call_target="tpu_custom_call" | custom-call | flops 1 | bytes 1 | tf_op jit(solution)/shard_map/times/pallas_call | solution.py:436
  288.0 11.9 %times_turned.12 = bf16[768,2048]{1,0:T(8,128)(2,1)} custom-call(bf16[768,2048]{1,0:T(8,128)(2,1)} %get-tuple-element.161.left_ref.right_ref, bf16[512,2048]{1,0:T(8,128)(2,1)} %pad_maximum_fusion.2.refs_0_, bf16[512,2048]{1,0:T(8,128)(2,1)} %collective-permute-done.21.refs_1_, bf16[512,2048]{1,0:T(8,128)(2,1)} %collective-permute-done.22.refs_2_, ...), custom_call_target="tpu_custom_call" | custom-call | flops 1 | bytes 1 | tf_op jit(solution)/shard_map/times_turned/pallas_call | solution.py:469
  306.9 48.2 %collective-permute-done.26.refs_1_ = bf16[512,2304]{1,0:T(8,128)(2,1)} collective-permute-done((bf16[512,2304]{1,0:T(8,128)(2,1)S(1)}, bf16[512,2304]{1,0:T(8,128)(2,1)}, u32[]{:S(2)}, u32[]{:S(2)}) %collective-permute-start.26) | collective-permute-done | bytes 2359328 | tf_op jit(solution)/shard_map/ppermute | solution.py:37
  356.2 6.7 collective-permute-done.30.refs_2_
  369.9 7.3 times.13.refs_0_
  384.6 19.4 %all-to-all-done.3 = bf16[4,192,256]{2,1,0:T(8,128)(2,1)S(1)} async-done(((bf16[4,192,256]{2,1,0:T(8,128)(2,1)}), bf16[4,192,256]{2,1,0:T(8,128)(2,1)S(1)}, u32[]{:S(2)}, u32[]{:S(2)}) %all-to-all-start.3) | async-done | bytes 393248 | tf_op jit(solution)/shard_map/all_to_all | solution.py:485
  405.7 9.9 attend.3
  415.6 7.7 times_turned.13.refs_0_
  438.9 39.3 %collective-permute-done.34.refs_1_ = bf16[512,2048]{1,0:T(8,128)(2,1)} collective-permute-done((bf16[512,2048]{1,0:T(8,128)(2,1)}, bf16[512,2048]{1,0:T(8,128)(2,1)}, u32[]{:S(2)}, u32[]{:S(2)}) %collective-permute-start.34) | collective-permute-done | bytes 2097184 | tf_op jit(solution)/shard_map/ppermute | solution.py:37
  486.3 11.7 %times.14.refs_5_ = f32[768,2048]{1,0:T(8,128)} custom-call(bf16[768,2048]{1,0:T(8,128)(2,1)} %copy-done.3, bf16[512,2048]{1,0:T(8,128)(2,1)} %pad_maximum_fusion.5.refs_0_, bf16[512,2048]{1,0:T(8,128)(2,1)} %collective-permute-done.37.refs_1_, bf16[512,2048]{1,0:T(8,128)(2,1)} %collective-permute-done.38.refs_2_, ...), custom_call_target="tpu_custom_call" | custom-call | flops 1 | bytes 1 | tf_op jit(solution)/shard_map/times/pallas_call | solution.py:436
  498.0 15.6 %times.15 = (bf16[768,2048]{1,0:T(8,128)(2,1)}, bf16[768,2048]{1,0:T(8,128)(2,1)}) custom-call(bf16[768,2048]{1,0:T(8,128)(2,1)} %all-gather.19.cloned.1.call-done.left_ref, bf16[512,2048]{1,0:T(8,128)(2,1)} %pad_maximum_fusion.4.refs_0_, bf16[512,2048]{1,0:T(8,128)(2,1)} %collective-permute-done.34.refs_1_, ...), custom_call_target="tpu_custom_call" | custom-call | flops 1 | bytes 1 | tf_op jit(solution)/shard_map/times/pallas_call | solution.py:436
  513.6 11.9 %times_turned.14 = bf16[768,2048]{1,0:T(8,128)(2,1)} custom-call(bf16[768,2048]{1,0:T(8,128)(2,1)} %get-tuple-element.187.left_ref.right_ref.values_ref, bf16[512,2048]{1,0:T(8,128)(2,1)} %pad_maximum_fusion.4.refs_0_, bf16[512,2048]{1,0:T(8,128)(2,1)} %collective-permute-done.34.refs_1_, bf16[512,2048]{1,0:T(8,128)(2,1)} %collective-permute-done.35.refs_2_, ...), custom_call_target="tpu_custom_call" | custom-call | flops 1 | bytes 1 | tf_op jit(solution)/shard_map/times_turned/pallas_call | solution.py:469
  526.0 7.4 turned_product.12
  534.0 7.4 turned_product.14
  541.4 8.3 turned_product.13.half_ref
  549.7 8.3 turned_product.15.half_ref
  563.2 12.0 %times_turned.15 = bf16[768,2048]{1,0:T(8,128)(2,1)} custom-call(bf16[768,2048]{1,0:T(8,128)(2,1)} %get-tuple-element.190.right_ref.left_ref, bf16[512,2048]{1,0:T(8,128)(2,1)} %pad_maximum_fusion.5.refs_0_, bf16[512,2048]{1,0:T(8,128)(2,1)} %collective-permute-done.37.refs_1_, bf16[512,2048]{1,0:T(8,128)(2,1)} %collective-permute-done.38.refs_2_, ...), custom_call_target="tpu_custom_call" | custom-call | flops 1 | bytes 1 | tf_op jit(solution)/shard_map/times_turned/pallas_call | solution.py:469
  575.2 8.9 reduce-scatter.11.cloned.1.call-done.grad_ref
  588.5 4.8 norm_back.4
  593.2 6.5 times.16.refs_1_
  599.7 12.7 %attend_back.2 = (bf16[192,2048]{1,0:T(8,128)(2,1)}, f32[768,256]{1,0:T(8,128)}) custom-call(bf16[192,2304]{1,0:T(8,128)(2,1)} %times.13.refs_0_, bf16[192,2048]{1,0:T(8,128)(2,1)} %times.16.refs_1_, bf16[768,128]{1,0:T(8,128)(2,1)} %get-tuple-element.345.refs_1_.refs_2_, bf16[768,128]{1,0:T(8,128)(2,1)} %get-tuple-element.344.refs_3_, ...), custom_call_target="tpu_custom_call" | custom-call | flops 1 | bytes 1 | tf_op jit(solution)/shard_map/attend_back/pallas_call | solution.py:666
  613.6 26.7 %all_to_all.90 = bf16[4,192,256]{2,1,0:T(8,128)(2,1)S(1)} all-to-all(bf16[4,192,256]{2,1,0:T(8,128)(2,1)S(1)} %bitcast.93), channel_id=1, replica_groups=mesh['dp'=8,'tensor'=4] {'tensor'}, dimensions={0} | all-to-all | bytes 786432 | tf_op jit(solution)/shard_map/all_to_all | solution.py:485
  641.5 8.5 times_turned.16.grad_ref
  652.8 5.3 norm_back.5
  664.9 5.2 turned_product.16
  670.2 5.0 turned_product.18
  678.4 6.4 turned_product.17.half_ref
  689.1 5.9 turned_product.19.half_ref
  709.4 6.4 place_rows.6
  715.8 24.2 %all-gather.23.cloned.1.call-done.left_ref = bf16[768,2048]{1,0:T(8,128)(2,1)} async-done(((bf16[192,2048]{1,0:T(8,128)(2,1)}), bf16[768,2048]{1,0:T(8,128)(2,1)}) %all-gather.23.cloned.1.call-update) | async-done | bytes 3145744 | tf_op jit(solution)/shard_map/all_gather | solution.py:489
  740.1 14.2 %times.17.left_ref.right_ref.values_ref = bf16[768,2048]{1,0:T(8,128)(2,1)} custom-call(bf16[768,2048]{1,0:T(8,128)(2,1)} %all-gather.23.cloned.1.call-done.left_ref, bf16[512,2048]{1,0:T(8,128)(2,1)} %pad_maximum_fusion.2.refs_0_, bf16[512,2048]{1,0:T(8,128)(2,1)} %collective-permute-done.21.refs_1_, bf16[512,2048]{1,0:T(8,128)(2,1)} %collective-permute-done.22.refs_2_, ...), custom_call_target="tpu_custom_call" | custom-call | flops 1 | bytes 1 | tf_op jit(solution)/shard_map/times/pallas_call | solution.py:436
  754.3 12.0 %times_turned.17 = bf16[768,2048]{1,0:T(8,128)(2,1)} custom-call(bf16[768,2048]{1,0:T(8,128)(2,1)} %times.17.left_ref.right_ref.values_ref, bf16[512,2048]{1,0:T(8,128)(2,1)} %copy-done.5, bf16[512,2048]{1,0:T(8,128)(2,1)} %collective-permute-done.18.refs_1_, bf16[512,2048]{1,0:T(8,128)(2,1)} %collective-permute-done.19.refs_2_, ...), custom_call_target="tpu_custom_call" | custom-call | flops 1 | bytes 1 | tf_op jit(solution)/shard_map/times_turned/pallas_call | solution.py:469
  767.9 8.6 turned_product.20
  776.5 7.5 turned_product.22
  798.3 8.3 turned_product.21.half_ref
  806.5 8.3 turned_product.23.half_ref
  830.4 4.8 norm_back.6
  859.7 12.7 %attend_back.3 = (bf16[192,2048]{1,0:T(8,128)(2,1)}, f32[768,256]{1,0:T(8,128)}) custom-call(bf16[192,2304]{1,0:T(8,128)(2,1)} %pad_maximum_fusion.15.refs_0_, bf16[192,2048]{1,0:T(8,128)(2,1)} %pad_maximum_fusion.18.refs_1_, bf16[768,128]{1,0:T(8,128)(2,1)} %get-tuple-element.341.refs_1_.refs_2_, bf16[768,128]{1,0:T(8,128)(2,1)} %get-tuple-element.340.refs_3_, ...), custom_call_target="tpu_custom_call" | custom-call | flops 1 | bytes 1 | tf_op jit(solution)/shard_map/attend_back/pallas_call | solution.py:666
  874.3 4.5 all-to-all-start.6
  883.6 7.8 all-to-all-done.6
  965.3 4.9 times_turned.18
  970.2 5.8 times_turned.19
  978.7 5.2 norm_back.7
  983.9 7.1 collective-permute-done.74.come_ref
  1017.4 4.8 reorder.3
  1045.2 6.4 place_rows.7
  1057.5 13.7 %collective-permute-done.67 = f32[18,2048]{1,0:T(8,128)S(1)} collective-permute-done((f32[18,2048]{1,0:T(8,128)S(1)}, f32[18,2048]{1,0:T(8,128)S(1)}, u32[]{:S(2)}, u32[]{:S(2)}) %collective-permute-start.67) | collective-permute-done | bytes 147488 | tf_op jit(solution)/shard_map/ppermute | solution.py:37
  1074.1 4.4 stack_sums.2
  1078.5 4.8 stack_sums.3
  (617 shorter events, 423.0 us)
Async XLA Ops:
  7.2 44.9 %all-gather.9.cloned.1.call-start = ((), (), s32[]{:S(2)}) async-start(), calls=%async_computation.16 | async-start | bytes 1556480 | tf_op jit(solution)/shard_map/all_gather | solution.py:489
  19.4 60.0 %all-gather.11.cloned.1.call-start = ((), (), s32[]{:S(2)}) async-start(), calls=%async_computation.17 | async-start | bytes 1310720 | tf_op jit(solution)/shard_map/all_gather | solution.py:489
  39.0 87.4 %all-gather.17.cloned.1.call-start = ((), (), s32[]{:S(2)}) async-start(), calls=%async_computation.20 | async-start | bytes 2867200 | tf_op jit(solution)/shard_map/all_gather | solution.py:489
  69.1 32.1 %collective-permute-start.5 = (bf16[512,1280]{1,0:T(8,128)(2,1)S(1)}, bf16[512,1280]{1,0:T(8,128)(2,1)}, u32[]{:S(2)}, u32[]{:S(2)}) collective-permute-start(bf16[512,1280]{1,0:T(8,128)(2,1)S(1)} %pad_maximum_fusion.6.refs_0_), channel_id=1, source_target_pairs={{0,8},{4,12},{8,0},{12,4},{16,24},{20,28},{24,16},{28,20},{1,9},{5... | collective-permute-start | bytes 3932168 | tf_op jit(solution)/shard_map/ppermute | solution.py:37
  82.5 49.3 %collective-permute-start.3 = (bf16[512,1024]{1,0:T(8,128)(2,1)S(1)}, bf16[512,1024]{1,0:T(8,128)(2,1)}, u32[]{:S(2)}, u32[]{:S(2)}) collective-permute-start(bf16[512,1024]{1,0:T(8,128)(2,1)S(1)} %pad_maximum_fusion.8.refs_0_), channel_id=1, source_target_pairs={{0,4},{4,0},{8,12},{12,8},{16,20},{20,16},{24,28},{28,24},{1,5},{5... | collective-permute-start | bytes 3145736 | tf_op jit(solution)/shard_map/ppermute | solution.py:37
  82.6 54.8 %collective-permute-start.6 = (bf16[512,1280]{1,0:T(8,128)(2,1)S(1)}, bf16[512,1280]{1,0:T(8,128)(2,1)}, u32[]{:S(2)}, u32[]{:S(2)}) collective-permute-start(bf16[512,1280]{1,0:T(8,128)(2,1)S(1)} %pad_maximum_fusion.6.refs_0_), channel_id=1, source_target_pairs={{0,4},{4,0},{8,12},{12,8},{16,20},{20,16},{24,28},{28,24},{1,5},{5... | collective-permute-start | bytes 3932168 | tf_op jit(solution)/shard_map/ppermute | solution.py:37
  97.1 36.3 %collective-permute-start.4 = (bf16[512,1024]{1,0:T(8,128)(2,1)S(1)}, bf16[512,1024]{1,0:T(8,128)(2,1)}, u32[]{:S(2)}, u32[]{:S(2)}) collective-permute-start(bf16[512,1024]{1,0:T(8,128)(2,1)S(1)} %collective-permute-done.2.refs_1_), channel_id=1, source_target_pairs={{0,4},{4,0},{8,12},{12,8},{16,20},{20,16},{24,28},{28,24},{1,5},{5... | collective-permute-start | bytes 3145736 | tf_op jit(solution)/shard_map/ppermute | solution.py:37
  101.1 36.2 %collective-permute-start.7 = (bf16[512,1280]{1,0:T(8,128)(2,1)}, bf16[512,1280]{1,0:T(8,128)(2,1)}, u32[]{:S(2)}, u32[]{:S(2)}) collective-permute-start(bf16[512,1280]{1,0:T(8,128)(2,1)} %collective-permute-done.5.refs_1_), channel_id=1, source_target_pairs={{0,4},{4,0},{8,12},{12,8},{16,20},{20,16},{24,28},{28,24},{1,5},{5... | collective-permute-start | bytes 3932168 | tf_op jit(solution)/shard_map/ppermute | solution.py:37
  109.6 39.8 %collective-permute-start.8 = (bf16[256,1024]{1,0:T(8,128)(2,1)}, bf16[256,1024]{1,0:T(8,128)(2,1)}, u32[]{:S(2)}, u32[]{:S(2)}) collective-permute-start(bf16[256,1024]{1,0:T(8,128)(2,1)} %pad_maximum_fusion.21), channel_id=1, source_target_pairs={{0,8},{4,12},{8,0},{12,4},{16,24},{20,28},{24,16},{28,20},{1,9},{5... | collective-permute-start | bytes 1572872 | tf_op jit(solution)/shard_map/ppermute | solution.py:37
  147.3 57.4 %all-gather.13.cloned.1.call-start = ((), (), s32[]{:S(2)}) async-start(), calls=%async_computation.18 | async-start | bytes 1966080 | tf_op jit(solution)/shard_map/all_gather | solution.py:489
  150.6 28.8 %collective-permute-start.11 = (bf16[512,1024]{1,0:T(8,128)(2,1)S(1)}, bf16[512,1024]{1,0:T(8,128)(2,1)}, u32[]{:S(2)}, u32[]{:S(2)}) collective-permute-start(bf16[512,1024]{1,0:T(8,128)(2,1)S(1)} %pad_maximum_fusion.9.refs_0_), channel_id=1, source_target_pairs={{0,4},{4,0},{8,12},{12,8},{16,20},{20,16},{24,28},{28,24},{1,5},{5... | collective-permute-start | bytes 3145736 | tf_op jit(solution)/shard_map/ppermute | solution.py:37
  150.7 25.7 %collective-permute-start.10 = (bf16[512,1024]{1,0:T(8,128)(2,1)S(1)}, bf16[512,1024]{1,0:T(8,128)(2,1)}, u32[]{:S(2)}, u32[]{:S(2)}) collective-permute-start(bf16[512,1024]{1,0:T(8,128)(2,1)S(1)} %pad_maximum_fusion.9.refs_0_), channel_id=1, source_target_pairs={{0,16},{4,20},{8,24},{12,28},{16,0},{20,4},{24,8},{28,12},{1,17},{... | collective-permute-start | bytes 3145736 | tf_op jit(solution)/shard_map/ppermute | solution.py:37
  152.4 25.4 %collective-permute-start.13 = (bf16[512,1024]{1,0:T(8,128)(2,1)S(1)}, bf16[512,1024]{1,0:T(8,128)(2,1)}, u32[]{:S(2)}, u32[]{:S(2)}) collective-permute-start(bf16[512,1024]{1,0:T(8,128)(2,1)S(1)} %pad_maximum_fusion.10.refs_0_), channel_id=1, source_target_pairs={{0,8},{4,12},{8,0},{12,4},{16,24},{20,28},{24,16},{28,20},{1,9},{5... | collective-permute-start | bytes 3145736 | tf_op jit(solution)/shard_map/ppermute | solution.py:37
  154.0 114.8 %all-gather.15.cloned.1.call-start = ((), (), s32[]{:S(2)}) async-start(), calls=%async_computation.19 | async-start | bytes 3932160 | tf_op jit(solution)/shard_map/all_gather | solution.py:489
  162.0 25.4 %collective-permute-start.14 = (bf16[512,1024]{1,0:T(8,128)(2,1)S(1)}, bf16[512,1024]{1,0:T(8,128)(2,1)}, u32[]{:S(2)}, u32[]{:S(2)}) collective-permute-start(bf16[512,1024]{1,0:T(8,128)(2,1)S(1)} %pad_maximum_fusion.10.refs_0_), channel_id=1, source_target_pairs={{0,4},{4,0},{8,12},{12,8},{16,20},{20,16},{24,28},{28,24},{1,5},{5... | collective-permute-start | bytes 3145736 | tf_op jit(solution)/shard_map/ppermute | solution.py:37
  177.8 25.9 %collective-permute-start.16 = (bf16[256,2048]{1,0:T(8,128)(2,1)}, bf16[256,2048]{1,0:T(8,128)(2,1)}, u32[]{:S(2)}, u32[]{:S(2)}) collective-permute-start(bf16[256,2048]{1,0:T(8,128)(2,1)} %get-tuple-element.151), channel_id=1, source_target_pairs={{0,8},{4,12},{8,0},{12,4},{16,24},{20,28},{24,16},{28,20},{1,9},{5... | collective-permute-start | bytes 3145736 | tf_op jit(solution)/shard_map/ppermute | solution.py:37
  179.3 25.4 %collective-permute-start.17 = (bf16[256,2048]{1,0:T(8,128)(2,1)S(1)}, bf16[256,2048]{1,0:T(8,128)(2,1)}, u32[]{:S(2)}, u32[]{:S(2)}) collective-permute-start(bf16[256,2048]{1,0:T(8,128)(2,1)S(1)} %bitcast.77), channel_id=1, source_target_pairs={{0,16},{4,20},{8,24},{12,28},{16,0},{20,4},{24,8},{28,12},{1,17},{... | collective-permute-start | bytes 3145736 | tf_op jit(solution)/shard_map/ppermute | solution.py:37
  204.8 161.2 %reduce-scatter.9.cloned.1.call-start = ((), (), s32[]{:S(2)}) async-start(), calls=%async_computation.21 | async-start | bytes 3932160 | tf_op jit(solution)/shard_map/reduce_scatter | solution.py:493
  206.5 47.1 %collective-permute-start.18 = (bf16[512,2048]{1,0:T(8,128)(2,1)S(1)}, bf16[512,2048]{1,0:T(8,128)(2,1)}, u32[]{:S(2)}, u32[]{:S(2)}) collective-permute-start(bf16[512,2048]{1,0:T(8,128)(2,1)S(1)} %pad_maximum_fusion.1.refs_0_), channel_id=1, source_target_pairs={{0,16},{4,20},{8,24},{12,28},{16,0},{20,4},{24,8},{28,12},{1,17},{... | collective-permute-start | bytes 6291464 | tf_op jit(solution)/shard_map/ppermute | solution.py:37
  210.3 47.0 %collective-permute-start.21 = (bf16[512,2048]{1,0:T(8,128)(2,1)}, bf16[512,2048]{1,0:T(8,128)(2,1)}, u32[]{:S(2)}, u32[]{:S(2)}) collective-permute-start(bf16[512,2048]{1,0:T(8,128)(2,1)} %pad_maximum_fusion.2.refs_0_), channel_id=1, source_target_pairs={{0,8},{4,12},{8,0},{12,4},{16,24},{20,28},{24,16},{28,20},{1,9},{5... | collective-permute-start | bytes 6291464 | tf_op jit(solution)/shard_map/ppermute | solution.py:37
  211.3 54.9 %collective-permute-start.19 = (bf16[512,2048]{1,0:T(8,128)(2,1)S(1)}, bf16[512,2048]{1,0:T(8,128)(2,1)}, u32[]{:S(2)}, u32[]{:S(2)}) collective-permute-start(bf16[512,2048]{1,0:T(8,128)(2,1)S(1)} %pad_maximum_fusion.1.refs_0_), channel_id=1, source_target_pairs={{0,4},{4,0},{8,12},{12,8},{16,20},{20,16},{24,28},{28,24},{1,5},{5... | collective-permute-start | bytes 6291464 | tf_op jit(solution)/shard_map/ppermute | solution.py:37
  211.3 54.9 %collective-permute-start.22 = (bf16[512,2048]{1,0:T(8,128)(2,1)}, bf16[512,2048]{1,0:T(8,128)(2,1)}, u32[]{:S(2)}, u32[]{:S(2)}) collective-permute-start(bf16[512,2048]{1,0:T(8,128)(2,1)} %pad_maximum_fusion.2.refs_0_), channel_id=1, source_target_pairs={{0,4},{4,0},{8,12},{12,8},{16,20},{20,16},{24,28},{28,24},{1,5},{5... | collective-permute-start | bytes 6291464 | tf_op jit(solution)/shard_map/ppermute | solution.py:37
  268.8 31.1 %collective-permute-start.24 = (bf16[256,2304]{1,0:T(8,128)(2,1)S(1)}, bf16[256,2304]{1,0:T(8,128)(2,1)S(1)}, u32[]{:S(2)}, u32[]{:S(2)}) collective-permute-start(bf16[256,2304]{1,0:T(8,128)(2,1)S(1)} %concatenate.130), channel_id=1, source_target_pairs={{0,8},{4,12},{8,0},{12,4},{16,24},{20,28},{24,16},{28,20},{1,9},{5... | collective-permute-start | bytes 3538952 | tf_op jit(solution)/shard_map/ppermute | solution.py:37
  272.5 27.5 %collective-permute-start.25 = (bf16[256,2048]{1,0:T(8,128)(2,1)}, bf16[256,2048]{1,0:T(8,128)(2,1)}, u32[]{:S(2)}, u32[]{:S(2)}) collective-permute-start(bf16[256,2048]{1,0:T(8,128)(2,1)} %pad_maximum_fusion.11), channel_id=1, source_target_pairs={{0,16},{4,20},{8,24},{12,28},{16,0},{20,4},{24,8},{28,12},{1,17},{... | collective-permute-start | bytes 3145736 | tf_op jit(solution)/shard_map/ppermute | solution.py:37
  301.0 135.2 %all-gather.21.cloned.1.call-start = ((), (), s32[]{:S(2)}) async-start(), calls=%async_computation.23 | async-start | bytes 1966080 | tf_op jit(solution)/shard_map/all_gather | solution.py:489
  302.5 52.6 %collective-permute-start.26 = (bf16[512,2304]{1,0:T(8,128)(2,1)S(1)}, bf16[512,2304]{1,0:T(8,128)(2,1)}, u32[]{:S(2)}, u32[]{:S(2)}) collective-permute-start(bf16[512,2304]{1,0:T(8,128)(2,1)S(1)} %pad_maximum_fusion.refs_0_), channel_id=1, source_target_pairs={{0,16},{4,20},{8,24},{12,28},{16,0},{20,4},{24,8},{28,12},{1,17},{... | collective-permute-start | bytes 7077896 | tf_op jit(solution)/shard_map/ppermute | solution.py:37
  306.5 49.1 %collective-permute-start.29 = (bf16[512,2048]{1,0:T(8,128)(2,1)}, bf16[512,2048]{1,0:T(8,128)(2,1)}, u32[]{:S(2)}, u32[]{:S(2)}) collective-permute-start(bf16[512,2048]{1,0:T(8,128)(2,1)} %pad_maximum_fusion.3.refs_0_), channel_id=1, source_target_pairs={{0,8},{4,12},{8,0},{12,4},{16,24},{20,28},{24,16},{28,20},{1,9},{5... | collective-permute-start | bytes 6291464 | tf_op jit(solution)/shard_map/ppermute | solution.py:37
  306.9 56.1 %collective-permute-start.27 = (bf16[512,2304]{1,0:T(8,128)(2,1)S(1)}, bf16[512,2304]{1,0:T(8,128)(2,1)}, u32[]{:S(2)}, u32[]{:S(2)}) collective-permute-start(bf16[512,2304]{1,0:T(8,128)(2,1)S(1)} %pad_maximum_fusion.refs_0_), channel_id=1, source_target_pairs={{0,4},{4,0},{8,12},{12,8},{16,20},{20,16},{24,28},{28,24},{1,5},{5... | collective-permute-start | bytes 7077896 | tf_op jit(solution)/shard_map/ppermute | solution.py:37
  379.0 24.9 %all-to-all-start.3 = ((bf16[4,192,256]{2,1,0:T(8,128)(2,1)}), bf16[4,192,256]{2,1,0:T(8,128)(2,1)S(1)}, u32[]{:S(2)}, u32[]{:S(2)}) async-start(bf16[4,192,256]{2,1,0:T(8,128)(2,1)} %bitcast.31), calls=%async_computation.4 | async-start | bytes 786432 | tf_op jit(solution)/shard_map/all_to_all | solution.py:485
  382.5 115.5 %all-gather.19.cloned.1.call-start = ((), (), s32[]{:S(2)}) async-start(), calls=%async_computation.22 | async-start | bytes 3932160 | tf_op jit(solution)/shard_map/all_gather | solution.py:489
  383.4 32.2 %collective-permute-start.32 = (bf16[256,2048]{1,0:T(8,128)(2,1)S(1)}, bf16[256,2048]{1,0:T(8,128)(2,1)}, u32[]{:S(2)}, u32[]{:S(2)}) collective-permute-start(bf16[256,2048]{1,0:T(8,128)(2,1)S(1)} %copy-done.23), channel_id=1, source_target_pairs={{0,8},{4,12},{8,0},{12,4},{16,24},{20,28},{24,16},{28,20},{1,9},{5... | collective-permute-start | bytes 3145736 | tf_op jit(solution)/shard_map/ppermute | solution.py:37
  384.1 31.6 %collective-permute-start.33 = (bf16[256,2048]{1,0:T(8,128)(2,1)S(1)}, bf16[256,2048]{1,0:T(8,128)(2,1)}, u32[]{:S(2)}, u32[]{:S(2)}) collective-permute-start(bf16[256,2048]{1,0:T(8,128)(2,1)S(1)} %bitcast.79), channel_id=1, source_target_pairs={{0,16},{4,20},{8,24},{12,28},{16,0},{20,4},{24,8},{28,12},{1,17},{... | collective-permute-start | bytes 3145736 | tf_op jit(solution)/shard_map/ppermute | solution.py:37
  427.5 156.6 %reduce-scatter.11.cloned.1.call-start = ((), (), s32[]{:S(2)}) async-start(), calls=%async_computation.24 | async-start | bytes 3932160 | tf_op jit(solution)/shard_map/reduce_scatter | solution.py:493
  430.3 48.0 %collective-permute-start.34 = (bf16[512,2048]{1,0:T(8,128)(2,1)}, bf16[512,2048]{1,0:T(8,128)(2,1)}, u32[]{:S(2)}, u32[]{:S(2)}) collective-permute-start(bf16[512,2048]{1,0:T(8,128)(2,1)} %pad_maximum_fusion.4.refs_0_), channel_id=1, source_target_pairs={{0,16},{4,20},{8,24},{12,28},{16,0},{20,4},{24,8},{28,12},{1,17},{... | collective-permute-start | bytes 6291464 | tf_op jit(solution)/shard_map/ppermute | solution.py:37
  434.3 47.1 %collective-permute-start.37 = (bf16[512,2048]{1,0:T(8,128)(2,1)}, bf16[512,2048]{1,0:T(8,128)(2,1)}, u32[]{:S(2)}, u32[]{:S(2)}) collective-permute-start(bf16[512,2048]{1,0:T(8,128)(2,1)} %pad_maximum_fusion.5.refs_0_), channel_id=1, source_target_pairs={{0,8},{4,12},{8,0},{12,4},{16,24},{20,28},{24,16},{28,20},{1,9},{5... | collective-permute-start | bytes 6291464 | tf_op jit(solution)/shard_map/ppermute | solution.py:37
  438.4 59.6 %collective-permute-start.35 = (bf16[512,2048]{1,0:T(8,128)(2,1)}, bf16[512,2048]{1,0:T(8,128)(2,1)}, u32[]{:S(2)}, u32[]{:S(2)}) collective-permute-start(bf16[512,2048]{1,0:T(8,128)(2,1)} %pad_maximum_fusion.4.refs_0_), channel_id=1, source_target_pairs={{0,4},{4,0},{8,12},{12,8},{16,20},{20,16},{24,28},{28,24},{1,5},{5... | collective-permute-start | bytes 6291464 | tf_op jit(solution)/shard_map/ppermute | solution.py:37
  438.4 46.2 %collective-permute-start.38 = (bf16[512,2048]{1,0:T(8,128)(2,1)}, bf16[512,2048]{1,0:T(8,128)(2,1)}, u32[]{:S(2)}, u32[]{:S(2)}) collective-permute-start(bf16[512,2048]{1,0:T(8,128)(2,1)} %pad_maximum_fusion.5.refs_0_), channel_id=1, source_target_pairs={{0,4},{4,0},{8,12},{12,8},{16,20},{20,16},{24,28},{28,24},{1,5},{5... | collective-permute-start | bytes 6291464 | tf_op jit(solution)/shard_map/ppermute | solution.py:37
  525.6 127.2 %reduce-scatter.13.cloned.1.call-start = ((), (), s32[]{:S(2)}) async-start(), calls=%async_computation.25 | async-start | bytes 3932160 | tf_op jit(solution)/shard_map/reduce_scatter | solution.py:493
  584.2 155.9 %all-gather.23.cloned.1.call-start = ((), (), s32[]{:S(2)}) async-start(), calls=%async_computation.26 | async-start | bytes 3932160 | tf_op jit(solution)/shard_map/all_gather | solution.py:489
  584.2 57.3 %collective-permute-start.42 = (bf16[512,2048]{1,0:T(8,128)(2,1)}, bf16[512,2048]{1,0:T(8,128)(2,1)}, u32[]{:S(2)}, u32[]{:S(2)}) collective-permute-start(bf16[512,2048]{1,0:T(8,128)(2,1)} %take_blocks.20), channel_id=1, source_target_pairs={{0,8},{4,12},{8,0},{12,4},{16,24},{20,28},{24,16},{28,20},{1,9},{5... | collective-permute-start | bytes 6291464 | tf_op jit(solution)/shard_map/ppermute | solution.py:37
  585.7 55.8 %collective-permute-start.43 = (bf16[512,2048]{1,0:T(8,128)(2,1)}, bf16[512,2048]{1,0:T(8,128)(2,1)}, u32[]{:S(2)}, u32[]{:S(2)}) collective-permute-start(bf16[512,2048]{1,0:T(8,128)(2,1)} %take_blocks.21), channel_id=1, source_target_pairs={{0,16},{4,20},{8,24},{12,28},{16,0},{20,4},{24,8},{28,12},{1,17},{... | collective-permute-start | bytes 6291464 | tf_op jit(solution)/shard_map/ppermute | solution.py:37
  675.6 154.7 %reduce-scatter.15.cloned.1.call-start = ((), (), s32[]{:S(2)}) async-start(), calls=%async_computation.27 | async-start | bytes 3932160 | tf_op jit(solution)/shard_map/reduce_scatter | solution.py:493
  687.7 80.1 %collective-permute-start.48 = (bf16[512,2304]{1,0:T(8,128)(2,1)}, bf16[512,2304]{1,0:T(8,128)(2,1)S(1)}, u32[]{:S(2)}, u32[]{:S(2)}) collective-permute-start(bf16[512,2304]{1,0:T(8,128)(2,1)} %take_blocks.24), channel_id=1, source_target_pairs={{0,8},{4,12},{8,0},{12,4},{16,24},{20,28},{24,16},{28,20},{1,9},{5... | collective-permute-start | bytes 7077896 | tf_op jit(solution)/shard_map/ppermute | solution.py:37
  697.7 70.1 %collective-permute-start.49 = (bf16[512,2048]{1,0:T(8,128)(2,1)}, bf16[512,2048]{1,0:T(8,128)(2,1)}, u32[]{:S(2)}, u32[]{:S(2)}) collective-permute-start(bf16[512,2048]{1,0:T(8,128)(2,1)} %take_blocks.25), channel_id=1, source_target_pairs={{0,16},{4,20},{8,24},{12,28},{16,0},{20,4},{24,8},{28,12},{1,17},{... | collective-permute-start | bytes 6291464 | tf_op jit(solution)/shard_map/ppermute | solution.py:37
  701.5 66.3 %collective-permute-start.46 = (bf16[256,2048]{1,0:T(8,128)(2,1)}, bf16[256,2048]{1,0:T(8,128)(2,1)S(1)}, u32[]{:S(2)}, u32[]{:S(2)}) collective-permute-start(bf16[256,2048]{1,0:T(8,128)(2,1)} %take_blocks.22), channel_id=1, source_target_pairs={{0,16},{4,20},{8,24},{12,28},{16,0},{20,4},{24,8},{28,12},{1,17},{... | collective-permute-start | bytes 3145736 | tf_op jit(solution)/shard_map/ppermute | solution.py:37
  704.3 63.5 %collective-permute-start.47 = (bf16[256,2048]{1,0:T(8,128)(2,1)}, bf16[256,2048]{1,0:T(8,128)(2,1)}, u32[]{:S(2)}, u32[]{:S(2)}) collective-permute-start(bf16[256,2048]{1,0:T(8,128)(2,1)} %take_blocks.23), channel_id=1, source_target_pairs={{0,8},{4,12},{8,0},{12,4},{16,24},{20,28},{24,16},{28,20},{1,9},{5... | collective-permute-start | bytes 3145736 | tf_op jit(solution)/shard_map/ppermute | solution.py:37
  790.5 32.3 %collective-permute-start.52 = (bf16[256,2304]{1,0:T(8,128)(2,1)}, bf16[256,2304]{1,0:T(8,128)(2,1)S(1)}, u32[]{:S(2)}, u32[]{:S(2)}) collective-permute-start(bf16[256,2304]{1,0:T(8,128)(2,1)} %take_blocks.26), channel_id=1, source_target_pairs={{0,16},{4,20},{8,24},{12,28},{16,0},{20,4},{24,8},{28,12},{1,17},{... | collective-permute-start | bytes 3538952 | tf_op jit(solution)/shard_map/ppermute | solution.py:37
  797.8 25.0 %collective-permute-start.53 = (bf16[256,2048]{1,0:T(8,128)(2,1)}, bf16[256,2048]{1,0:T(8,128)(2,1)S(1)}, u32[]{:S(2)}, u32[]{:S(2)}) collective-permute-start(bf16[256,2048]{1,0:T(8,128)(2,1)} %take_blocks.27), channel_id=1, source_target_pairs={{0,8},{4,12},{8,0},{12,4},{16,24},{20,28},{24,16},{28,20},{1,9},{5... | collective-permute-start | bytes 3145736 | tf_op jit(solution)/shard_map/ppermute | solution.py:37
  847.6 47.9 %collective-permute-start.56 = (bf16[512,2048]{1,0:T(8,128)(2,1)}, bf16[512,2048]{1,0:T(8,128)(2,1)}, u32[]{:S(2)}, u32[]{:S(2)}) collective-permute-start(bf16[512,2048]{1,0:T(8,128)(2,1)} %take_blocks.28), channel_id=1, source_target_pairs={{0,8},{4,12},{8,0},{12,4},{16,24},{20,28},{24,16},{28,20},{1,9},{5... | collective-permute-start | bytes 6291464 | tf_op jit(solution)/shard_map/ppermute | solution.py:37
  848.1 47.6 %collective-permute-start.57 = (bf16[512,2048]{1,0:T(8,128)(2,1)}, bf16[512,2048]{1,0:T(8,128)(2,1)}, u32[]{:S(2)}, u32[]{:S(2)}) collective-permute-start(bf16[512,2048]{1,0:T(8,128)(2,1)} %take_blocks.29), channel_id=1, source_target_pairs={{0,16},{4,20},{8,24},{12,28},{16,0},{20,4},{24,8},{28,12},{1,17},{... | collective-permute-start | bytes 6291464 | tf_op jit(solution)/shard_map/ppermute | solution.py:37
  878.8 164.5 %reduce-scatter.19.cloned.1.call-start = ((), (), s32[]{:S(2)}) async-start(), calls=%async_computation.29 | async-start | bytes 1474560 | tf_op jit(solution)/shard_map/reduce_scatter | solution.py:493
  899.5 185.6 %reduce-scatter.23.cloned.1.call-start = ((), (), s32[]{:S(2)}) async-start(), calls=%async_computation.31 | async-start | bytes 1310720 | tf_op jit(solution)/shard_map/reduce_scatter | solution.py:493
  910.0 39.0 %collective-permute-start.60 = (bf16[512,1024]{1,0:T(8,128)(2,1)}, bf16[512,1024]{1,0:T(8,128)(2,1)}, u32[]{:S(2)}, u32[]{:S(2)}) collective-permute-start(bf16[512,1024]{1,0:T(8,128)(2,1)} %take_blocks.30), channel_id=1, source_target_pairs={{0,8},{4,12},{8,0},{12,4},{16,24},{20,28},{24,16},{28,20},{1,9},{5... | collective-permute-start | bytes 3145736 | tf_op jit(solution)/shard_map/ppermute | solution.py:37
  911.6 37.5 %collective-permute-start.61 = (bf16[512,1024]{1,0:T(8,128)(2,1)S(1)}, bf16[512,1024]{1,0:T(8,128)(2,1)}, u32[]{:S(2)}, u32[]{:S(2)}) collective-permute-start(bf16[512,1024]{1,0:T(8,128)(2,1)S(1)} %copy-done.51), channel_id=1, source_target_pairs={{0,16},{4,20},{8,24},{12,28},{16,0},{20,4},{24,8},{28,12},{1,17},{... | collective-permute-start | bytes 3145736 | tf_op jit(solution)/shard_map/ppermute | solution.py:37
  925.1 73.5 %collective-permute-start.70 = (bf16[512,1280]{1,0:T(8,128)(2,1)}, bf16[512,1280]{1,0:T(8,128)(2,1)}, u32[]{:S(2)}, u32[]{:S(2)}) collective-permute-start(bf16[512,1280]{1,0:T(8,128)(2,1)} %take_blocks.33), channel_id=1, source_target_pairs={{0,16},{4,20},{8,24},{12,28},{16,0},{20,4},{24,8},{28,12},{1,17},{... | collective-permute-start | bytes 3932168 | tf_op jit(solution)/shard_map/ppermute | solution.py:37
  937.1 86.2 %all-to-all-start.5 = ((bf16[8,24,2048]{2,1,0:T(8,128)(2,1)}), bf16[8,24,2048]{2,1,0:T(8,128)(2,1)S(1)}, u32[]{:S(2)}, u32[]{:S(2)}) async-start(bf16[8,24,2048]{2,1,0:T(8,128)(2,1)} %bitcast.40), calls=%async_computation.8 | async-start | bytes 1572864 | tf_op jit(solution)/shard_map/all_to_all | solution.py:858
  940.7 144.5 %reduce-scatter.21.cloned.1.call-start = ((), (), s32[]{:S(2)}) async-start(), calls=%async_computation.30 | async-start | bytes 1310720 | tf_op jit(solution)/shard_map/reduce_scatter | solution.py:493
  954.0 44.7 %collective-permute-start.69 = (bf16[512,1024]{1,0:T(8,128)(2,1)}, bf16[512,1024]{1,0:T(8,128)(2,1)}, u32[]{:S(2)}, u32[]{:S(2)}) collective-permute-start(bf16[512,1024]{1,0:T(8,128)(2,1)} %take_blocks.32), channel_id=1, source_target_pairs={{0,8},{4,12},{8,0},{12,4},{16,24},{20,28},{24,16},{28,20},{1,9},{5... | collective-permute-start | bytes 3145736 | tf_op jit(solution)/shard_map/ppermute | solution.py:37
  959.7 31.3 %collective-permute-start.74 = (bf16[256,1024]{1,0:T(8,128)(2,1)}, bf16[256,1024]{1,0:T(8,128)(2,1)}, u32[]{:S(2)}, u32[]{:S(2)}) collective-permute-start(bf16[256,1024]{1,0:T(8,128)(2,1)} %take_blocks.37), channel_id=1, source_target_pairs={{0,8},{4,12},{8,0},{12,4},{16,24},{20,28},{24,16},{28,20},{1,9},{5... | collective-permute-start | bytes 1572872 | tf_op jit(solution)/shard_map/ppermute | solution.py:37
  959.9 32.8 %collective-permute-start.73 = (bf16[256,1024]{1,0:T(8,128)(2,1)}, bf16[256,1024]{1,0:T(8,128)(2,1)}, u32[]{:S(2)}, u32[]{:S(2)}) collective-permute-start(bf16[256,1024]{1,0:T(8,128)(2,1)} %take_blocks.36), channel_id=1, source_target_pairs={{0,16},{4,20},{8,24},{12,28},{16,0},{20,4},{24,8},{28,12},{1,17},{... | collective-permute-start | bytes 1572872 | tf_op jit(solution)/shard_map/ppermute | solution.py:37
  965.1 48.2 %collective-permute-start.62 = (bf16[256,2048]{1,0:T(8,128)(2,1)}, bf16[256,2048]{1,0:T(8,128)(2,1)S(1)}, u32[]{:S(2)}, u32[]{:S(2)}) collective-permute-start(bf16[256,2048]{1,0:T(8,128)(2,1)} %take_blocks.34), channel_id=1, source_target_pairs={{0,16},{4,20},{8,24},{12,28},{16,0},{20,4},{24,8},{28,12},{1,17},{... | collective-permute-start | bytes 3145736 | tf_op jit(solution)/shard_map/ppermute | solution.py:37
  991.0 26.4 %collective-permute-start.63 = (bf16[256,2048]{1,0:T(8,128)(2,1)}, bf16[256,2048]{1,0:T(8,128)(2,1)}, u32[]{:S(2)}, u32[]{:S(2)}) collective-permute-start(bf16[256,2048]{1,0:T(8,128)(2,1)} %take_blocks.35), channel_id=1, source_target_pairs={{0,8},{4,12},{8,0},{12,4},{16,24},{20,28},{24,16},{28,20},{1,9},{5... | collective-permute-start | bytes 3145736 | tf_op jit(solution)/shard_map/ppermute | solution.py:37
  1003.4 26.6 %collective-permute-start.72 = (bf16[256,1280]{1,0:T(8,128)(2,1)}, bf16[256,1280]{1,0:T(8,128)(2,1)}, u32[]{:S(2)}, u32[]{:S(2)}) collective-permute-start(bf16[256,1280]{1,0:T(8,128)(2,1)} %take_blocks.39), channel_id=1, source_target_pairs={{0,8},{4,12},{8,0},{12,4},{16,24},{20,28},{24,16},{28,20},{1,9},{5... | collective-permute-start | bytes 1966088 | tf_op jit(solution)/shard_map/ppermute | solution.py:37
  1007.3 80.3 %reduce-scatter.17.cloned.1.call-start = ((), (), s32[]{:S(2)}) async-start(), calls=%async_computation.28 | async-start | bytes 1474560 | tf_op jit(solution)/shard_map/reduce_scatter | solution.py:493
  (118 other events, 1248.1 us)
Sparse Core Ops, SparseCore 0:
  11.8 34.2 all-gather.8
  48.3 26.9 all-gather.10
  77.4 48.9 all-gather.16
  154.2 37.4 all-gather.12
  204.9 63.8 all-gather.14
  300.1 57.2 reduce-scatter.8
  359.0 45.5 all-gather.20
  427.6 61.4 all-gather.18
  525.7 58.3 reduce-scatter.10
  586.3 66.4 reduce-scatter.12
  675.8 64.2 all-gather.22
  768.0 60.2 reduce-scatter.14
  899.6 29.3 reduce-scatter.18
  931.2 25.8 reduce-scatter.22
  1007.4 31.1 reduce-scatter.20
  1040.7 28.1 reduce-scatter.16

commit v5 on v4

--- a/solution.py
+++ b/solution.py
@@ -875,7 +875,7 @@
             out_gather.settle(projected).send(projected)
             if last > 0:
                 branch_early = tensor_rows(after(last_branch[:early_rows], projected))
-            ff_gather = Gather([up_weight[0]], [down_turned[0]]).send(pair_all)
+            ff_gather = Gather([up_weight[0]], [down_turned[0]]).send(projected)
         mixed, log_totals = attend(
             queries, width, pair_all[:, :HEAD], pair_t[HEAD:], score_bias, score_scale
         )

time: 1110 us -> 1110 us (level)
  no operation moved by 1% of the time
where the time goes in v5:
time: 1110 us; the launch traced here: 1100 us
  Pallas kernels  488 us (44%)
  waiting for transfers between devices  312 us (28%)
  starting transfers between devices  88.2 us (8%)
  local copies, waits for them, and re-layouts  85.7 us (8%)
  other arithmetic  59 us (5%)
  blocking collectives  26.7 us (2%)
  matrix products  23 us (2%)
  between operations  16 us (1%)
    ppermute x73, waiting for transfers between devices, flip(): return lax.ppermute(values, 'dp', [(i, i ^ bit) for i in range(count)])  217 us
    pallas_call x12, Pallas kernels, turned_product(): pl.pallas_call(kernel, grid=(steps,), in_specs=[pl.BlockSpec((rows, tile)...  86.5 us
    pallas_call x10, Pallas kernels, times(): pl.pallas_call(kernel, grid=(columns // tile,), in_specs=[pl.BlockSpec((r...  85.7 us
    pallas_call x10, Pallas kernels, times_turned(): pl.pallas_call(kernel, grid=(rows // tile,), in_specs=[pl.BlockSpec((tile...  84.8 us
    ppermute x73, starting transfers between devices, flip(): return lax.ppermute(values, 'dp', [(i, i ^ bit) for i in range(count)])  52.3 us
    pallas_call x16, Pallas kernels, add_blocks(): pl.pallas_call(kernel, grid=(len(keep),), in_specs=[pl.BlockSpec(block, l...  46.8 us
    pallas_call x20, Pallas kernels, take_blocks(): pl.pallas_call(lambda half_ref, out_ref: out_ref.__setitem__(..., half_re...  46.1 us
    all_gather x8, waiting for transfers between devices, tensor_rows(): return lax.all_gather(values, 'tensor', axis=0, tiled=True)  38.4 us
  transfers between devices with their start and end apart: 98, of which 36 were waited for; matrix products, arithmetic and copies ran while one was open for 14% of the time, Pallas kernels for 39%

profile of v5, /device:TPU:0, one launch (start us, length us, event | category | flops | bytes accessed | tf_op | source)
XLA Modules:
  0.0 1098.4 jit_solution(10153590101917792965)
XLA Ops:
  14.1 5.3 all-to-all-start.1
  20.3 11.7 %all-to-all-done.1 = bf16[8,24,2048]{2,1,0:T(8,128)(2,1)S(1)} async-done(((bf16[8,24,2048]{2,1,0:T(8,128)(2,1)}), bf16[8,24,2048]{2,1,0:T(8,128)(2,1)S(1)}, u32[]{:S(2)}, u32[]{:S(2)}) %all-to-all-start.1) | async-done | bytes 786464 | tf_op jit(solution)/shard_map/all_to_all | solution.py:741
  39.1 4.8 reorder.2
  46.7 5.4 all-to-all-done
  58.2 10.8 collective-permute-done.1
  83.1 6.5 place_rows.5.values_ref
  89.6 7.5 collective-permute-done.2.refs_1_
  103.2 6.4 place_rows.4.base_ref
  114.8 11.6 %all-gather.17.cloned.1.call-done = bf16[2240,512]{1,0:T(8,128)(2,1)} async-done(((bf16[560,512]{1,0:T(8,128)(2,1)}), bf16[2240,512]{1,0:T(8,128)(2,1)}) %all-gather.17.cloned.1.call-update) | async-done | bytes 2293776 | tf_op jit(solution)/shard_map/all_gather | solution.py:489
  137.4 4.7 times.11
  165.4 9.9 attend.2
  182.4 5.0 times_turned.10
  187.4 5.1 times_turned.11
  199.3 4.4 collective-permute-done.16
  211.8 41.8 %collective-permute-done.18.refs_1_ = bf16[512,2048]{1,0:T(8,128)(2,1)} collective-permute-done((bf16[512,2048]{1,0:T(8,128)(2,1)S(1)}, bf16[512,2048]{1,0:T(8,128)(2,1)}, u32[]{:S(2)}, u32[]{:S(2)}) %collective-permute-start.18) | collective-permute-done | bytes 2097184 | tf_op jit(solution)/shard_map/ppermute | solution.py:37
  274.6 13.5 %times.12 = (f32[768,2048]{1,0:T(8,128)}, bf16[768,2048]{1,0:T(8,128)(2,1)}) custom-call(bf16[768,2048]{1,0:T(8,128)(2,1)} %all-gather.15.cloned.1.call-done.left_ref, bf16[512,2048]{1,0:T(8,128)(2,1)} %copy-done.5, bf16[512,2048]{1,0:T(8,128)(2,1)} %collective-permute-done.18.refs_1_, bf16[512,2048]{1,0:T(8,128)(2,1)} %collective-permute-done.19.refs_2_, ...), custom_call_target="tpu_custom_call" | custom-call | flops 1 | bytes 1 | tf_op jit(solution)/shard_map/times/pallas_call | solution.py:436
  288.0 11.9 %times_turned.12 = bf16[768,2048]{1,0:T(8,128)(2,1)} custom-call(bf16[768,2048]{1,0:T(8,128)(2,1)} %get-tuple-element.161.left_ref.right_ref, bf16[512,2048]{1,0:T(8,128)(2,1)} %pad_maximum_fusion.2.refs_0_, bf16[512,2048]{1,0:T(8,128)(2,1)} %collective-permute-done.21.refs_1_, bf16[512,2048]{1,0:T(8,128)(2,1)} %collective-permute-done.22.refs_2_, ...), custom_call_target="tpu_custom_call" | custom-call | flops 1 | bytes 1 | tf_op jit(solution)/shard_map/times_turned/pallas_call | solution.py:469
  306.9 48.2 %collective-permute-done.26.refs_1_ = bf16[512,2304]{1,0:T(8,128)(2,1)} collective-permute-done((bf16[512,2304]{1,0:T(8,128)(2,1)S(1)}, bf16[512,2304]{1,0:T(8,128)(2,1)}, u32[]{:S(2)}, u32[]{:S(2)}) %collective-permute-start.26) | collective-permute-done | bytes 2359328 | tf_op jit(solution)/shard_map/ppermute | solution.py:37
  356.2 6.7 collective-permute-done.30.refs_2_
  369.9 7.3 times.13.refs_0_
  384.6 19.4 %all-to-all-done.3 = bf16[4,192,256]{2,1,0:T(8,128)(2,1)S(1)} async-done(((bf16[4,192,256]{2,1,0:T(8,128)(2,1)}), bf16[4,192,256]{2,1,0:T(8,128)(2,1)S(1)}, u32[]{:S(2)}, u32[]{:S(2)}) %all-to-all-start.3) | async-done | bytes 393248 | tf_op jit(solution)/shard_map/all_to_all | solution.py:485
  405.7 9.9 attend.3
  415.6 7.7 times_turned.13.refs_0_
  438.9 39.3 %collective-permute-done.34.refs_1_ = bf16[512,2048]{1,0:T(8,128)(2,1)} collective-permute-done((bf16[512,2048]{1,0:T(8,128)(2,1)}, bf16[512,2048]{1,0:T(8,128)(2,1)}, u32[]{:S(2)}, u32[]{:S(2)}) %collective-permute-start.34) | collective-permute-done | bytes 2097184 | tf_op jit(solution)/shard_map/ppermute | solution.py:37
  486.3 11.7 %times.14.refs_5_ = f32[768,2048]{1,0:T(8,128)} custom-call(bf16[768,2048]{1,0:T(8,128)(2,1)} %copy-done.3, bf16[512,2048]{1,0:T(8,128)(2,1)} %pad_maximum_fusion.5.refs_0_, bf16[512,2048]{1,0:T(8,128)(2,1)} %collective-permute-done.37.refs_1_, bf16[512,2048]{1,0:T(8,128)(2,1)} %collective-permute-done.38.refs_2_, ...), custom_call_target="tpu_custom_call" | custom-call | flops 1 | bytes 1 | tf_op jit(solution)/shard_map/times/pallas_call | solution.py:436
  498.0 15.6 %times.15 = (bf16[768,2048]{1,0:T(8,128)(2,1)}, bf16[768,2048]{1,0:T(8,128)(2,1)}) custom-call(bf16[768,2048]{1,0:T(8,128)(2,1)} %all-gather.19.cloned.1.call-done.left_ref, bf16[512,2048]{1,0:T(8,128)(2,1)} %pad_maximum_fusion.4.refs_0_, bf16[512,2048]{1,0:T(8,128)(2,1)} %collective-permute-done.34.refs_1_, ...), custom_call_target="tpu_custom_call" | custom-call | flops 1 | bytes 1 | tf_op jit(solution)/shard_map/times/pallas_call | solution.py:436
  513.6 11.9 %times_turned.14 = bf16[768,2048]{1,0:T(8,128)(2,1)} custom-call(bf16[768,2048]{1,0:T(8,128)(2,1)} %get-tuple-element.187.left_ref.right_ref.values_ref, bf16[512,2048]{1,0:T(8,128)(2,1)} %pad_maximum_fusion.4.refs_0_, bf16[512,2048]{1,0:T(8,128)(2,1)} %collective-permute-done.34.refs_1_, bf16[512,2048]{1,0:T(8,128)(2,1)} %collective-permute-done.35.refs_2_, ...), custom_call_target="tpu_custom_call" | custom-call | flops 1 | bytes 1 | tf_op jit(solution)/shard_map/times_turned/pallas_call | solution.py:469
  526.0 7.4 turned_product.12
  534.0 7.4 turned_product.14
  541.4 8.3 turned_product.13.half_ref
  549.7 8.3 turned_product.15.half_ref
  563.2 12.0 %times_turned.15 = bf16[768,2048]{1,0:T(8,128)(2,1)} custom-call(bf16[768,2048]{1,0:T(8,128)(2,1)} %get-tuple-element.190.right_ref.left_ref, bf16[512,2048]{1,0:T(8,128)(2,1)} %pad_maximum_fusion.5.refs_0_, bf16[512,2048]{1,0:T(8,128)(2,1)} %collective-permute-done.37.refs_1_, bf16[512,2048]{1,0:T(8,128)(2,1)} %collective-permute-done.38.refs_2_, ...), custom_call_target="tpu_custom_call" | custom-call | flops 1 | bytes 1 | tf_op jit(solution)/shard_map/times_turned/pallas_call | solution.py:469
  575.2 8.9 reduce-scatter.11.cloned.1.call-done.grad_ref
  588.5 4.8 norm_back.4
  593.2 6.5 times.16.refs_1_
  599.7 12.7 %attend_back.2 = (bf16[192,2048]{1,0:T(8,128)(2,1)}, f32[768,256]{1,0:T(8,128)}) custom-call(bf16[192,2304]{1,0:T(8,128)(2,1)} %times.13.refs_0_, bf16[192,2048]{1,0:T(8,128)(2,1)} %times.16.refs_1_, bf16[768,128]{1,0:T(8,128)(2,1)} %get-tuple-element.345.refs_1_.refs_2_, bf16[768,128]{1,0:T(8,128)(2,1)} %get-tuple-element.344.refs_3_, ...), custom_call_target="tpu_custom_call" | custom-call | flops 1 | bytes 1 | tf_op jit(solution)/shard_map/attend_back/pallas_call | solution.py:666
  613.6 26.7 %all_to_all.90 = bf16[4,192,256]{2,1,0:T(8,128)(2,1)S(1)} all-to-all(bf16[4,192,256]{2,1,0:T(8,128)(2,1)S(1)} %bitcast.93), channel_id=1, replica_groups=mesh['dp'=8,'tensor'=4] {'tensor'}, dimensions={0} | all-to-all | bytes 786432 | tf_op jit(solution)/shard_map/all_to_all | solution.py:485
  641.5 8.5 times_turned.16.grad_ref
  652.8 5.3 norm_back.5
  664.9 5.2 turned_product.16
  670.2 5.0 turned_product.18
  678.4 6.4 turned_product.17.half_ref
  689.1 5.9 turned_product.19.half_ref
  709.4 6.4 place_rows.6
  715.8 24.2 %all-gather.23.cloned.1.call-done.left_ref = bf16[768,2048]{1,0:T(8,128)(2,1)} async-done(((bf16[192,2048]{1,0:T(8,128)(2,1)}), bf16[768,2048]{1,0:T(8,128)(2,1)}) %all-gather.23.cloned.1.call-update) | async-done | bytes 3145744 | tf_op jit(solution)/shard_map/all_gather | solution.py:489
  740.1 14.2 %times.17.left_ref.right_ref.values_ref = bf16[768,2048]{1,0:T(8,128)(2,1)} custom-call(bf16[768,2048]{1,0:T(8,128)(2,1)} %all-gather.23.cloned.1.call-done.left_ref, bf16[512,2048]{1,0:T(8,128)(2,1)} %pad_maximum_fusion.2.refs_0_, bf16[512,2048]{1,0:T(8,128)(2,1)} %collective-permute-done.21.refs_1_, bf16[512,2048]{1,0:T(8,128)(2,1)} %collective-permute-done.22.refs_2_, ...), custom_call_target="tpu_custom_call" | custom-call | flops 1 | bytes 1 | tf_op jit(solution)/shard_map/times/pallas_call | solution.py:436
  754.3 12.0 %times_turned.17 = bf16[768,2048]{1,0:T(8,128)(2,1)} custom-call(bf16[768,2048]{1,0:T(8,128)(2,1)} %times.17.left_ref.right_ref.values_ref, bf16[512,2048]{1,0:T(8,128)(2,1)} %copy-done.5, bf16[512,2048]{1,0:T(8,128)(2,1)} %collective-permute-done.18.refs_1_, bf16[512,2048]{1,0:T(8,128)(2,1)} %collective-permute-done.19.refs_2_, ...), custom_call_target="tpu_custom_call" | custom-call | flops 1 | bytes 1 | tf_op jit(solution)/shard_map/times_turned/pallas_call | solution.py:469
  767.9 8.6 turned_product.20
  776.5 7.5 turned_product.22
  798.3 8.3 turned_product.21.half_ref
  806.5 8.3 turned_product.23.half_ref
  830.4 4.8 norm_back.6
  859.7 12.7 %attend_back.3 = (bf16[192,2048]{1,0:T(8,128)(2,1)}, f32[768,256]{1,0:T(8,128)}) custom-call(bf16[192,2304]{1,0:T(8,128)(2,1)} %pad_maximum_fusion.15.refs_0_, bf16[192,2048]{1,0:T(8,128)(2,1)} %pad_maximum_fusion.18.refs_1_, bf16[768,128]{1,0:T(8,128)(2,1)} %get-tuple-element.341.refs_1_.refs_2_, bf16[768,128]{1,0:T(8,128)(2,1)} %get-tuple-element.340.refs_3_, ...), custom_call_target="tpu_custom_call" | custom-call | flops 1 | bytes 1 | tf_op jit(solution)/shard_map/attend_back/pallas_call | solution.py:666
  874.3 4.5 all-to-all-start.6
  883.6 7.8 all-to-all-done.6
  965.3 4.9 times_turned.18
  970.2 5.8 times_turned.19
  978.7 5.2 norm_back.7
  983.9 7.1 collective-permute-done.74.come_ref
  1017.4 4.8 reorder.3
  1045.2 6.4 place_rows.7
  1057.5 13.7 %collective-permute-done.67 = f32[18,2048]{1,0:T(8,128)S(1)} collective-permute-done((f32[18,2048]{1,0:T(8,128)S(1)}, f32[18,2048]{1,0:T(8,128)S(1)}, u32[]{:S(2)}, u32[]{:S(2)}) %collective-permute-start.67) | collective-permute-done | bytes 147488 | tf_op jit(solution)/shard_map/ppermute | solution.py:37
  1074.1 4.4 stack_sums.2
  1078.5 4.8 stack_sums.3
  (617 shorter events, 423.0 us)
Async XLA Ops:
  7.2 44.9 %all-gather.9.cloned.1.call-start = ((), (), s32[]{:S(2)}) async-start(), calls=%async_computation.16 | async-start | bytes 1556480 | tf_op jit(solution)/shard_map/all_gather | solution.py:489
  19.4 60.0 %all-gather.11.cloned.1.call-start = ((), (), s32[]{:S(2)}) async-start(), calls=%async_computation.17 | async-start | bytes 1310720 | tf_op jit(solution)/shard_map/all_gather | solution.py:489
  39.0 87.4 %all-gather.17.cloned.1.call-start = ((), (), s32[]{:S(2)}) async-start(), calls=%async_computation.20 | async-start | bytes 2867200 | tf_op jit(solution)/shard_map/all_gather | solution.py:489
  69.1 32.1 %collective-permute-start.5 = (bf16[512,1280]{1,0:T(8,128)(2,1)S(1)}, bf16[512,1280]{1,0:T(8,128)(2,1)}, u32[]{:S(2)}, u32[]{:S(2)}) collective-permute-start(bf16[512,1280]{1,0:T(8,128)(2,1)S(1)} %pad_maximum_fusion.6.refs_0_), channel_id=1, source_target_pairs={{0,8},{4,12},{8,0},{12,4},{16,24},{20,28},{24,16},{28,20},{1,9},{5... | collective-permute-start | bytes 3932168 | tf_op jit(solution)/shard_map/ppermute | solution.py:37
  82.5 49.3 %collective-permute-start.3 = (bf16[512,1024]{1,0:T(8,128)(2,1)S(1)}, bf16[512,1024]{1,0:T(8,128)(2,1)}, u32[]{:S(2)}, u32[]{:S(2)}) collective-permute-start(bf16[512,1024]{1,0:T(8,128)(2,1)S(1)} %pad_maximum_fusion.8.refs_0_), channel_id=1, source_target_pairs={{0,4},{4,0},{8,12},{12,8},{16,20},{20,16},{24,28},{28,24},{1,5},{5... | collective-permute-start | bytes 3145736 | tf_op jit(solution)/shard_map/ppermute | solution.py:37
  82.6 54.8 %collective-permute-start.6 = (bf16[512,1280]{1,0:T(8,128)(2,1)S(1)}, bf16[512,1280]{1,0:T(8,128)(2,1)}, u32[]{:S(2)}, u32[]{:S(2)}) collective-permute-start(bf16[512,1280]{1,0:T(8,128)(2,1)S(1)} %pad_maximum_fusion.6.refs_0_), channel_id=1, source_target_pairs={{0,4},{4,0},{8,12},{12,8},{16,20},{20,16},{24,28},{28,24},{1,5},{5... | collective-permute-start | bytes 3932168 | tf_op jit(solution)/shard_map/ppermute | solution.py:37
  97.1 36.3 %collective-permute-start.4 = (bf16[512,1024]{1,0:T(8,128)(2,1)S(1)}, bf16[512,1024]{1,0:T(8,128)(2,1)}, u32[]{:S(2)}, u32[]{:S(2)}) collective-permute-start(bf16[512,1024]{1,0:T(8,128)(2,1)S(1)} %collective-permute-done.2.refs_1_), channel_id=1, source_target_pairs={{0,4},{4,0},{8,12},{12,8},{16,20},{20,16},{24,28},{28,24},{1,5},{5... | collective-permute-start | bytes 3145736 | tf_op jit(solution)/shard_map/ppermute | solution.py:37
  101.1 36.2 %collective-permute-start.7 = (bf16[512,1280]{1,0:T(8,128)(2,1)}, bf16[512,1280]{1,0:T(8,128)(2,1)}, u32[]{:S(2)}, u32[]{:S(2)}) collective-permute-start(bf16[512,1280]{1,0:T(8,128)(2,1)} %collective-permute-done.5.refs_1_), channel_id=1, source_target_pairs={{0,4},{4,0},{8,12},{12,8},{16,20},{20,16},{24,28},{28,24},{1,5},{5... | collective-permute-start | bytes 3932168 | tf_op jit(solution)/shard_map/ppermute | solution.py:37
  109.6 39.8 %collective-permute-start.8 = (bf16[256,1024]{1,0:T(8,128)(2,1)}, bf16[256,1024]{1,0:T(8,128)(2,1)}, u32[]{:S(2)}, u32[]{:S(2)}) collective-permute-start(bf16[256,1024]{1,0:T(8,128)(2,1)} %pad_maximum_fusion.21), channel_id=1, source_target_pairs={{0,8},{4,12},{8,0},{12,4},{16,24},{20,28},{24,16},{28,20},{1,9},{5... | collective-permute-start | bytes 1572872 | tf_op jit(solution)/shard_map/ppermute | solution.py:37
  147.3 57.4 %all-gather.13.cloned.1.call-start = ((), (), s32[]{:S(2)}) async-start(), calls=%async_computation.18 | async-start | bytes 1966080 | tf_op jit(solution)/shard_map/all_gather | solution.py:489
  150.6 28.8 %collective-permute-start.11 = (bf16[512,1024]{1,0:T(8,128)(2,1)S(1)}, bf16[512,1024]{1,0:T(8,128)(2,1)}, u32[]{:S(2)}, u32[]{:S(2)}) collective-permute-start(bf16[512,1024]{1,0:T(8,128)(2,1)S(1)} %pad_maximum_fusion.9.refs_0_), channel_id=1, source_target_pairs={{0,4},{4,0},{8,12},{12,8},{16,20},{20,16},{24,28},{28,24},{1,5},{5... | collective-permute-start | bytes 3145736 | tf_op jit(solution)/shard_map/ppermute | solution.py:37
  150.7 25.7 %collective-permute-start.10 = (bf16[512,1024]{1,0:T(8,128)(2,1)S(1)}, bf16[512,1024]{1,0:T(8,128)(2,1)}, u32[]{:S(2)}, u32[]{:S(2)}) collective-permute-start(bf16[512,1024]{1,0:T(8,128)(2,1)S(1)} %pad_maximum_fusion.9.refs_0_), channel_id=1, source_target_pairs={{0,16},{4,20},{8,24},{12,28},{16,0},{20,4},{24,8},{28,12},{1,17},{... | collective-permute-start | bytes 3145736 | tf_op jit(solution)/shard_map/ppermute | solution.py:37
  152.4 25.4 %collective-permute-start.13 = (bf16[512,1024]{1,0:T(8,128)(2,1)S(1)}, bf16[512,1024]{1,0:T(8,128)(2,1)}, u32[]{:S(2)}, u32[]{:S(2)}) collective-permute-start(bf16[512,1024]{1,0:T(8,128)(2,1)S(1)} %pad_maximum_fusion.10.refs_0_), channel_id=1, source_target_pairs={{0,8},{4,12},{8,0},{12,4},{16,24},{20,28},{24,16},{28,20},{1,9},{5... | collective-permute-start | bytes 3145736 | tf_op jit(solution)/shard_map/ppermute | solution.py:37
  154.0 114.8 %all-gather.15.cloned.1.call-start = ((), (), s32[]{:S(2)}) async-start(), calls=%async_computation.19 | async-start | bytes 3932160 | tf_op jit(solution)/shard_map/all_gather | solution.py:489
  162.0 25.4 %collective-permute-start.14 = (bf16[512,1024]{1,0:T(8,128)(2,1)S(1)}, bf16[512,1024]{1,0:T(8,128)(2,1)}, u32[]{:S(2)}, u32[]{:S(2)}) collective-permute-start(bf16[512,1024]{1,0:T(8,128)(2,1)S(1)} %pad_maximum_fusion.10.refs_0_), channel_id=1, source_target_pairs={{0,4},{4,0},{8,12},{12,8},{16,20},{20,16},{24,28},{28,24},{1,5},{5... | collective-permute-start | bytes 3145736 | tf_op jit(solution)/shard_map/ppermute | solution.py:37
  177.8 25.9 %collective-permute-start.16 = (bf16[256,2048]{1,0:T(8,128)(2,1)}, bf16[256,2048]{1,0:T(8,128)(2,1)}, u32[]{:S(2)}, u32[]{:S(2)}) collective-permute-start(bf16[256,2048]{1,0:T(8,128)(2,1)} %get-tuple-element.151), channel_id=1, source_target_pairs={{0,8},{4,12},{8,0},{12,4},{16,24},{20,28},{24,16},{28,20},{1,9},{5... | collective-permute-start | bytes 3145736 | tf_op jit(solution)/shard_map/ppermute | solution.py:37
  179.3 25.4 %collective-permute-start.17 = (bf16[256,2048]{1,0:T(8,128)(2,1)S(1)}, bf16[256,2048]{1,0:T(8,128)(2,1)}, u32[]{:S(2)}, u32[]{:S(2)}) collective-permute-start(bf16[256,2048]{1,0:T(8,128)(2,1)S(1)} %bitcast.77), channel_id=1, source_target_pairs={{0,16},{4,20},{8,24},{12,28},{16,0},{20,4},{24,8},{28,12},{1,17},{... | collective-permute-start | bytes 3145736 | tf_op jit(solution)/shard_map/ppermute | solution.py:37
  204.8 161.2 %reduce-scatter.9.cloned.1.call-start = ((), (), s32[]{:S(2)}) async-start(), calls=%async_computation.21 | async-start | bytes 3932160 | tf_op jit(solution)/shard_map/reduce_scatter | solution.py:493
  206.5 47.1 %collective-permute-start.18 = (bf16[512,2048]{1,0:T(8,128)(2,1)S(1)}, bf16[512,2048]{1,0:T(8,128)(2,1)}, u32[]{:S(2)}, u32[]{:S(2)}) collective-permute-start(bf16[512,2048]{1,0:T(8,128)(2,1)S(1)} %pad_maximum_fusion.1.refs_0_), channel_id=1, source_target_pairs={{0,16},{4,20},{8,24},{12,28},{16,0},{20,4},{24,8},{28,12},{1,17},{... | collective-permute-start | bytes 6291464 | tf_op jit(solution)/shard_map/ppermute | solution.py:37
  210.3 47.0 %collective-permute-start.21 = (bf16[512,2048]{1,0:T(8,128)(2,1)}, bf16[512,2048]{1,0:T(8,128)(2,1)}, u32[]{:S(2)}, u32[]{:S(2)}) collective-permute-start(bf16[512,2048]{1,0:T(8,128)(2,1)} %pad_maximum_fusion.2.refs_0_), channel_id=1, source_target_pairs={{0,8},{4,12},{8,0},{12,4},{16,24},{20,28},{24,16},{28,20},{1,9},{5... | collective-permute-start | bytes 6291464 | tf_op jit(solution)/shard_map/ppermute | solution.py:37
  211.3 54.9 %collective-permute-start.19 = (bf16[512,2048]{1,0:T(8,128)(2,1)S(1)}, bf16[512,2048]{1,0:T(8,128)(2,1)}, u32[]{:S(2)}, u32[]{:S(2)}) collective-permute-start(bf16[512,2048]{1,0:T(8,128)(2,1)S(1)} %pad_maximum_fusion.1.refs_0_), channel_id=1, source_target_pairs={{0,4},{4,0},{8,12},{12,8},{16,20},{20,16},{24,28},{28,24},{1,5},{5... | collective-permute-start | bytes 6291464 | tf_op jit(solution)/shard_map/ppermute | solution.py:37
  211.3 54.9 %collective-permute-start.22 = (bf16[512,2048]{1,0:T(8,128)(2,1)}, bf16[512,2048]{1,0:T(8,128)(2,1)}, u32[]{:S(2)}, u32[]{:S(2)}) collective-permute-start(bf16[512,2048]{1,0:T(8,128)(2,1)} %pad_maximum_fusion.2.refs_0_), channel_id=1, source_target_pairs={{0,4},{4,0},{8,12},{12,8},{16,20},{20,16},{24,28},{28,24},{1,5},{5... | collective-permute-start | bytes 6291464 | tf_op jit(solution)/shard_map/ppermute | solution.py:37
  268.8 31.1 %collective-permute-start.24 = (bf16[256,2304]{1,0:T(8,128)(2,1)S(1)}, bf16[256,2304]{1,0:T(8,128)(2,1)S(1)}, u32[]{:S(2)}, u32[]{:S(2)}) collective-permute-start(bf16[256,2304]{1,0:T(8,128)(2,1)S(1)} %concatenate.130), channel_id=1, source_target_pairs={{0,8},{4,12},{8,0},{12,4},{16,24},{20,28},{24,16},{28,20},{1,9},{5... | collective-permute-start | bytes 3538952 | tf_op jit(solution)/shard_map/ppermute | solution.py:37
  272.5 27.5 %collective-permute-start.25 = (bf16[256,2048]{1,0:T(8,128)(2,1)}, bf16[256,2048]{1,0:T(8,128)(2,1)}, u32[]{:S(2)}, u32[]{:S(2)}) collective-permute-start(bf16[256,2048]{1,0:T(8,128)(2,1)} %pad_maximum_fusion.11), channel_id=1, source_target_pairs={{0,16},{4,20},{8,24},{12,28},{16,0},{20,4},{24,8},{28,12},{1,17},{... | collective-permute-start | bytes 3145736 | tf_op jit(solution)/shard_map/ppermute | solution.py:37
  301.0 135.2 %all-gather.21.cloned.1.call-start = ((), (), s32[]{:S(2)}) async-start(), calls=%async_computation.23 | async-start | bytes 1966080 | tf_op jit(solution)/shard_map/all_gather | solution.py:489
  302.5 52.6 %collective-permute-start.26 = (bf16[512,2304]{1,0:T(8,128)(2,1)S(1)}, bf16[512,2304]{1,0:T(8,128)(2,1)}, u32[]{:S(2)}, u32[]{:S(2)}) collective-permute-start(bf16[512,2304]{1,0:T(8,128)(2,1)S(1)} %pad_maximum_fusion.refs_0_), channel_id=1, source_target_pairs={{0,16},{4,20},{8,24},{12,28},{16,0},{20,4},{24,8},{28,12},{1,17},{... | collective-permute-start | bytes 7077896 | tf_op jit(solution)/shard_map/ppermute | solution.py:37
  306.5 49.1 %collective-permute-start.29 = (bf16[512,2048]{1,0:T(8,128)(2,1)}, bf16[512,2048]{1,0:T(8,128)(2,1)}, u32[]{:S(2)}, u32[]{:S(2)}) collective-permute-start(bf16[512,2048]{1,0:T(8,128)(2,1)} %pad_maximum_fusion.3.refs_0_), channel_id=1, source_target_pairs={{0,8},{4,12},{8,0},{12,4},{16,24},{20,28},{24,16},{28,20},{1,9},{5... | collective-permute-start | bytes 6291464 | tf_op jit(solution)/shard_map/ppermute | solution.py:37
  306.9 56.1 %collective-permute-start.27 = (bf16[512,2304]{1,0:T(8,128)(2,1)S(1)}, bf16[512,2304]{1,0:T(8,128)(2,1)}, u32[]{:S(2)}, u32[]{:S(2)}) collective-permute-start(bf16[512,2304]{1,0:T(8,128)(2,1)S(1)} %pad_maximum_fusion.refs_0_), channel_id=1, source_target_pairs={{0,4},{4,0},{8,12},{12,8},{16,20},{20,16},{24,28},{28,24},{1,5},{5... | collective-permute-start | bytes 7077896 | tf_op jit(solution)/shard_map/ppermute | solution.py:37
  379.0 24.9 %all-to-all-start.3 = ((bf16[4,192,256]{2,1,0:T(8,128)(2,1)}), bf16[4,192,256]{2,1,0:T(8,128)(2,1)S(1)}, u32[]{:S(2)}, u32[]{:S(2)}) async-start(bf16[4,192,256]{2,1,0:T(8,128)(2,1)} %bitcast.31), calls=%async_computation.4 | async-start | bytes 786432 | tf_op jit(solution)/shard_map/all_to_all | solution.py:485
  382.5 115.5 %all-gather.19.cloned.1.call-start = ((), (), s32[]{:S(2)}) async-start(), calls=%async_computation.22 | async-start | bytes 3932160 | tf_op jit(solution)/shard_map/all_gather | solution.py:489
  383.4 32.2 %collective-permute-start.32 = (bf16[256,2048]{1,0:T(8,128)(2,1)S(1)}, bf16[256,2048]{1,0:T(8,128)(2,1)}, u32[]{:S(2)}, u32[]{:S(2)}) collective-permute-start(bf16[256,2048]{1,0:T(8,128)(2,1)S(1)} %copy-done.23), channel_id=1, source_target_pairs={{0,8},{4,12},{8,0},{12,4},{16,24},{20,28},{24,16},{28,20},{1,9},{5... | collective-permute-start | bytes 3145736 | tf_op jit(solution)/shard_map/ppermute | solution.py:37
  384.1 31.6 %collective-permute-start.33 = (bf16[256,2048]{1,0:T(8,128)(2,1)S(1)}, bf16[256,2048]{1,0:T(8,128)(2,1)}, u32[]{:S(2)}, u32[]{:S(2)}) collective-permute-start(bf16[256,2048]{1,0:T(8,128)(2,1)S(1)} %bitcast.79), channel_id=1, source_target_pairs={{0,16},{4,20},{8,24},{12,28},{16,0},{20,4},{24,8},{28,12},{1,17},{... | collective-permute-start | bytes 3145736 | tf_op jit(solution)/shard_map/ppermute | solution.py:37
  427.5 156.6 %reduce-scatter.11.cloned.1.call-start = ((), (), s32[]{:S(2)}) async-start(), calls=%async_computation.24 | async-start | bytes 3932160 | tf_op jit(solution)/shard_map/reduce_scatter | solution.py:493
  430.3 48.0 %collective-permute-start.34 = (bf16[512,2048]{1,0:T(8,128)(2,1)}, bf16[512,2048]{1,0:T(8,128)(2,1)}, u32[]{:S(2)}, u32[]{:S(2)}) collective-permute-start(bf16[512,2048]{1,0:T(8,128)(2,1)} %pad_maximum_fusion.4.refs_0_), channel_id=1, source_target_pairs={{0,16},{4,20},{8,24},{12,28},{16,0},{20,4},{24,8},{28,12},{1,17},{... | collective-permute-start | bytes 6291464 | tf_op jit(solution)/shard_map/ppermute | solution.py:37
  434.3 47.1 %collective-permute-start.37 = (bf16[512,2048]{1,0:T(8,128)(2,1)}, bf16[512,2048]{1,0:T(8,128)(2,1)}, u32[]{:S(2)}, u32[]{:S(2)}) collective-permute-start(bf16[512,2048]{1,0:T(8,128)(2,1)} %pad_maximum_fusion.5.refs_0_), channel_id=1, source_target_pairs={{0,8},{4,12},{8,0},{12,4},{16,24},{20,28},{24,16},{28,20},{1,9},{5... | collective-permute-start | bytes 6291464 | tf_op jit(solution)/shard_map/ppermute | solution.py:37
  438.4 59.6 %collective-permute-start.35 = (bf16[512,2048]{1,0:T(8,128)(2,1)}, bf16[512,2048]{1,0:T(8,128)(2,1)}, u32[]{:S(2)}, u32[]{:S(2)}) collective-permute-start(bf16[512,2048]{1,0:T(8,128)(2,1)} %pad_maximum_fusion.4.refs_0_), channel_id=1, source_target_pairs={{0,4},{4,0},{8,12},{12,8},{16,20},{20,16},{24,28},{28,24},{1,5},{5... | collective-permute-start | bytes 6291464 | tf_op jit(solution)/shard_map/ppermute | solution.py:37
  438.4 46.2 %collective-permute-start.38 = (bf16[512,2048]{1,0:T(8,128)(2,1)}, bf16[512,2048]{1,0:T(8,128)(2,1)}, u32[]{:S(2)}, u32[]{:S(2)}) collective-permute-start(bf16[512,2048]{1,0:T(8,128)(2,1)} %pad_maximum_fusion.5.refs_0_), channel_id=1, source_target_pairs={{0,4},{4,0},{8,12},{12,8},{16,20},{20,16},{24,28},{28,24},{1,5},{5... | collective-permute-start | bytes 6291464 | tf_op jit(solution)/shard_map/ppermute | solution.py:37
  525.6 127.2 %reduce-scatter.13.cloned.1.call-start = ((), (), s32[]{:S(2)}) async-start(), calls=%async_computation.25 | async-start | bytes 3932160 | tf_op jit(solution)/shard_map/reduce_scatter | solution.py:493
  584.2 155.9 %all-gather.23.cloned.1.call-start = ((), (), s32[]{:S(2)}) async-start(), calls=%async_computation.26 | async-start | bytes 3932160 | tf_op jit(solution)/shard_map/all_gather | solution.py:489
  584.2 57.3 %collective-permute-start.42 = (bf16[512,2048]{1,0:T(8,128)(2,1)}, bf16[512,2048]{1,0:T(8,128)(2,1)}, u32[]{:S(2)}, u32[]{:S(2)}) collective-permute-start(bf16[512,2048]{1,0:T(8,128)(2,1)} %take_blocks.20), channel_id=1, source_target_pairs={{0,8},{4,12},{8,0},{12,4},{16,24},{20,28},{24,16},{28,20},{1,9},{5... | collective-permute-start | bytes 6291464 | tf_op jit(solution)/shard_map/ppermute | solution.py:37
  585.7 55.8 %collective-permute-start.43 = (bf16[512,2048]{1,0:T(8,128)(2,1)}, bf16[512,2048]{1,0:T(8,128)(2,1)}, u32[]{:S(2)}, u32[]{:S(2)}) collective-permute-start(bf16[512,2048]{1,0:T(8,128)(2,1)} %take_blocks.21), channel_id=1, source_target_pairs={{0,16},{4,20},{8,24},{12,28},{16,0},{20,4},{24,8},{28,12},{1,17},{... | collective-permute-start | bytes 6291464 | tf_op jit(solution)/shard_map/ppermute | solution.py:37
  675.6 154.7 %reduce-scatter.15.cloned.1.call-start = ((), (), s32[]{:S(2)}) async-start(), calls=%async_computation.27 | async-start | bytes 3932160 | tf_op jit(solution)/shard_map/reduce_scatter | solution.py:493
  687.7 80.1 %collective-permute-start.48 = (bf16[512,2304]{1,0:T(8,128)(2,1)}, bf16[512,2304]{1,0:T(8,128)(2,1)S(1)}, u32[]{:S(2)}, u32[]{:S(2)}) collective-permute-start(bf16[512,2304]{1,0:T(8,128)(2,1)} %take_blocks.24), channel_id=1, source_target_pairs={{0,8},{4,12},{8,0},{12,4},{16,24},{20,28},{24,16},{28,20},{1,9},{5... | collective-permute-start | bytes 7077896 | tf_op jit(solution)/shard_map/ppermute | solution.py:37
  697.7 70.1 %collective-permute-start.49 = (bf16[512,2048]{1,0:T(8,128)(2,1)}, bf16[512,2048]{1,0:T(8,128)(2,1)}, u32[]{:S(2)}, u32[]{:S(2)}) collective-permute-start(bf16[512,2048]{1,0:T(8,128)(2,1)} %take_blocks.25), channel_id=1, source_target_pairs={{0,16},{4,20},{8,24},{12,28},{16,0},{20,4},{24,8},{28,12},{1,17},{... | collective-permute-start | bytes 6291464 | tf_op jit(solution)/shard_map/ppermute | solution.py:37
  701.5 66.3 %collective-permute-start.46 = (bf16[256,2048]{1,0:T(8,128)(2,1)}, bf16[256,2048]{1,0:T(8,128)(2,1)S(1)}, u32[]{:S(2)}, u32[]{:S(2)}) collective-permute-start(bf16[256,2048]{1,0:T(8,128)(2,1)} %take_blocks.22), channel_id=1, source_target_pairs={{0,16},{4,20},{8,24},{12,28},{16,0},{20,4},{24,8},{28,12},{1,17},{... | collective-permute-start | bytes 3145736 | tf_op jit(solution)/shard_map/ppermute | solution.py:37
  704.3 63.5 %collective-permute-start.47 = (bf16[256,2048]{1,0:T(8,128)(2,1)}, bf16[256,2048]{1,0:T(8,128)(2,1)}, u32[]{:S(2)}, u32[]{:S(2)}) collective-permute-start(bf16[256,2048]{1,0:T(8,128)(2,1)} %take_blocks.23), channel_id=1, source_target_pairs={{0,8},{4,12},{8,0},{12,4},{16,24},{20,28},{24,16},{28,20},{1,9},{5... | collective-permute-start | bytes 3145736 | tf_op jit(solution)/shard_map/ppermute | solution.py:37
  790.5 32.3 %collective-permute-start.52 = (bf16[256,2304]{1,0:T(8,128)(2,1)}, bf16[256,2304]{1,0:T(8,128)(2,1)S(1)}, u32[]{:S(2)}, u32[]{:S(2)}) collective-permute-start(bf16[256,2304]{1,0:T(8,128)(2,1)} %take_blocks.26), channel_id=1, source_target_pairs={{0,16},{4,20},{8,24},{12,28},{16,0},{20,4},{24,8},{28,12},{1,17},{... | collective-permute-start | bytes 3538952 | tf_op jit(solution)/shard_map/ppermute | solution.py:37
  797.8 25.0 %collective-permute-start.53 = (bf16[256,2048]{1,0:T(8,128)(2,1)}, bf16[256,2048]{1,0:T(8,128)(2,1)S(1)}, u32[]{:S(2)}, u32[]{:S(2)}) collective-permute-start(bf16[256,2048]{1,0:T(8,128)(2,1)} %take_blocks.27), channel_id=1, source_target_pairs={{0,8},{4,12},{8,0},{12,4},{16,24},{20,28},{24,16},{28,20},{1,9},{5... | collective-permute-start | bytes 3145736 | tf_op jit(solution)/shard_map/ppermute | solution.py:37
  847.6 47.9 %collective-permute-start.56 = (bf16[512,2048]{1,0:T(8,128)(2,1)}, bf16[512,2048]{1,0:T(8,128)(2,1)}, u32[]{:S(2)}, u32[]{:S(2)}) collective-permute-start(bf16[512,2048]{1,0:T(8,128)(2,1)} %take_blocks.28), channel_id=1, source_target_pairs={{0,8},{4,12},{8,0},{12,4},{16,24},{20,28},{24,16},{28,20},{1,9},{5... | collective-permute-start | bytes 6291464 | tf_op jit(solution)/shard_map/ppermute | solution.py:37
  848.1 47.6 %collective-permute-start.57 = (bf16[512,2048]{1,0:T(8,128)(2,1)}, bf16[512,2048]{1,0:T(8,128)(2,1)}, u32[]{:S(2)}, u32[]{:S(2)}) collective-permute-start(bf16[512,2048]{1,0:T(8,128)(2,1)} %take_blocks.29), channel_id=1, source_target_pairs={{0,16},{4,20},{8,24},{12,28},{16,0},{20,4},{24,8},{28,12},{1,17},{... | collective-permute-start | bytes 6291464 | tf_op jit(solution)/shard_map/ppermute | solution.py:37
  878.8 164.5 %reduce-scatter.19.cloned.1.call-start = ((), (), s32[]{:S(2)}) async-start(), calls=%async_computation.29 | async-start | bytes 1474560 | tf_op jit(solution)/shard_map/reduce_scatter | solution.py:493
  899.5 185.6 %reduce-scatter.23.cloned.1.call-start = ((), (), s32[]{:S(2)}) async-start(), calls=%async_computation.31 | async-start | bytes 1310720 | tf_op jit(solution)/shard_map/reduce_scatter | solution.py:493
  910.0 39.0 %collective-permute-start.60 = (bf16[512,1024]{1,0:T(8,128)(2,1)}, bf16[512,1024]{1,0:T(8,128)(2,1)}, u32[]{:S(2)}, u32[]{:S(2)}) collective-permute-start(bf16[512,1024]{1,0:T(8,128)(2,1)} %take_blocks.30), channel_id=1, source_target_pairs={{0,8},{4,12},{8,0},{12,4},{16,24},{20,28},{24,16},{28,20},{1,9},{5... | collective-permute-start | bytes 3145736 | tf_op jit(solution)/shard_map/ppermute | solution.py:37
  911.6 37.5 %collective-permute-start.61 = (bf16[512,1024]{1,0:T(8,128)(2,1)S(1)}, bf16[512,1024]{1,0:T(8,128)(2,1)}, u32[]{:S(2)}, u32[]{:S(2)}) collective-permute-start(bf16[512,1024]{1,0:T(8,128)(2,1)S(1)} %copy-done.51), channel_id=1, source_target_pairs={{0,16},{4,20},{8,24},{12,28},{16,0},{20,4},{24,8},{28,12},{1,17},{... | collective-permute-start | bytes 3145736 | tf_op jit(solution)/shard_map/ppermute | solution.py:37
  925.1 73.5 %collective-permute-start.70 = (bf16[512,1280]{1,0:T(8,128)(2,1)}, bf16[512,1280]{1,0:T(8,128)(2,1)}, u32[]{:S(2)}, u32[]{:S(2)}) collective-permute-start(bf16[512,1280]{1,0:T(8,128)(2,1)} %take_blocks.33), channel_id=1, source_target_pairs={{0,16},{4,20},{8,24},{12,28},{16,0},{20,4},{24,8},{28,12},{1,17},{... | collective-permute-start | bytes 3932168 | tf_op jit(solution)/shard_map/ppermute | solution.py:37
  937.1 86.2 %all-to-all-start.5 = ((bf16[8,24,2048]{2,1,0:T(8,128)(2,1)}), bf16[8,24,2048]{2,1,0:T(8,128)(2,1)S(1)}, u32[]{:S(2)}, u32[]{:S(2)}) async-start(bf16[8,24,2048]{2,1,0:T(8,128)(2,1)} %bitcast.40), calls=%async_computation.8 | async-start | bytes 1572864 | tf_op jit(solution)/shard_map/all_to_all | solution.py:858
  940.7 144.5 %reduce-scatter.21.cloned.1.call-start = ((), (), s32[]{:S(2)}) async-start(), calls=%async_computation.30 | async-start | bytes 1310720 | tf_op jit(solution)/shard_map/reduce_scatter | solution.py:493
  954.0 44.7 %collective-permute-start.69 = (bf16[512,1024]{1,0:T(8,128)(2,1)}, bf16[512,1024]{1,0:T(8,128)(2,1)}, u32[]{:S(2)}, u32[]{:S(2)}) collective-permute-start(bf16[512,1024]{1,0:T(8,128)(2,1)} %take_blocks.32), channel_id=1, source_target_pairs={{0,8},{4,12},{8,0},{12,4},{16,24},{20,28},{24,16},{28,20},{1,9},{5... | collective-permute-start | bytes 3145736 | tf_op jit(solution)/shard_map/ppermute | solution.py:37
  959.7 31.3 %collective-permute-start.74 = (bf16[256,1024]{1,0:T(8,128)(2,1)}, bf16[256,1024]{1,0:T(8,128)(2,1)}, u32[]{:S(2)}, u32[]{:S(2)}) collective-permute-start(bf16[256,1024]{1,0:T(8,128)(2,1)} %take_blocks.37), channel_id=1, source_target_pairs={{0,8},{4,12},{8,0},{12,4},{16,24},{20,28},{24,16},{28,20},{1,9},{5... | collective-permute-start | bytes 1572872 | tf_op jit(solution)/shard_map/ppermute | solution.py:37
  959.9 32.8 %collective-permute-start.73 = (bf16[256,1024]{1,0:T(8,128)(2,1)}, bf16[256,1024]{1,0:T(8,128)(2,1)}, u32[]{:S(2)}, u32[]{:S(2)}) collective-permute-start(bf16[256,1024]{1,0:T(8,128)(2,1)} %take_blocks.36), channel_id=1, source_target_pairs={{0,16},{4,20},{8,24},{12,28},{16,0},{20,4},{24,8},{28,12},{1,17},{... | collective-permute-start | bytes 1572872 | tf_op jit(solution)/shard_map/ppermute | solution.py:37
  965.1 48.2 %collective-permute-start.62 = (bf16[256,2048]{1,0:T(8,128)(2,1)}, bf16[256,2048]{1,0:T(8,128)(2,1)S(1)}, u32[]{:S(2)}, u32[]{:S(2)}) collective-permute-start(bf16[256,2048]{1,0:T(8,128)(2,1)} %take_blocks.34), channel_id=1, source_target_pairs={{0,16},{4,20},{8,24},{12,28},{16,0},{20,4},{24,8},{28,12},{1,17},{... | collective-permute-start | bytes 3145736 | tf_op jit(solution)/shard_map/ppermute | solution.py:37
  991.0 26.4 %collective-permute-start.63 = (bf16[256,2048]{1,0:T(8,128)(2,1)}, bf16[256,2048]{1,0:T(8,128)(2,1)}, u32[]{:S(2)}, u32[]{:S(2)}) collective-permute-start(bf16[256,2048]{1,0:T(8,128)(2,1)} %take_blocks.35), channel_id=1, source_target_pairs={{0,8},{4,12},{8,0},{12,4},{16,24},{20,28},{24,16},{28,20},{1,9},{5... | collective-permute-start | bytes 3145736 | tf_op jit(solution)/shard_map/ppermute | solution.py:37
  1003.4 26.6 %collective-permute-start.72 = (bf16[256,1280]{1,0:T(8,128)(2,1)}, bf16[256,1280]{1,0:T(8,128)(2,1)}, u32[]{:S(2)}, u32[]{:S(2)}) collective-permute-start(bf16[256,1280]{1,0:T(8,128)(2,1)} %take_blocks.39), channel_id=1, source_target_pairs={{0,8},{4,12},{8,0},{12,4},{16,24},{20,28},{24,16},{28,20},{1,9},{5... | collective-permute-start | bytes 1966088 | tf_op jit(solution)/shard_map/ppermute | solution.py:37
  1007.3 80.3 %reduce-scatter.17.cloned.1.call-start = ((), (), s32[]{:S(2)}) async-start(), calls=%async_computation.28 | async-start | bytes 1474560 | tf_op jit(solution)/shard_map/reduce_scatter | solution.py:493
  (118 other events, 1248.1 us)
Sparse Core Ops, SparseCore 0:
  11.8 34.2 all-gather.8
  48.3 26.9 all-gather.10
  77.4 48.9 all-gather.16
  154.2 37.4 all-gather.12
  204.9 63.8 all-gather.14
  300.1 57.2 reduce-scatter.8
  359.0 45.5 all-gather.20
  427.6 61.4 all-gather.18
  525.7 58.3 reduce-scatter.10
  586.3 66.4 reduce-scatter.12
  675.8 64.2 all-gather.22
  768.0 60.2 reduce-scatter.14
  899.6 29.3 reduce-scatter.18
  931.2 25.8 reduce-scatter.22
  1007.4 31.1 reduce-scatter.20
  1040.7 28.1 reduce-scatter.16
